TPU v7x, 32 devices: a whole 2x2x4 slice. The times are simulated.
32 devices in a mesh: dp: 8 (over y, x, core), ctx: 4 (over z).
Axes of the slice: x: 2, y: 2, z: 4, core: 2. Of those that a mesh axis runs over, the one named last changes fastest.
Arguments:
- activations: bfloat16 [8, 512, 2048], P('dp', 'ctx'), may hold values from -6 to 6
- segment_ids: int32 [8, 512], P('dp'), may hold values from 0 to 3, never falling along the last dimension, each value on 1 to 256 neighbouring positions
- ln1_gain: bfloat16 [2048], P(('dp', 'ctx')), may hold values from 0.25 to 1.75
- ln1_bias: bfloat16 [2048], P(('dp', 'ctx')), may hold values from -3 to 3
- q_weight: bfloat16 [2048, 2048], P(('dp', 'ctx')), may hold values from -0.125 to 0.125
- q_bias: bfloat16 [2048], P(('dp', 'ctx')), may hold values from -3 to 3
- kv_weight: bfloat16 [2048, 256], P(('dp', 'ctx')), may hold values from -0.125 to 0.125
- v_bias: bfloat16 [128], P(('dp', 'ctx')), may hold values from -3 to 3
- out_weight: bfloat16 [2048, 2048], P(('dp', 'ctx')), may hold values from -1 to 1
- out_bias: bfloat16 [2048], P(('dp', 'ctx')), may hold values from -3 to 3
- ln2_gain: bfloat16 [2048], P(('dp', 'ctx')), may hold values from 0.25 to 1.75
- ln2_bias: bfloat16 [2048], P(('dp', 'ctx')), may hold values from -3 to 3
- up_weight: bfloat16 [2048, 8192], P(('dp', 'ctx')), may hold values from -0.125 to 0.125
- up_bias: bfloat16 [8192], P(('dp', 'ctx')), may hold values from -3 to 3
- down_weight: bfloat16 [8192, 2048], P(('dp', 'ctx')), may hold values from -0.0625 to 0.0625
- down_bias: bfloat16 [2048], P(('dp', 'ctx')), may hold values from -3 to 3
- cotangent: bfloat16 [8, 512, 2048], P('dp', 'ctx'), may hold values from -6 to 6
Outputs:
- output: bfloat16 [8, 512, 2048], P('dp', 'ctx')
- input_grad: bfloat16 [8, 512, 2048], P('dp', 'ctx')
- ln1_gain_grad: float32 [2048], P(('dp', 'ctx'))
- ln1_bias_grad: float32 [2048], P(('dp', 'ctx'))
- q_weight_grad: float32 [2048, 2048], P(('dp', 'ctx'))
- q_bias_grad: float32 [2048], P(('dp', 'ctx'))
- kv_weight_grad: float32 [2048, 256], P(('dp', 'ctx'))
- v_bias_grad: float32 [128], P(('dp', 'ctx'))
- out_weight_grad: float32 [2048, 2048], P(('dp', 'ctx'))
- out_bias_grad: float32 [2048], P(('dp', 'ctx'))
- ln2_gain_grad: float32 [2048], P(('dp', 'ctx'))
- ln2_bias_grad: float32 [2048], P(('dp', 'ctx'))
- up_weight_grad: float32 [2048, 8192], P(('dp', 'ctx'))
- up_bias_grad: float32 [8192], P(('dp', 'ctx'))
- down_weight_grad: float32 [8192, 2048], P(('dp', 'ctx'))
- down_bias_grad: float32 [2048], P(('dp', 'ctx'))
Inputs may be any that keep to these rules, and one draw needn't show every extreme that they name: segment_ids of a row never fall; every one of the 4 documents of a row holds 1 to 256 tokens, and one holds exactly 256.
All inputs are finite; a program needn't handle non-finite values.
Results may differ from a plain program's by a relative error of at most 0.013.
Values may be sent and summed in bfloat16 or wider, within the bound.
No kernel may reach another device: no remote copies, remote signals or barrier semaphores. Data moves between devices by JAX's collectives and lax.ppermute only.
A program may use at most 320 MiB of HBM per device.

v0:
```python
import jax
import jax.numpy as jnp
from jax import lax
from jax.sharding import PartitionSpec as P

HEADS = 16
HD = 128


epsilon = 1e-05


def norm_rows(values, gain, shift):
    center = jnp.mean(values, axis=-1, keepdims=True)
    centered = values - center
    variance = jnp.mean(centered * centered, axis=-1, keepdims=True)
    return centered * lax.rsqrt(variance + epsilon) * gain + shift


def gelu_tanh(values):
    return jax.nn.gelu(values, approximate=True)


def local(
    activations,
    segment_ids,
    ln1_gain,
    ln1_bias,
    q_weight,
    q_bias,
    kv_weight,
    v_bias,
    out_weight,
    out_bias,
    ln2_gain,
    ln2_bias,
    up_weight,
    up_bias,
    down_weight,
    down_bias,
    cotangent,
):
    row_input = activations[0].astype(jnp.float32)
    tokens_here = row_input.shape[0]
    block_index = lax.axis_index("ctx")
    row_segments = segment_ids[0]
    attn_full = (
        lax.all_gather(ln1_gain, ("dp", "ctx"), axis=0, tiled=True),
        lax.all_gather(ln1_bias, ("dp", "ctx"), axis=0, tiled=True),
        lax.all_gather(q_weight, ("dp", "ctx"), axis=0, tiled=True),
        lax.all_gather(q_bias, ("dp", "ctx"), axis=0, tiled=True),
        lax.all_gather(kv_weight, ("dp", "ctx"), axis=0, tiled=True),
        lax.all_gather(v_bias, ("dp", "ctx"), axis=0, tiled=True),
        lax.all_gather(out_weight, ("dp", "ctx"), axis=0, tiled=True),
        lax.all_gather(out_bias, ("dp", "ctx"), axis=0, tiled=True),
    )
    gain_one, shift_one, weight_query, bias_query, weight_kv, bias_value, weight_out, bias_out = (
        attn_full
    )
    normed_one, norm_back_one = jax.vjp(
        norm_rows, row_input, gain_one.astype(jnp.float32), shift_one.astype(jnp.float32)
    )
    hidden_one = normed_one.astype(jnp.bfloat16)
    query_low = (
        jnp.dot(hidden_one, weight_query, preferred_element_type=jnp.float32)
        + bias_query.astype(jnp.float32)
    ).astype(jnp.bfloat16)
    kv_shift = jnp.concatenate([jnp.zeros((HD,), jnp.float32), bias_value.astype(jnp.float32)])
    kv_low = (jnp.dot(hidden_one, weight_kv, preferred_element_type=jnp.float32) + kv_shift).astype(
        jnp.bfloat16
    )
    kv_whole = lax.all_gather(kv_low, "ctx", axis=0, tiled=True)
    key_rows = kv_whole[:, :HD]
    value_rows = kv_whole[:, HD:]
    query_heads = query_low.reshape(tokens_here, HEADS, HD)
    scale_factor = HD ** (-0.5)
    query_start = block_index * tokens_here
    query_places = query_start + jnp.arange(tokens_here, dtype=jnp.int32)
    key_places = jnp.arange(kv_whole.shape[0], dtype=jnp.int32)
    query_segments = lax.dynamic_slice_in_dim(row_segments, query_start, tokens_here)
    allowed = (key_places[None, :] <= query_places[:, None]) & (
        row_segments[None, :] == query_segments[:, None]
    )

    def masked_scores():
        raw_scores = (
            jnp.einsum("thd,jd->htj", query_heads, key_rows, preferred_element_type=jnp.float32)
            * scale_factor
        )
        return jnp.where(allowed[None], raw_scores, -1e30)

    scores = masked_scores()
    biggest = jnp.max(scores, axis=-1, keepdims=True)
    expons = jnp.exp(scores - biggest)
    row_total = jnp.sum(expons, axis=-1, keepdims=True)
    log_total = biggest + jnp.log(row_total)
    soft_low = (expons / row_total).astype(jnp.bfloat16)
    attended = (
        jnp.einsum("htj,jd->thd", soft_low, value_rows, preferred_element_type=jnp.float32)
        .reshape(tokens_here, HEADS * HD)
        .astype(jnp.bfloat16)
    )
    middle = (
        row_input
        + jnp.dot(attended, weight_out, preferred_element_type=jnp.float32)
        + bias_out.astype(jnp.float32)
    )
    mlp_full = (
        lax.all_gather(ln2_gain, ("dp", "ctx"), axis=0, tiled=True),
        lax.all_gather(ln2_bias, ("dp", "ctx"), axis=0, tiled=True),
        lax.all_gather(up_weight, ("dp", "ctx"), axis=0, tiled=True),
        lax.all_gather(up_bias, ("dp", "ctx"), axis=0, tiled=True),
        lax.all_gather(down_weight, ("dp", "ctx"), axis=0, tiled=True),
        lax.all_gather(down_bias, ("dp", "ctx"), axis=0, tiled=True),
    )
    gain_two, shift_two, weight_up, bias_up, weight_down, bias_down = mlp_full
    normed_two, norm_back_two = jax.vjp(
        norm_rows, middle, gain_two.astype(jnp.float32), shift_two.astype(jnp.float32)
    )
    hidden_two = normed_two.astype(jnp.bfloat16)
    preact = jnp.dot(hidden_two, weight_up, preferred_element_type=jnp.float32) + bias_up.astype(
        jnp.float32
    )
    activ_full, gelu_back = jax.vjp(gelu_tanh, preact)
    activ = activ_full.astype(jnp.bfloat16)
    result = (
        middle
        + jnp.dot(activ, weight_down, preferred_element_type=jnp.float32)
        + bias_down.astype(jnp.float32)
    )
    mlp_back = (
        lax.all_gather(ln2_gain, ("dp", "ctx"), axis=0, tiled=True),
        lax.all_gather(ln2_bias, ("dp", "ctx"), axis=0, tiled=True),
        lax.all_gather(up_weight, ("dp", "ctx"), axis=0, tiled=True),
        lax.all_gather(up_bias, ("dp", "ctx"), axis=0, tiled=True),
        lax.all_gather(down_weight, ("dp", "ctx"), axis=0, tiled=True),
        lax.all_gather(down_bias, ("dp", "ctx"), axis=0, tiled=True),
    )
    weight_up_back = mlp_back[2]
    weight_down_back = mlp_back[4]
    grad_low = cotangent[0]
    grad_result = grad_low.astype(jnp.float32)
    grad_activ = jnp.einsum(
        "td,fd->tf", grad_low, weight_down_back, preferred_element_type=jnp.float32
    )
    grad_bias_down = jnp.sum(grad_result, axis=0)
    grad_weight_down = jnp.einsum("tf,td->fd", activ, grad_low, preferred_element_type=jnp.float32)
    down_sums = (
        lax.psum_scatter(grad_weight_down, ("dp", "ctx"), scatter_dimension=0, tiled=True),
        lax.psum_scatter(grad_bias_down, ("dp", "ctx"), scatter_dimension=0, tiled=True),
    )
    grad_preact = gelu_back(grad_activ)[0].astype(jnp.bfloat16)
    grad_bias_up = jnp.sum(grad_preact.astype(jnp.float32), axis=0)
    grad_hidden_two = jnp.einsum(
        "tf,df->td", grad_preact, weight_up_back, preferred_element_type=jnp.float32
    )
    grad_weight_up = jnp.einsum(
        "td,tf->df", hidden_two, grad_preact, preferred_element_type=jnp.float32
    )
    grad_mid_norm, grad_gain_two, grad_shift_two = norm_back_two(grad_hidden_two)
    grad_middle = grad_result + grad_mid_norm
    up_sums = (
        lax.psum_scatter(grad_gain_two, ("dp", "ctx"), scatter_dimension=0, tiled=True),
        lax.psum_scatter(grad_shift_two, ("dp", "ctx"), scatter_dimension=0, tiled=True),
        lax.psum_scatter(grad_weight_up, ("dp", "ctx"), scatter_dimension=0, tiled=True),
        lax.psum_scatter(grad_bias_up, ("dp", "ctx"), scatter_dimension=0, tiled=True),
    )
    attn_back = (
        lax.all_gather(ln1_gain, ("dp", "ctx"), axis=0, tiled=True),
        lax.all_gather(ln1_bias, ("dp", "ctx"), axis=0, tiled=True),
        lax.all_gather(q_weight, ("dp", "ctx"), axis=0, tiled=True),
        lax.all_gather(q_bias, ("dp", "ctx"), axis=0, tiled=True),
        lax.all_gather(kv_weight, ("dp", "ctx"), axis=0, tiled=True),
        lax.all_gather(v_bias, ("dp", "ctx"), axis=0, tiled=True),
        lax.all_gather(out_weight, ("dp", "ctx"), axis=0, tiled=True),
        lax.all_gather(out_bias, ("dp", "ctx"), axis=0, tiled=True),
    )
    weight_query_back = attn_back[2]
    weight_kv_back = attn_back[4]
    weight_out_back = attn_back[6]
    grad_branch = grad_middle.astype(jnp.bfloat16)
    grad_bias_out = jnp.sum(grad_branch.astype(jnp.float32), axis=0)
    grad_weight_out = jnp.einsum(
        "ti,td->id", attended, grad_branch, preferred_element_type=jnp.float32
    )
    grad_attended = (
        jnp.einsum("td,id->ti", grad_branch, weight_out_back, preferred_element_type=jnp.float32)
        .astype(jnp.bfloat16)
        .reshape(tokens_here, HEADS, HD)
    )
    soft_rows = jnp.exp(masked_scores() - log_total)
    soft_again = soft_rows.astype(jnp.bfloat16)
    grad_soft = jnp.einsum(
        "thd,jd->htj", grad_attended, value_rows, preferred_element_type=jnp.float32
    )
    inner_sum = jnp.sum(soft_rows * grad_soft, axis=-1, keepdims=True)
    grad_scores = (soft_rows * (grad_soft - inner_sum)).astype(jnp.bfloat16)
    grad_query = (
        (
            jnp.einsum("htj,jd->thd", grad_scores, key_rows, preferred_element_type=jnp.float32)
            * scale_factor
        )
        .astype(jnp.bfloat16)
        .reshape(tokens_here, HEADS * HD)
    )
    grad_keys = (
        jnp.einsum("htj,thd->jd", grad_scores, query_heads, preferred_element_type=jnp.float32)
        * scale_factor
    )
    grad_values = jnp.einsum(
        "htj,thd->jd", soft_again, grad_attended, preferred_element_type=jnp.float32
    )
    grad_kv_part = jnp.concatenate([grad_keys, grad_values], axis=1)
    grad_kv = lax.psum_scatter(
        grad_kv_part.astype(jnp.bfloat16), "ctx", scatter_dimension=0, tiled=True
    )
    grad_bias_query = jnp.sum(grad_query.astype(jnp.float32), axis=0)
    grad_weight_query = jnp.einsum(
        "td,te->de", hidden_one, grad_query, preferred_element_type=jnp.float32
    )
    grad_bias_value = jnp.sum(grad_kv[:, HD:].astype(jnp.float32), axis=0)
    grad_weight_kv = jnp.einsum(
        "td,te->de", hidden_one, grad_kv, preferred_element_type=jnp.float32
    )
    grad_hidden_one = jnp.einsum(
        "te,de->td", grad_query, weight_query_back, preferred_element_type=jnp.float32
    ) + jnp.einsum("te,de->td", grad_kv, weight_kv_back, preferred_element_type=jnp.float32)
    grad_row_norm, grad_gain_one, grad_shift_one = norm_back_one(grad_hidden_one)
    grad_input = grad_middle + grad_row_norm
    attn_sums = (
        lax.psum_scatter(grad_gain_one, ("dp", "ctx"), scatter_dimension=0, tiled=True),
        lax.psum_scatter(grad_shift_one, ("dp", "ctx"), scatter_dimension=0, tiled=True),
        lax.psum_scatter(grad_weight_query, ("dp", "ctx"), scatter_dimension=0, tiled=True),
        lax.psum_scatter(grad_bias_query, ("dp", "ctx"), scatter_dimension=0, tiled=True),
        lax.psum_scatter(grad_weight_kv, ("dp", "ctx"), scatter_dimension=0, tiled=True),
        lax.psum_scatter(grad_bias_value, ("dp", "ctx"), scatter_dimension=0, tiled=True),
        lax.psum_scatter(grad_weight_out, ("dp", "ctx"), scatter_dimension=0, tiled=True),
        lax.psum_scatter(grad_bias_out, ("dp", "ctx"), scatter_dimension=0, tiled=True),
    )
    return (
        result.astype(jnp.bfloat16)[None],
        grad_input.astype(jnp.bfloat16)[None],
        attn_sums[0],
        attn_sums[1],
        attn_sums[2],
        attn_sums[3],
        attn_sums[4],
        attn_sums[5],
        attn_sums[6],
        attn_sums[7],
        up_sums[0],
        up_sums[1],
        up_sums[2],
        up_sums[3],
        down_sums[0],
        down_sums[1],
    )


def solution(mesh):
    in_specs = (
        P("dp", "ctx", None),
        P("dp", None),
        P(("dp", "ctx")),
        P(("dp", "ctx")),
        P(("dp", "ctx"), None),
        P(("dp", "ctx")),
        P(("dp", "ctx"), None),
        P(("dp", "ctx")),
        P(("dp", "ctx"), None),
        P(("dp", "ctx")),
        P(("dp", "ctx")),
        P(("dp", "ctx")),
        P(("dp", "ctx"), None),
        P(("dp", "ctx")),
        P(("dp", "ctx"), None),
        P(("dp", "ctx")),
        P("dp", "ctx", None),
    )
    out_specs = (
        P("dp", "ctx", None),
        P("dp", "ctx", None),
        P(("dp", "ctx")),
        P(("dp", "ctx")),
        P(("dp", "ctx"), None),
        P(("dp", "ctx")),
        P(("dp", "ctx"), None),
        P(("dp", "ctx")),
        P(("dp", "ctx"), None),
        P(("dp", "ctx")),
        P(("dp", "ctx")),
        P(("dp", "ctx")),
        P(("dp", "ctx"), None),
        P(("dp", "ctx")),
        P(("dp", "ctx"), None),
        P(("dp", "ctx")),
    )
    return jax.shard_map(local, mesh=mesh, in_specs=in_specs, out_specs=out_specs, check_vma=False)
```

profile of v0, /device:TPU:0, one launch (start us, length us, event | category | flops | bytes accessed | tf_op | source)
XLA Modules:
  0.0 4535.9 jit_solution(195619505325914754)
XLA Ops:
  17.4 42.8 all-reduce.19
  60.9 66.4 %all-gather = bf16[32,1,256]{2,1,0:T(2,128)(2,1)S(1)} all-gather(bf16[1,1,256]{2,1,0:T(2,128)(2,1)S(1)} %reshape.225), channel_id=1, replica_groups=mesh['dp'=8,'ctx'=4] {'dp','ctx'}, dimensions={0}, use_global_device_ids=true | all-gather | bytes 16896 | tf_op jit(solution)/shard_map/all_gather | solution.py:112
  128.1 1.2 convert_reduce_fusion.1
  129.3 1.3 fusion.42
  131.5 1.8 fusion.38
  133.3 15.9 all_gather.54
  149.3 4.7 fusion.14
  155.6 1.4 copy-done
  157.1 0.9 fusion.27
  158.0 70.8 %all-gather.11.cloned.1.call-done = bf16[2048,2048]{1,0:T(8,128)(2,1)} async-done(((bf16[64,2048]{1,0:T(8,128)(2,1)}), bf16[2048,2048]{1,0:T(8,128)(2,1)}) %all-gather.11.cloned.1.call-update) | async-done | bytes 8388624 | tf_op jit(solution)/shard_map/all_gather | solution.py:54
  228.8 4.7 fusion.77
  233.9 191.2 %all-gather.13.cloned.1.call-done = bf16[2048,8192]{1,0:T(8,128)(2,1)} async-done(((bf16[64,8192]{1,0:T(8,128)(2,1)}), bf16[2048,8192]{1,0:T(8,128)(2,1)}) %all-gather.13.cloned.1.call-update) | async-done | bytes 33554448 | tf_op jit(solution)/shard_map/all_gather | solution.py:111
  425.0 18.0 convolution_add_fusion
  443.0 177.8 %all-gather.15.cloned.1.call-done = bf16[8192,2048]{1,0:T(8,128)(2,1)} async-done(((bf16[256,2048]{1,0:T(8,128)(2,1)}), bf16[8192,2048]{1,0:T(8,128)(2,1)}) %all-gather.15.cloned.1.call-update) | async-done | bytes 33554448 | tf_op jit(solution)/shard_map/all_gather | solution.py:113
  620.8 19.8 convert_reduce_fusion
  640.6 19.9 multiply_reduce_fusion
  660.5 1.6 fusion.75
  663.7 7.1 convolution_convert_fusion
  670.8 2.0 copy.65
  672.8 3.3 fusion.7
  678.3 1.9 convert_reduce_fusion.4
  682.0 7.5 fusion.78
  689.4 10.5 reduce-scatter.19.cloned.1.call-done
  699.9 2.8 fusion.73
  702.7 1.1 fusion.41
  703.8 2.0 convert_reduce_fusion.2
  706.6 1.9 fusion.69
  709.1 8.2 fusion.51
  717.3 1.0 copy-done.5
  718.5 8.0 fusion.79
  726.6 24.9 fusion.68
  751.7 25.5 fusion.53
  777.9 17.7 fusion.16
  795.6 35.9 all-reduce.22.cloned.1.call-done
  831.5 1.3 dynamic-slice.1
  832.8 1.3 dynamic-slice.2
  834.0 1.3 dynamic-slice.3
  835.3 1.3 dynamic-slice.5
  836.5 1.3 dynamic-slice.6
  837.8 1.3 dynamic-slice.7
  839.1 1.3 dynamic-slice.9
  840.3 1.2 dynamic-slice.4
  841.5 1.3 dynamic-slice.8
  842.9 130.5 %reduce-scatter.11.cloned.1.call-done = f32[64,256]{1,0:T(8,128)} async-done(((f32[2048,256]{1,0:T(8,128)}), f32[64,256]{1,0:T(8,128)}) %reduce-scatter.11.cloned.1.call-update) | async-done | bytes 65552 | tf_op jit(solution)/shard_map/reduce_scatter | solution.py:235
  973.4 365.3 %reduce-scatter.9.cloned.1.call-done = f32[64,2048]{1,0:T(8,128)} async-done(((f32[2048,2048]{1,0:T(8,128)}), f32[64,2048]{1,0:T(8,128)}) %reduce-scatter.9.cloned.1.call-update) | async-done | bytes 524304 | tf_op jit(solution)/shard_map/reduce_scatter | solution.py:233
  1338.6 365.0 %reduce-scatter.13.cloned.1.call-done = f32[64,2048]{1,0:T(8,128)} async-done(((f32[2048,2048]{1,0:T(8,128)}), f32[64,2048]{1,0:T(8,128)}) %reduce-scatter.13.cloned.1.call-update) | async-done | bytes 524304 | tf_op jit(solution)/shard_map/reduce_scatter | solution.py:237
  1703.7 1411.7 %reduce-scatter.15.cloned.1.call-done = f32[64,8192]{1,0:T(8,128)} async-done(((f32[2048,8192]{1,0:T(8,128)}), f32[64,8192]{1,0:T(8,128)}) %reduce-scatter.15.cloned.1.call-update) | async-done | bytes 2097168 | tf_op jit(solution)/shard_map/reduce_scatter | solution.py:165
  3115.3 1413.5 %reduce-scatter.17.cloned.1.call-done = f32[256,2048]{1,0:T(8,128)} async-done(((f32[8192,2048]{1,0:T(8,128)}), f32[256,2048]{1,0:T(8,128)}) %reduce-scatter.17.cloned.1.call-update) | async-done | bytes 2097168 | tf_op jit(solution)/shard_map/reduce_scatter | solution.py:149
  (104 shorter events, 22.4 us)
Async XLA Ops:
  7.2 142.1 %copy-start.2 = (bf16[1,128,2048]{2,1,0:T(8,128)(2,1)S(1)}, bf16[1,128,2048]{2,1,0:T(8,128)(2,1)}, u32[]{:S(2)}) copy-start(bf16[1,128,2048]{2,1,0:T(8,128)(2,1)} %param.17) | copy-start | bytes 1572868
  7.2 124.3 %all-gather.7.cloned.1.call-start = ((), (), s32[]{:S(2)}) async-start(), calls=%async_computation.6 | async-start | bytes 1081344 | tf_op jit(solution)/shard_map/all_gather | solution.py:52
  7.9 141.3 %all-gather.9.cloned.1.call-start = ((), (), s32[]{:S(2)}) async-start(), calls=%async_computation.7 | async-start | bytes 8650752 | tf_op jit(solution)/shard_map/all_gather | solution.py:50
  8.7 220.1 %all-gather.11.cloned.1.call-start = ((), (), s32[]{:S(2)}) async-start(), calls=%async_computation.8 | async-start | bytes 8650752 | tf_op jit(solution)/shard_map/all_gather | solution.py:54
  9.4 415.6 %all-gather.13.cloned.1.call-start = ((), (), s32[]{:S(2)}) async-start(), calls=%async_computation.9 | async-start | bytes 34603008 | tf_op jit(solution)/shard_map/all_gather | solution.py:111
  10.0 610.8 %all-gather.15.cloned.1.call-start = ((), (), s32[]{:S(2)}) async-start(), calls=%async_computation.10 | async-start | bytes 34603008 | tf_op jit(solution)/shard_map/all_gather | solution.py:113
  10.6 689.3 %reduce-scatter.19.cloned.1.call-start = ((), (), s32[]{:S(2)}) async-start(), calls=%async_computation.16 | async-start | bytes 327680
  154.3 1.4 copy-start.10
  155.0 2.0 copy-start
  158.0 75.6 %copy-start.8 = (bf16[128,16,128]{2,0,1:T(8,128)(2,1)}, bf16[128,16,128]{2,0,1:T(8,128)(2,1)S(1)}, u32[]{:S(2)}) copy-start(bf16[128,16,128]{2,0,1:T(8,128)(2,1)S(1)} %fusion.27) | copy-start | bytes 1572868
  425.0 195.8 %copy-start.3 = (bf16[1,128,2048]{2,1,0:T(8,128)(2,1)S(1)}, bf16[1,128,2048]{2,1,0:T(8,128)(2,1)}, u32[]{:S(2)}) copy-start(bf16[1,128,2048]{2,1,0:T(8,128)(2,1)} %param.33) | copy-start | bytes 1572868
  662.9 0.8 copy-start.4
  672.8 3.6 copy-start.1
  672.8 3.7 copy-start.6
  677.4 2.8 copy-start.11
  681.9 149.6 %all-reduce.22.cloned.1.call-start = ((), (), s32[]{:S(2)}) async-start(), calls=%async_computation.17 | async-start | bytes 181248
  699.9 5.9 slice-start
  699.9 6.7 copy-start.12
  705.8 3.3 copy-start.7
  706.5 266.8 %reduce-scatter.11.cloned.1.call-start = ((), (), s32[]{:S(2)}) async-start(), calls=%async_computation.12 | async-start | bytes 2162688 | tf_op jit(solution)/shard_map/reduce_scatter | solution.py:235
  708.6 630.1 %reduce-scatter.9.cloned.1.call-start = ((), (), s32[]{:S(2)}) async-start(), calls=%async_computation.11 | async-start | bytes 17301504 | tf_op jit(solution)/shard_map/reduce_scatter | solution.py:233
  717.3 1.0 copy-start.5
  717.3 1.2 copy-start.9
  717.3 986.4 %reduce-scatter.13.cloned.1.call-start = ((), (), s32[]{:S(2)}) async-start(), calls=%async_computation.13 | async-start | bytes 17301504 | tf_op jit(solution)/shard_map/reduce_scatter | solution.py:237
  726.5 2388.8 %reduce-scatter.15.cloned.1.call-start = ((), (), s32[]{:S(2)}) async-start(), calls=%async_computation.14 | async-start | bytes 69206016 | tf_op jit(solution)/shard_map/reduce_scatter | solution.py:165
  751.5 3777.3 %reduce-scatter.17.cloned.1.call-start = ((), (), s32[]{:S(2)}) async-start(), calls=%async_computation.15 | async-start | bytes 69206016 | tf_op jit(solution)/shard_map/reduce_scatter | solution.py:149
  777.2 0.7 copy-start.13
Sparse Core Ops, SparseCore 0:
  11.0 56.6 all-gather.6
  70.7 78.5 all-gather.8
  152.2 76.5 all-gather.10
  231.6 193.3 all-gather.12
  427.8 192.9 all-gather.14
  682.0 17.8 reduce-scatter.18
  708.0 123.4 all-reduce.21
  834.3 138.9 reduce-scatter.10
  976.3 362.2 reduce-scatter.8
  1341.5 362.1 reduce-scatter.12
  1706.7 1408.5 reduce-scatter.14
  3118.2 1410.5 reduce-scatter.16
where the time goes:
time: 4540 us
  waiting for transfers between devices  4180 us (92%)
  matrix products  181 us (4%)
  blocking collectives  125 us (3%)
    reduce_scatter x1, waiting for transfers between devices, local(): lax.psum_scatter(grad_weight_down, ('dp', 'ctx'), scatter_dimension=0, ti...  1410 us
    reduce_scatter x1, waiting for transfers between devices, local(): lax.psum_scatter(grad_weight_up, ('dp', 'ctx'), scatter_dimension=0, tile...  1410 us
    reduce_scatter x1, waiting for transfers between devices, local(): lax.psum_scatter(grad_weight_query, ('dp', 'ctx'), scatter_dimension=0, t...  365 us
    reduce_scatter x1, waiting for transfers between devices, local(): lax.psum_scatter(grad_weight_out, ('dp', 'ctx'), scatter_dimension=0, til...  365 us
    all_gather x1, waiting for transfers between devices, local(): lax.all_gather(up_weight, ('dp', 'ctx'), axis=0, tiled=True)  191 us
    all_gather x1, waiting for transfers between devices, local(): lax.all_gather(down_weight, ('dp', 'ctx'), axis=0, tiled=True)  178 us
    reduce_scatter x1, waiting for transfers between devices, local(): lax.psum_scatter(grad_weight_kv, ('dp', 'ctx'), scatter_dimension=0, tile...  131 us
  transfers between devices with their start and end apart: 12, of which 11 were waited for; matrix products, arithmetic and copies ran while one was open for 3% of the time, Pallas kernels for 0%

commit v1 on v0

v1 whole, which is shorter than its diff:
```python
import jax
import jax.numpy as jnp
from jax import lax
from jax.sharding import Mesh, PartitionSpec as P

HEADS = 16
HD = 128
EPS = 1e-05
GELU_K = 0.7978845608028654
GELU_C = 0.044715

BF = jnp.bfloat16
F32 = jnp.float32
CHIP = ("a", "b")
EVERY = ("a", "b", "core", "ctx")


def dot(a, b, dims):
    return lax.dot_general(a, b, (dims, ((), ())), preferred_element_type=F32)


def mm(a, b):
    return dot(a, b, ((1,), (0,)))


def mm_nt(a, b):
    return dot(a, b, ((1,), (1,)))


def mm_tn(a, b):
    return dot(a, b, ((0,), (0,)))


def ln_stats(x):
    mean = jnp.mean(x, axis=-1, keepdims=True)
    cen = x - mean
    var = jnp.mean(cen * cen, axis=-1, keepdims=True)
    rstd = lax.rsqrt(var + EPS)
    return cen * rstd, rstd


def ln_back(dh, gain, xhat, rstd):
    e = dh * gain
    me = jnp.mean(e, axis=-1, keepdims=True)
    mx = jnp.mean(e * xhat, axis=-1, keepdims=True)
    return (e - me - xhat * mx) * rstd


def make_local(A, B, Z):
    C = 2
    AB = A * B
    N = AB * C * Z
    mates = [(0, 1), (1, 0)]

    def swap_core(x):
        return lax.ppermute(x, "core", mates)

    def gather(x, axes, axis=0):
        return lax.all_gather(x, axes, axis=axis, tiled=False)

    def scatter(x, axes, axis=0):
        return lax.psum_scatter(x, axes, scatter_dimension=axis, tiled=False)

    def local(
        activations, segment_ids,
        ln1_gain, ln1_bias, q_weight, q_bias, kv_weight, v_bias, out_weight, out_bias,
        ln2_gain, ln2_bias, up_weight, up_bias, down_weight, down_bias, cotangent,
    ):
        T, D = activations.shape[1:]
        S = segment_ids.shape[1]
        R = q_weight.shape[0]
        F0 = down_weight.shape[0]
        F = AB * F0
        FF = up_weight.shape[1]
        DH = D // 2
        HH = HEADS // 2
        aligned = (Z * R) % HD == 0
        G = AB if aligned else 1
        W0 = DH // G
        c = lax.axis_index("core")
        z = lax.axis_index("ctx")

        vb0 = v_bias.shape[0]
        small = jnp.concatenate(
            [ln1_gain, ln1_bias, q_bias, out_bias, ln2_gain, ln2_bias, down_bias, up_bias, v_bias]
        )
        small = jnp.broadcast_to(small[None], (N, small.shape[0]))
        small = lax.all_to_all(small, EVERY, 0, 0, tiled=True).astype(F32)
        g1, b1, bq, bo, g2, b2, bd = (small[:, i * R : (i + 1) * R].reshape(D) for i in range(7))
        bu = small[:, 7 * R : 7 * R + F0].reshape(AB, C * Z, F0)
        bu = lax.dynamic_index_in_dim(bu, c * Z + z, 1, keepdims=False).reshape(F)
        bv = small[:, 7 * R + F0 :].reshape(HD)
        bq = lax.dynamic_index_in_dim(bq.reshape(G, 2, W0), c, 1, keepdims=False).reshape(DH)
        b_ext = jnp.concatenate([bq, jnp.where(c == 1, bv, 0.0)])

        w_ext = jnp.concatenate(
            [
                q_weight.reshape(R, G, 2, W0).transpose(2, 0, 1, 3).reshape(2, R, DH),
                kv_weight.reshape(R, 2, HD).transpose(1, 0, 2),
            ],
            axis=2,
        )
        E = DH + HD
        w_ext = lax.all_to_all(w_ext, "core", 0, 0, tiled=True)
        w_ext = gather(w_ext, "ctx", axis=1)
        w_ext = gather(w_ext, CHIP).reshape(D, E)
        if aligned:
            w_out = gather(gather(out_weight, "ctx"), CHIP).reshape(DH, D)
        else:
            w_out = gather(out_weight, EVERY).reshape(2, DH, D)
            w_out = lax.dynamic_index_in_dim(w_out, c, 0, keepdims=False)

        w_up = up_weight.reshape(R, AB, C * Z, F0).transpose(2, 0, 1, 3).reshape(C * Z, R, F)
        w_up = lax.all_to_all(w_up, ("core", "ctx"), 0, 0, tiled=True)
        w_up = gather(w_up, CHIP).reshape(D, F)
        w_down = gather(down_weight, CHIP).reshape(F, D)

        cot = cotangent[0]
        cot_z = gather(cot, "ctx")
        cot_all = jnp.stack([cot_z, swap_core(cot_z)]).reshape(2 * Z * T, D)

        x = activations[0].astype(F32)
        xhat1, rstd1 = ln_stats(x)
        h1 = (xhat1 * g1 + b1).astype(BF)
        h1 = jnp.concatenate([h1, swap_core(h1)])
        q_ext = (mm(h1, w_ext) + b_ext).astype(BF)
        q = q_ext[:, :DH].reshape(2, T, HH, HD)
        kv = gather(q_ext[:, DH:].reshape(2, T, HD), "ctx", axis=1).reshape(2, S, HD)
        kv_mate = swap_core(kv)[::-1]
        k = jnp.where(c == 0, kv, kv_mate)
        v = jnp.where(c == 0, kv_mate, kv)
        seg = jnp.concatenate([segment_ids, swap_core(segment_ids)])
        start = z * T
        seg_q = lax.dynamic_slice_in_dim(seg, start, T, axis=1)
        q_at = start + jnp.arange(T, dtype=jnp.int32)
        k_at = jnp.arange(S, dtype=jnp.int32)
        allowed = (k_at[None, None, :] <= q_at[None, :, None]) & (seg[:, None, :] == seg_q[:, :, None])
        s = jnp.einsum("rthd,rjd->rhtj", q, k, preferred_element_type=F32) * HD**-0.5
        s = jnp.where(allowed[:, None], s, -1e30)
        p = jnp.exp(s - jnp.max(s, axis=-1, keepdims=True))
        p = p / jnp.sum(p, axis=-1, keepdims=True)
        pb = p.astype(BF)
        o = jnp.einsum("rhtj,rjd->rthd", pb, v, preferred_element_type=F32)
        o = o.astype(BF).reshape(2 * T, DH)
        part = mm(o, w_out)
        mid = x + bo + part[:T] + swap_core(part[T:])

        xhat2, rstd2 = ln_stats(mid)
        h2 = (xhat2 * g2 + b2).astype(BF)
        h2_z = gather(h2, "ctx")
        h2_all = jnp.stack([h2_z, swap_core(h2_z)]).reshape(2 * Z * T, D)
        pre = mm(h2_all, w_up) + bu
        th = jnp.tanh(GELU_K * (pre + GELU_C * pre * pre * pre))
        act = (0.5 * pre * (1.0 + th)).astype(BF)
        dgelu = 0.5 * (1.0 + th) + 0.5 * pre * (1.0 - th * th) * GELU_K * (1.0 + 3.0 * GELU_C * pre * pre)

        def token_sum(part):
            half = Z * T
            mine = part[:half] + swap_core(part[half:].astype(BF)).astype(F32)
            return scatter(mine.reshape(Z, T, D).astype(BF), "ctx").astype(F32)

        dact = mm_nt(cot_all, w_down)
        dpre = (dact * dgelu).astype(BF)
        dh2 = token_sum(mm_nt(dpre, w_up))
        result = mid + token_sum(mm(act, w_down)) + bd
        g_down = scatter(mm_tn(act, cot_all).astype(BF).reshape(AB, F0, D), CHIP).astype(F32)
        g_up = scatter(mm_tn(h2_all, dpre).astype(BF).reshape(AB, C * Z, R, F), CHIP)
        g_up = lax.all_to_all(g_up, ("core", "ctx"), 0, 0, tiled=True)
        g_up = g_up.reshape(C * Z, R, AB, F0).transpose(1, 2, 0, 3).reshape(R, FF).astype(F32)
        gb_up = jnp.sum(dpre.astype(F32), axis=0)

        cot32 = cot.astype(F32)
        dmid = cot32 + ln_back(dh2, g2, xhat2, rstd2)
        db_own = dmid.astype(BF)
        db = jnp.concatenate([db_own, swap_core(db_own)])
        g_out = mm_tn(o, db).astype(BF)
        if aligned:
            g_out = scatter(scatter(g_out.reshape(AB, Z, R, D), CHIP), "ctx").astype(F32)
        else:
            full = jnp.where(lax.broadcasted_iota(jnp.int32, (2, 1, 1), 0) == c, g_out[None], 0)
            g_out = scatter(full.reshape(N, R, D), EVERY).astype(F32)
        do = mm_nt(db, w_out).astype(BF).reshape(2, T, HH, HD)
        dp = jnp.einsum("rthd,rjd->rhtj", do, v, preferred_element_type=F32)
        ds = (p * (dp - jnp.sum(p * dp, axis=-1, keepdims=True))).astype(BF)
        dq = jnp.einsum("rhtj,rjd->rthd", ds, k, preferred_element_type=F32) * HD**-0.5
        dk = jnp.einsum("rhtj,rthd->rjd", ds, q, preferred_element_type=F32) * HD**-0.5
        dv = jnp.einsum("rhtj,rthd->rjd", pb, do, preferred_element_type=F32)
        away = jnp.where(c == 0, dv, dk).astype(BF)
        here = jnp.where(c == 0, dk, dv)
        here = here + swap_core(away)[::-1].astype(F32)
        dkv = here.astype(BF).reshape(2, Z, T, HD).transpose(1, 0, 2, 3)
        dkv = lax.all_to_all(dkv, "ctx", 0, 0, tiled=True)
        dkv = jnp.sum(dkv.astype(F32), axis=0).astype(BF).reshape(2 * T, HD)
        dq_ext = jnp.concatenate([dq.astype(BF).reshape(2 * T, DH), dkv], axis=1)
        part1 = mm_nt(dq_ext, w_ext)
        dh1 = part1[:T] + swap_core(part1[T:])
        g_ext = mm_tn(h1, dq_ext).astype(BF).reshape(AB, 2, Z, R, E)
        g_ext = scatter(scatter(g_ext, CHIP), "ctx", axis=1)
        g_ext = lax.all_to_all(g_ext, "core", 0, 0, tiled=True)
        g_q = g_ext[:, :, :DH].reshape(2, R, G, W0).transpose(1, 2, 0, 3).reshape(R, D).astype(F32)
        g_kv = g_ext[:, :, DH:].transpose(1, 0, 2).reshape(R, 2 * HD).astype(F32)
        gb_ext = jnp.sum(dq_ext.astype(F32), axis=0)
        dx = dmid + ln_back(dh1, g1, xhat1, rstd1)

        own_core = (lax.broadcasted_iota(jnp.int32, (1, 2, 1), 1) == c).astype(F32)
        own_cz = (lax.broadcasted_iota(jnp.int32, (1, C * Z, 1), 1) == c * Z + z).astype(F32)
        wide = [
            jnp.sum(dh1 * xhat1, axis=0),
            jnp.sum(dh1, axis=0),
            (gb_ext[:DH].reshape(G, 1, W0) * own_core).reshape(D),
            jnp.sum(db_own.astype(F32), axis=0),
            jnp.sum(dh2 * xhat2, axis=0),
            jnp.sum(dh2, axis=0),
            jnp.sum(cot32, axis=0),
        ]
        packed = jnp.concatenate(
            [w.reshape(N, R) for w in wide]
            + [
                (gb_up.reshape(AB, 1, F0) * own_cz).reshape(N, F0),
                jnp.where(c == 1, gb_ext[DH:], 0.0).reshape(N, vb0),
            ],
            axis=1,
        )
        packed = jnp.sum(lax.all_to_all(packed, EVERY, 0, 0, tiled=True), axis=0)
        v_ = [packed[i * R : (i + 1) * R] for i in range(7)]
        gb_up = packed[7 * R : 7 * R + F0]
        gb_v = packed[7 * R + F0 :]
        return (
            result.astype(BF)[None], dx.astype(BF)[None],
            v_[0], v_[1], g_q, v_[2], g_kv, gb_v, g_out, v_[3],
            v_[4], v_[5], g_up, gb_up, g_down, v_[6],
        )

    return local


def solution(mesh):
    dp, ctx = mesh.shape["dp"], mesh.shape["ctx"]
    chips = dp // 2
    a = next(i for i in range(int(chips**0.5), 0, -1) if chips % i == 0)
    b = chips // a
    fine = Mesh(mesh.devices.reshape(a, b, 2, ctx), EVERY)
    tok = P(("a", "b", "core"), "ctx", None)
    vec = P(EVERY)
    mat = P(EVERY, None)
    in_specs = (
        tok, P(("a", "b", "core"), None),
        vec, vec, mat, vec, mat, vec, mat, vec, vec, vec, mat, vec, mat, vec, tok,
    )
    out_specs = (tok, tok, vec, vec, mat, vec, mat, vec, mat, vec, vec, vec, mat, vec, mat, vec)
    return jax.shard_map(
        make_local(a, b, ctx), mesh=fine, in_specs=in_specs, out_specs=out_specs, check_vma=False
    )
```

time: 4540 us -> 869 us (0.19)
  waiting for transfers between devices: 4180 us -> 601 us
  matrix products: 181 us -> 82.9 us
  blocking collectives: 125 us -> 77.6 us
    reduce_scatter x5 -> x3, waiting for transfers between devices: 3690 us -> 93.8 us  [scatter(): return lax.psum_scatter(x, axes, scatter_dimension=axis, tiled=False)]
    all_gather x5 -> x8, waiting for transfers between devices: 440 us -> 268 us  [gather(): return lax.all_gather(x, axes, axis=axis, tiled=False)]
    unnamed x14 -> x21, waiting for transfers between devices: 49.6 us -> 208 us
    dot_general x21 -> x18, matrix products: 181 us -> 82.9 us  [the longest x12 78.2 us: dot(): return lax.dot_general(a, b, (dims, ((), ())), preferred_element_type=F32)]
    all_gather x2 -> x1, blocking collectives: 82.3 us -> 13.9 us  [gather(): return lax.all_gather(x, axes, axis=axis, tiled=False)]
    all_to_all x0 -> x3, blocking collectives: none -> 63.7 us  [the longest x1 55 us: local(): w_up = lax.all_to_all(w_up, ('core', 'ctx'), 0, 0, tiled=True)]
  transfers between devices with their start and end apart: 12 -> 31, of which waited for: 11 -> 26; matrix products, arithmetic and copies ran while one was open for 3% -> 13% of each run, Pallas kernels for 0% -> 0%
where the time goes in v1:
time: 869 us; the launch traced here: 860 us
  waiting for transfers between devices  601 us (69%)
  matrix products  82.9 us (10%)
  blocking collectives  77.6 us (9%)
  other arithmetic  35.5 us (4%)
  local copies, waits for them, and re-layouts  29 us (3%)
  starting transfers between devices  19.2 us (2%)
  between operations  15.3 us (2%)
    all_gather x8, waiting for transfers between devices, gather(): return lax.all_gather(x, axes, axis=axis, tiled=False)  268 us
    unnamed x21, waiting for transfers between devices  208 us
    reduce_scatter x3, waiting for transfers between devices, scatter(): return lax.psum_scatter(x, axes, scatter_dimension=axis, tiled=False)  93.8 us
    dot_general x12, matrix products, dot(): return lax.dot_general(a, b, (dims, ((), ())), preferred_element_type=F32)  78.2 us
    all_to_all x1, blocking collectives, local(): w_up = lax.all_to_all(w_up, ('core', 'ctx'), 0, 0, tiled=True)  55 us
    ppermute x11, waiting for transfers between devices, swap_core(): return lax.ppermute(x, 'core', mates)  18.3 us
  transfers between devices with their start and end apart: 31, of which 26 were waited for; matrix products, arithmetic and copies ran while one was open for 13% of the time, Pallas kernels for 0%

profile of v1, /device:TPU:0, one launch (start us, length us, event | category | flops | bytes accessed | tf_op | source)
XLA Modules:
  0.0 860.3 jit_solution(12961263074182423622)
XLA Ops:
  8.9 4.7 all_to_all.40
  14.5 32.5 %all-gather.18.cloned.1.call-done = bf16[2,256,1152]{2,1,0:T(8,128)(2,1)} async-done(((bf16[2,64,1152]{2,1,0:T(8,128)(2,1)}), bf16[2,256,1152]{2,1,0:T(8,128)(2,1)}) %all-gather.18.cloned.1.call-update) | async-done | bytes 1179664 | tf_op jit(solution)/shard_map/all_gather | solution.py:59
  47.0 28.6 %all-gather.22.cloned.1.call-done = bf16[256,2048]{1,0:T(8,128)(2,1)} async-done(((bf16[64,2048]{1,0:T(8,128)(2,1)}), bf16[256,2048]{1,0:T(8,128)(2,1)}) %all-gather.22.cloned.1.call-update) | async-done | bytes 1048592 | tf_op jit(solution)/shard_map/all_gather | solution.py:59
  78.1 4.1 all-to-all-start
  83.4 6.1 all-to-all-done
  92.3 41.7 %all-gather.20.cloned.1.call-done = bf16[8,4,64,1152]{3,2,1,0:T(8,128)(2,1)} async-done(((bf16[2,4,64,1152]{3,2,1,0:T(8,128)(2,1)}), bf16[8,4,64,1152]{3,2,1,0:T(8,128)(2,1)}) %all-gather.20.cloned.1.call-update) | async-done | bytes 4718608 | tf_op jit(solution)/shard_map/all_gather | solution.py:59
  134.0 3.9 fusion.14
  137.9 13.9 %all_gather.52 = bf16[2,4,128,128]{3,2,0,1:T(8,128)(2,1)S(1)} all-gather(bf16[2,1,128,128]{3,2,0,1:T(8,128)(2,1)S(1)} %bitcast.295), channel_id=1, replica_groups=mesh['a'=2,'b'=2,'core'=2,'ctx'=4] {'ctx'}, dimensions={1}, use_global_device_ids=true | all-gather | bytes 327680 | tf_op jit(solution)/shard_map/all_gather | solution.py:59
  156.3 2.0 copy-done.7
  159.2 29.3 %all-gather.24.cloned.1.call-done = bf16[16,64,2048]{2,1,0:T(8,128)(2,1)} async-done(((bf16[4,64,2048]{2,1,0:T(8,128)(2,1)}), bf16[16,64,2048]{2,1,0:T(8,128)(2,1)}) %all-gather.24.cloned.1.call-update) | async-done | bytes 4194320 | tf_op jit(solution)/shard_map/all_gather | solution.py:59
  188.5 3.4 fusion.59
  193.8 2.2 collective-permute-done.3
  201.6 55.0 %all_to_all.41 = bf16[8,64,1024]{2,1,0:T(8,128)(2,1)} all-to-all(bf16[8,64,1024]{2,1,0:T(8,128)(2,1)} %reshape.295), channel_id=1, replica_groups=mesh['a'=2,'b'=2,'core'=2,'ctx'=4] {'core','ctx'}, dimensions={0} | all-to-all | bytes 2097152 | tf_op jit(solution)/shard_map/all_to_all | solution.py:114
  258.4 46.4 %all-gather.26.cloned.1.call-done = bf16[512,2048]{1,0:T(8,128)(2,1)} async-done(((bf16[128,2048]{1,0:T(8,128)(2,1)}), bf16[512,2048]{1,0:T(8,128)(2,1)}) %all-gather.26.cloned.1.call-update) | async-done | bytes 2097168 | tf_op jit(solution)/shard_map/all_gather | solution.py:59
  305.0 4.7 pad_maximum_fusion.1
  309.7 4.0 pad_maximum_fusion
  313.7 44.4 %all-gather.28.cloned.1.call-done = bf16[32,64,1024]{2,1,0:T(8,128)(2,1)} async-done(((bf16[8,64,1024]{2,1,0:T(8,128)(2,1)}), bf16[32,64,1024]{2,1,0:T(8,128)(2,1)}) %all-gather.28.cloned.1.call-update) | async-done | bytes 4194320 | tf_op jit(solution)/shard_map/all_gather | solution.py:59
  358.2 9.9 %fusion.89 = f32[1024,1024]{1,0:T(8,128)} fusion(bf16[1024,2048]{1,0:T(8,128)(2,1)} %bitcast.262, bf16[2048,1024]{1,0:T(8,128)(2,1)} %bitcast.304), kind=kOutput, calls=%fused_computation.171 | convolution fusion | flops 4294967296 | bytes 12582912 | tf_op jit(solution)/shard_map/dot_general | solution.py:19
  368.1 44.7 %all-gather.30.cloned.1.call-done = bf16[1024,2048]{1,0:T(8,128)(2,1)} async-done(((bf16[256,2048]{1,0:T(8,128)(2,1)}), bf16[1024,2048]{1,0:T(8,128)(2,1)}) %all-gather.30.cloned.1.call-update) | async-done | bytes 4194320 | tf_op jit(solution)/shard_map/all_gather | solution.py:59
  412.8 11.5 %convert_reduce_fusion = (f32[1024]{0:T(1024)S(1)}, bf16[1024,1024]{1,0:T(8,128)(2,1)S(1)}) fusion(f32[1024,1024]{1,0:T(8,128)} %fusion.89, f32[1024]{0:T(1024)S(1)} %bitcast.297, bf16[1024,2048]{1,0:T(8,128)(2,1)} %bitcast.260, bf16[1024,2048]{1,0:T(8,128)(2,1)} %all-gather.30.cloned.1.call-done), kind=kOutput, calls=%fused_computation.25 | convolution fusion | flops 4318034944 | bytes 14688256 | tf_op jit(solution)/shard_map/dot_general | solution.py:19
  424.3 4.7 fusion.90
  429.4 4.1 collective-permute-done.7
  433.6 2.0 fusion.8
  435.7 8.4 fusion.82
  444.6 4.0 collective-permute-done.5
  448.7 2.1 fusion.9
  450.9 28.8 %reduce-scatter.21.cloned.1.call-done = bf16[1,128,2048]{2,1,0:T(8,128)(2,1)} async-done(((bf16[4,128,2048]{2,1,0:T(8,128)(2,1)}), bf16[1,128,2048]{2,1,0:T(8,128)(2,1)}) %reduce-scatter.21.cloned.1.call-update) | async-done | bytes 524304 | tf_op jit(solution)/shard_map/reduce_scatter | solution.py:62
  481.2 44.5 %reduce-scatter.19.cloned.1.call-done = bf16[1,128,2048]{2,1,0:T(8,128)(2,1)} async-done(((bf16[4,128,2048]{2,1,0:T(8,128)(2,1)}), bf16[1,128,2048]{2,1,0:T(8,128)(2,1)}) %reduce-scatter.19.cloned.1.call-update) | async-done | bytes 524304 | tf_op jit(solution)/shard_map/reduce_scatter | solution.py:62
  525.7 3.0 convert_reduce_fusion.5
  530.6 3.3 convolution_convert_fusion.1
  534.0 9.4 %convolution_convert_fusion.3 = bf16[2048,1024]{1,0:T(8,128)(2,1)} fusion(bf16[1024,2048]{1,0:T(8,128)(2,1)} %bitcast.263, bf16[1024,1024]{1,0:T(8,128)(2,1)} %copy-done.32), kind=kOutput, calls=%fused_computation.30 | convolution fusion | flops 4297064448 | bytes 10485760 | tf_op jit(solution)/shard_map/dot_general | solution.py:19
  543.7 11.0 %convolution_convert_fusion.2 = bf16[1024,2048]{1,0:T(8,128)(2,1)} fusion(bf16[1024,2048]{1,0:T(8,128)(2,1)} %bitcast.261, f32[1024,1024]{1,0:T(8,128)} %fusion.89, f32[1024]{0:T(1024)S(1)} %bitcast.299), kind=kOutput, calls=%fused_computation.29 | convolution fusion | flops 4307550208 | bytes 12587008 | tf_op jit(solution)/shard_map/dot_general | solution.py:19
  554.8 3.6 fusion.32
  564.2 4.0 all-to-all-start.3
  571.0 6.8 all-to-all-done.3
  578.8 5.0 convolution_convert_fusion
  584.2 4.0 fusion.73
  596.2 3.6 all-to-all-start.4
  599.8 43.2 %reduce-scatter.29.cloned.1.call-done = bf16[1,8,64,1024]{3,2,1,0:T(8,128)(2,1)} async-done(((bf16[4,8,64,1024]{3,2,1,0:T(8,128)(2,1)}), bf16[1,8,64,1024]{3,2,1,0:T(8,128)(2,1)}) %reduce-scatter.29.cloned.1.call-update) | async-done | bytes 1048592
  643.0 4.6 all-to-all-start.6
  648.2 50.5 %reduce-scatter.31.cloned.1.call-done = bf16[1,256,2048]{2,1,0:T(8,128)(2,1)} async-done(((bf16[4,256,2048]{2,1,0:T(8,128)(2,1)}), bf16[1,256,2048]{2,1,0:T(8,128)(2,1)}) %reduce-scatter.31.cloned.1.call-update) | async-done | bytes 1048592
  698.7 2.8 bitcast_convert_fusion
  701.5 57.4 %reduce-scatter.25.cloned.1.call-done = bf16[1,2,4,64,1152]{4,3,2,1,0:T(8,128)(2,1)} async-done(((bf16[4,2,4,64,1152]{4,3,2,1,0:T(8,128)(2,1)}), bf16[1,2,4,64,1152]{4,3,2,1,0:T(8,128)(2,1)}) %reduce-scatter.25.cloned.1.call-update) | async-done | bytes 1179664
  762.1 2.0 reshape.322
  765.3 2.5 copy.136
  767.8 20.5 %reduce-scatter.23.cloned.1.call-done = bf16[1,64,2048]{2,1,0:T(8,128)(2,1)} async-done(((bf16[4,64,2048]{2,1,0:T(8,128)(2,1)}), bf16[1,64,2048]{2,1,0:T(8,128)(2,1)}) %reduce-scatter.23.cloned.1.call-update) | async-done | bytes 262160 | tf_op jit(solution)/shard_map/reduce_scatter | solution.py:62
  790.1 55.1 %all-reduce.7.cloned.1.call-done = bf16[2,4,64,1152]{3,2,1,0:T(8,128)(2,1)} async-done(((bf16[2,4,64,1152]{3,2,1,0:T(8,128)(2,1)}), bf16[2,4,64,1152]{3,2,1,0:T(8,128)(2,1)}) %all-reduce.7.cloned.1.call-update) | async-done | bytes 1179664
  846.8 4.0 all_to_all.42
  (230 shorter events, 56.8 us)
Async XLA Ops:
  7.2 68.4 %copy-start.20 = (bf16[64]{0:T(256)(128)(2,1)S(1)}, bf16[64]{0:T(256)(128)(2,1)}, u32[]{:S(2)}) copy-start(bf16[64]{0:T(256)(128)(2,1)} %param.19) | copy-start | bytes 388
  7.2 68.4 %copy-start.21 = (bf16[64]{0:T(256)(128)(2,1)S(1)}, bf16[64]{0:T(256)(128)(2,1)}, u32[]{:S(2)}) copy-start(bf16[64]{0:T(256)(128)(2,1)} %param.20) | copy-start | bytes 388
  7.2 68.4 %copy-start.22 = (bf16[64]{0:T(256)(128)(2,1)S(1)}, bf16[64]{0:T(256)(128)(2,1)}, u32[]{:S(2)}) copy-start(bf16[64]{0:T(256)(128)(2,1)} %param.22) | copy-start | bytes 388
  7.2 68.4 %copy-start.28 = (bf16[4]{0:T(256)(128)(2,1)S(1)}, bf16[4]{0:T(256)(128)(2,1)}, u32[]{:S(2)}) copy-start(bf16[4]{0:T(256)(128)(2,1)} %param.24) | copy-start | bytes 28
  7.2 68.4 %copy-start.23 = (bf16[64]{0:T(256)(128)(2,1)S(1)}, bf16[64]{0:T(256)(128)(2,1)}, u32[]{:S(2)}) copy-start(bf16[64]{0:T(256)(128)(2,1)} %param.26) | copy-start | bytes 388
  7.3 68.4 %copy-start.24 = (bf16[64]{0:T(256)(128)(2,1)S(1)}, bf16[64]{0:T(256)(128)(2,1)}, u32[]{:S(2)}) copy-start(bf16[64]{0:T(256)(128)(2,1)} %param.27) | copy-start | bytes 388
  7.3 68.4 %copy-start.25 = (bf16[64]{0:T(256)(128)(2,1)S(1)}, bf16[64]{0:T(256)(128)(2,1)}, u32[]{:S(2)}) copy-start(bf16[64]{0:T(256)(128)(2,1)} %param.28) | copy-start | bytes 388
  7.3 68.4 %copy-start.27 = (bf16[256]{0:T(256)(128)(2,1)S(1)}, bf16[256]{0:T(256)(128)(2,1)}, u32[]{:S(2)}) copy-start(bf16[256]{0:T(256)(128)(2,1)} %param.30) | copy-start | bytes 1540
  7.3 68.4 %copy-start.26 = (bf16[64]{0:T(256)(128)(2,1)S(1)}, bf16[64]{0:T(256)(128)(2,1)}, u32[]{:S(2)}) copy-start(bf16[64]{0:T(256)(128)(2,1)} %param.32) | copy-start | bytes 388
  7.3 74.9 %copy-start.19 = (s32[1,512]{1,0:T(1,128)S(1)}, s32[1,512]{1,0:T(1,128)}, u32[]{:S(2)}) copy-start(s32[1,512]{1,0:T(1,128)} %param.18) | copy-start | bytes 6148
  7.3 75.5 %copy-start.2 = (bf16[1,128,2048]{2,1,0:T(8,128)(2,1)S(1)}, bf16[1,128,2048]{2,1,0:T(8,128)(2,1)}, u32[]{:S(2)}) copy-start(bf16[1,128,2048]{2,1,0:T(8,128)(2,1)} %param.17) | copy-start | bytes 1572868
  7.3 39.6 %all-gather.18.cloned.1.call-start = ((), (), s32[]{:S(2)}) async-start(), calls=%async_computation.18 | async-start | bytes 1474560 | tf_op jit(solution)/shard_map/all_gather | solution.py:59
  13.7 61.9 %all-gather.22.cloned.1.call-start = ((), (), s32[]{:S(2)}) async-start(), calls=%async_computation.20 | async-start | bytes 1310720 | tf_op jit(solution)/shard_map/all_gather | solution.py:59
  14.4 119.6 %all-gather.20.cloned.1.call-start = ((), (), s32[]{:S(2)}) async-start(), calls=%async_computation.19 | async-start | bytes 5898240 | tf_op jit(solution)/shard_map/all_gather | solution.py:59
  47.0 141.5 %all-gather.24.cloned.1.call-start = ((), (), s32[]{:S(2)}) async-start(), calls=%async_computation.21 | async-start | bytes 5242880 | tf_op jit(solution)/shard_map/all_gather | solution.py:59
  78.1 11.5 %all-to-all-start = ((bf16[32,2,354]{2,1,0:T(2,128)(2,1)}), bf16[32,2,354]{2,1,0:T(2,128)(2,1)S(1)}, u32[]{:S(2)}, u32[]{:S(2)}) async-start(bf16[32,2,354]{2,1,0:T(2,128)(2,1)} %reshape.348), calls=%async_computation | async-start | bytes 98304 | tf_op jit(solution)/shard_map/all_to_all | solution.py:88
  82.2 176.0 %all-gather.16.cloned.1.call-start = ((), (), s32[]{:S(2)}) async-start(), calls=%async_computation.15 | async-start | bytes 2621440 | tf_op jit(solution)/shard_map/all_gather | solution.py:59
  82.2 1.2 collective-permute-start.2
  82.7 222.1 %all-gather.26.cloned.1.call-start = ((), (), s32[]{:S(2)}) async-start(), calls=%async_computation.22 | async-start | bytes 2621440 | tf_op jit(solution)/shard_map/all_gather | solution.py:59
  90.3 47.6 %copy-start.16 = (bf16[128,2048]{1,0:T(8,128)(2,1)}, bf16[128,2048]{1,0:T(8,128)(2,1)S(1)}, u32[]{:S(2)}) copy-start(bf16[128,2048]{1,0:T(8,128)(2,1)S(1)} %fusion.37) | copy-start | bytes 1572868
  90.4 2.0 collective-permute-start
  151.9 1.6 collective-permute-start.1
  193.0 3.0 collective-permute-start.3
  199.3 158.9 %all-gather.28.cloned.1.call-start = ((), (), s32[]{:S(2)}) async-start(), calls=%async_computation.23 | async-start | bytes 5242880 | tf_op jit(solution)/shard_map/all_gather | solution.py:59
  256.6 156.1 %all-gather.30.cloned.1.call-start = ((), (), s32[]{:S(2)}) async-start(), calls=%async_computation.24 | async-start | bytes 5242880 | tf_op jit(solution)/shard_map/all_gather | solution.py:59
  257.4 222.3 %reduce-scatter.21.cloned.1.call-start = ((), (), s32[]{:S(2)}) async-start(), calls=%async_computation.16 | async-start | bytes 2621440 | tf_op jit(solution)/shard_map/reduce_scatter | solution.py:62
  258.2 46.8 %collective-permute-start.6 = (bf16[4,128,2048]{2,1,0:T(8,128)(2,1)}, bf16[4,128,2048]{2,1,0:T(8,128)(2,1)}, u32[]{:S(2)}, u32[]{:S(2)}) collective-permute-start(bf16[4,128,2048]{2,1,0:T(8,128)(2,1)} %all-gather.16.cloned.1.call-done), channel_id=1, source_target_pairs={{0,4},{4,0},{1,5},{5,1},{2,6},{6,2},{3,7},{7,3},{8,12},{12,8},{9,1... | collective-permute-start | bytes 6291464 | tf_op jit(solution)/shard_map/ppermute | solution.py:56
  304.9 4.8 collective-permute-start.4
  429.3 4.2 collective-permute-start.7
  435.6 90.1 %reduce-scatter.19.cloned.1.call-start = ((), (), s32[]{:S(2)}) async-start(), calls=%async_computation.14 | async-start | bytes 2621440 | tf_op jit(solution)/shard_map/reduce_scatter | solution.py:62
  444.4 81.3 %copy-start.3 = (bf16[1,128,2048]{2,1,0:T(8,128)(2,1)S(1)}, bf16[1,128,2048]{2,1,0:T(8,128)(2,1)}, u32[]{:S(2)}) copy-start(bf16[1,128,2048]{2,1,0:T(8,128)(2,1)} %param.33) | copy-start | bytes 1572868
  444.4 4.2 collective-permute-start.5
  450.7 79.9 %copy-start.11 = (bf16[2,128,8,128]{3,2,1,0:T(8,128)(2,1)S(1)}, bf16[2,128,8,128]{3,2,1,0:T(8,128)(2,1)}, u32[]{:S(2)}) copy-start(bf16[2,128,8,128]{3,2,1,0:T(8,128)(2,1)} %copy-done.10) | copy-start | bytes 1572868
  450.8 140.1 %reduce-scatter.27.cloned.1.call-start = ((), (), s32[]{:S(2)}) async-start(), calls=%async_computation.27 | async-start | bytes 5242880
  528.7 1.9 collective-permute-start.8
  534.0 109.0 %reduce-scatter.29.cloned.1.call-start = ((), (), s32[]{:S(2)}) async-start(), calls=%async_computation.28 | async-start | bytes 5242880
  543.5 155.2 %reduce-scatter.31.cloned.1.call-start = ((), (), s32[]{:S(2)}) async-start(), calls=%async_computation.29 | async-start | bytes 5242880
  561.8 1.6 collective-permute-start.9
  564.2 13.6 %all-to-all-start.3 = ((bf16[4,2,128,128]{3,2,1,0:T(8,128)(2,1)}), bf16[4,2,128,128]{3,2,1,0:T(8,128)(2,1)}, u32[]{:S(2)}, u32[]{:S(2)}) async-start(bf16[4,2,128,128]{3,2,1,0:T(8,128)(2,1)} %bitcast.283), calls=%async_computation.5 | async-start | bytes 524288 | tf_op jit(solution)/shard_map/all_to_all | solution.py:192
  568.2 190.6 %reduce-scatter.25.cloned.1.call-start = ((), (), s32[]{:S(2)}) async-start(), calls=%async_computation.26 | async-start | bytes 5898240
  583.8 204.5 %reduce-scatter.23.cloned.1.call-start = ((), (), s32[]{:S(2)}) async-start(), calls=%async_computation.17 | async-start | bytes 1310720 | tf_op jit(solution)/shard_map/reduce_scatter | solution.py:62
  590.6 2.9 collective-permute-start.10
  590.8 56.8 %copy-start.31 = (u32[32]{0:T(128)S(1)}, u32[32]{0:T(128)}, u32[]{:S(2)}) copy-start(u32[32]{0:T(128)} %constant.73) | copy-start | bytes 388
  595.2 163.7 %copy-start.9 = (f32[128,2048]{1,0:T(8,128)S(1)}, f32[128,2048]{1,0:T(8,128)}, u32[]{:S(2)}) copy-start(f32[128,2048]{1,0:T(8,128)} %get-tuple-element.25) | copy-start | bytes 3145732
  596.2 46.8 %all-to-all-start.4 = ((f32[32,1,708]{2,1,0:T(1,128)}), f32[32,1,708]{2,1,0:T(1,128)S(1)}, u32[]{:S(2)}, u32[]{:S(2)}) async-start(f32[32,1,708]{2,1,0:T(1,128)} %all_to_all.29), calls=%async_computation.6 | async-start | bytes 196608 | tf_op jit(solution)/shard_map/all_to_all | solution.py:224
  643.0 119.1 %all-to-all-start.6 = ((bf16[8,64,1024]{2,1,0:T(8,128)(2,1)}), bf16[8,64,1024]{2,1,0:T(8,128)(2,1)}, u32[]{:S(2)}, u32[]{:S(2)}) async-start(bf16[8,64,1024]{2,1,0:T(8,128)(2,1)} %bitcast.281), calls=%async_computation.9 | async-start | bytes 2097152 | tf_op jit(solution)/shard_map/all_to_all | solution.py:168
  647.6 197.5 %all-reduce.7.cloned.1.call-start = ((), (), s32[]{:S(2)}) async-start(), calls=%async_computation.25 | async-start | bytes 2359296
  765.3 88.0 %copy-start.1 = (bf16[64,256]{1,0:T(8,128)(2,1)S(1)}, bf16[64,256]{1,0:T(8,128)(2,1)}, u32[]{:S(2)}) copy-start(bf16[64,256]{1,0:T(8,128)(2,1)} %param.23) | copy-start | bytes 98308
  (16 other events, 133.7 us)
Sparse Core Ops, SparseCore 0:
  13.8 33.1 all-gather.17
  48.5 27.0 all-gather.21
  77.4 56.5 all-gather.19
  135.7 52.6 all-gather.23
  189.9 68.2 all-gather.15
  260.2 44.6 all-gather.25
  306.7 51.4 all-gather.27
  360.0 52.6 all-gather.29
  435.8 43.8 reduce-scatter.20
  482.5 43.1 reduce-scatter.18
  534.1 51.9 reduce-scatter.26
  589.2 53.7 reduce-scatter.28
  645.9 52.6 reduce-scatter.30
  701.8 57.0 reduce-scatter.24
  761.1 27.1 reduce-scatter.22
  790.5 54.5 all-reduce.6

commit v2 on v1

v2 whole, which is shorter than its diff:
```python
import jax
import jax.numpy as jnp
from jax import lax
from jax.sharding import Mesh, PartitionSpec as P

HEADS = 16
HD = 128
EPS = 1e-05
GELU_K = 0.7978845608028654
GELU_C = 0.044715

BF = jnp.bfloat16
F32 = jnp.float32
CHIP = ("a", "b")
EVERY = ("a", "b", "core", "ctx")
MATES = [(0, 1), (1, 0)]


def dot(a, b, dims):
    return lax.dot_general(a, b, (dims, ((), ())), preferred_element_type=F32)


def mm(a, b):
    return dot(a, b, ((1,), (0,)))


def mm_nt(a, b):
    return dot(a, b, ((1,), (1,)))


def mm_tn(a, b):
    return dot(a, b, ((0,), (0,)))


def ln_stats(x):
    mean = jnp.mean(x, axis=-1, keepdims=True)
    cen = x - mean
    var = jnp.mean(cen * cen, axis=-1, keepdims=True)
    rstd = lax.rsqrt(var + EPS)
    return cen * rstd, rstd


def ln_back(dh, gain, xhat, rstd):
    e = dh * gain
    me = jnp.mean(e, axis=-1, keepdims=True)
    mx = jnp.mean(e * xhat, axis=-1, keepdims=True)
    return (e - me - xhat * mx) * rstd


def after(x, *others):
    return lax.optimization_barrier((x, others))[0]


def swap_core(x):
    return lax.ppermute(x, "core", MATES)


def over_a(x):
    return lax.ppermute(x, "a", MATES)


def over_b(x):
    return lax.ppermute(x, "b", MATES)


def gather(x, axes):
    return lax.all_gather(x, axes, axis=0, tiled=False)


def scatter(x, axes):
    return lax.psum_scatter(x, axes, scatter_dimension=0, tiled=False)


class Order:
    def __init__(self):
        self.last = []

    def mark(self, *done):
        self.last = list(done)

    def __call__(self, *xs):
        xs = lax.optimization_barrier((xs, self.last))[0]
        return xs[0] if len(xs) == 1 else xs


class ChipGather:
    def __init__(self, x, square):
        self.square = square
        if not square:
            self.pieces = list(gather(x, CHIP).reshape((-1,) + x.shape))
            return
        self.pieces = [x, over_b(x), over_a(x)]

    def pass_on(self, order):
        if self.square:
            x, x1, x2 = self.pieces
            x1, x2 = order(x1, x2)
            half = x.shape[0] // 2
            self.pieces = [x, x1, x2, over_a(x1[:half]), over_b(x2[half:])]


class ChipSum:
    def __init__(self, term, square, count):
        self.square, self.term = square, term
        self.far = []
        if not square:
            full = jnp.stack([term((i, 0), (i, 1)) for i in range(count)])
            self.result = scatter(full.astype(BF), CHIP).astype(F32)
            self.sent = [full]
            return
        u = term((3, 0), (1, 0)).astype(BF)
        w = term((3, 1), (2, 1)).astype(BF)
        self.sent = [u, w]
        self.near = [over_b(u), over_a(w)]

    def pass_on(self, order):
        if self.square:
            u, w = self.near = order(*self.near)
            half = u.shape[0] // 2
            u = (self.term((2, 0)) + u[:half].astype(F32)).astype(BF)
            w = (self.term((1, 1)) + w[:half].astype(F32)).astype(BF)
            self.sent = [u, w]
            self.far = [over_a(u), over_b(w)]

    def finish(self, order):
        if not self.square:
            return self.result
        f0, f1 = order(*self.far)
        half = f0.shape[0]
        n0, n1 = self.near[0][half:], self.near[1][half:]
        return self.term((0, 0), (0, 1)) + (
            jnp.concatenate([n0, n1]).astype(F32) + jnp.concatenate([f0, f1]).astype(F32)
        )


def make_local(A, B, Z):
    C = 2
    AB = A * B
    N = AB * C * Z
    square = A == 2 and B == 2

    def turn(x, me):
        if not square:
            return x
        w = x.shape[1] // AB
        cols = [x[:, i * w : (i + 1) * w] for i in range(AB)]
        return jnp.concatenate([lax.select_n(me ^ i, *cols) for i in range(AB)], axis=1)

    def product(left, right):
        half = left.shape[1] // AB // 2
        return lambda *parts: mm_tn(
            jnp.concatenate([left[:, (2 * i + j) * half : (2 * i + j + 1) * half] for i, j in parts], axis=1), right
        )

    def local(
        activations, segment_ids,
        ln1_gain, ln1_bias, q_weight, q_bias, kv_weight, v_bias, out_weight, out_bias,
        ln2_gain, ln2_bias, up_weight, up_bias, down_weight, down_bias, cotangent,
    ):
        T, D = activations.shape[1:]
        S = segment_ids.shape[1]
        R = q_weight.shape[0]
        F0 = down_weight.shape[0]
        F = AB * F0
        FF = up_weight.shape[1]
        DH = D // 2
        HH = HEADS // 2
        aligned = (Z * R) % HD == 0
        G = AB if aligned else 1
        W0 = DH // G
        E = DH + HD
        c = lax.axis_index("core")
        z = lax.axis_index("ctx")
        me = lax.axis_index("a") * B + lax.axis_index("b")

        order = Order()

        def half_of(i):
            cols = [q_weight[:, (g * 2 + i) * W0 : (g * 2 + i + 1) * W0] for g in range(G)]
            return jnp.concatenate(cols + [kv_weight[:, i * HD : (i + 1) * HD]], axis=1)

        first, second = half_of(0), half_of(1)
        mine = jnp.where(c == 0, first, second)
        mate = swap_core(jnp.where(c == 0, second, first))
        w_ext = jnp.concatenate([jnp.where(c == 0, mine, mate), jnp.where(c == 0, mate, mine)])
        order.mark(w_ext)
        w_ext_z = gather(w_ext, "ctx").reshape(Z, 2, R, E).transpose(1, 0, 2, 3).reshape(2 * Z * R, E)

        down_gather = ChipGather(order(down_weight), square)
        order.mark(w_ext)
        small, xin = order(
            [ln1_gain, ln1_bias, q_bias, out_bias, ln2_gain, ln2_bias, down_bias, up_bias, v_bias], activations[0]
        )
        vb0 = v_bias.shape[0]
        small = jnp.concatenate(small)
        small = jnp.broadcast_to(small[None], (N, small.shape[0]))
        small = lax.all_to_all(small, EVERY, 0, 0, tiled=True).astype(F32)
        g1, b1, bq, bo, g2, b2, bd = (small[:, i * R : (i + 1) * R].reshape(D) for i in range(7))
        bu = small[:, 7 * R : 7 * R + F0].reshape(AB, C * Z, F0)
        bu = lax.dynamic_index_in_dim(bu, c * Z + z, 1, keepdims=False).reshape(F)
        bv = small[:, 7 * R + F0 :].reshape(HD)
        bq = lax.dynamic_index_in_dim(bq.reshape(G, 2, W0), c, 1, keepdims=False).reshape(DH)
        b_ext = jnp.concatenate([bq, jnp.where(c == 1, bv, 0.0)])
        x = xin.astype(F32)
        xhat1, rstd1 = ln_stats(x)
        h1 = turn((xhat1 * g1 + b1).astype(BF), me)
        h1 = jnp.concatenate([h1, swap_core(h1)])
        seg = jnp.concatenate([segment_ids, swap_core(segment_ids)])
        start = z * T
        seg_q = lax.dynamic_slice_in_dim(seg, start, T, axis=1)
        q_at = start + jnp.arange(T, dtype=jnp.int32)
        k_at = jnp.arange(S, dtype=jnp.int32)
        allowed = (k_at[None, None, :] <= q_at[None, :, None]) & (seg[:, None, :] == seg_q[:, :, None])
        order.mark(b_ext)
        down_gather.pass_on(order)
        order.mark(h1, down_gather.pieces[1:3])

        out_in = after(out_weight, w_ext_z)
        up_in = after(up_weight, w_ext_z)
        w_ext_z = order(w_ext_z)
        ext_gather = ChipGather(w_ext_z, square)
        if aligned:
            w_out_z = gather(out_in, "ctx").reshape(Z * R, D)
        else:
            w_out = gather(out_in, EVERY).reshape(2, DH, D)
            w_out = w_out_z = lax.dynamic_index_in_dim(w_out, c, 0, keepdims=False)
        up_cols = [
            jnp.concatenate([up_in[:, (i * C * Z + j) * F0 : (i * C * Z + j + 1) * F0] for i in range(AB)], axis=1)
            for j in range(C * Z)
        ]
        w_up = lax.all_to_all(jnp.stack(up_cols), ("core", "ctx"), 0, 0, tiled=True)
        ext_gather.pass_on(order)

        w_ext = jnp.concatenate(ext_gather.pieces)
        order.mark(w_ext)
        w_out_z, h1, w_up = order(w_out_z, h1, w_up)
        if aligned:
            out_gather = ChipGather(w_out_z, square)
        cot_z = gather(after(cotangent[0], w_out_z), "ctx").reshape(Z * T, D)
        q_ext = (mm(h1, w_ext) + b_ext).astype(BF)
        kv = gather(q_ext[:, DH:].reshape(2, T, HD), "ctx").transpose(1, 0, 2, 3).reshape(2, S, HD)
        q = q_ext[:, :DH]
        if aligned:
            q = turn(q, me)
        q = q.reshape(2, T, HH, HD)
        kv_mate = swap_core(kv)[::-1]
        k = jnp.where(c == 0, kv, kv_mate)
        v = jnp.where(c == 0, kv_mate, kv)
        order.mark(kv)
        q, k, cot_z = order(q, k, cot_z)
        s = jnp.einsum("rthd,rjd->rhtj", q, k, preferred_element_type=F32) * HD**-0.5
        s = jnp.where(allowed[:, None], s, -1e30)
        p = jnp.exp(s - jnp.max(s, axis=-1, keepdims=True))
        p = p / jnp.sum(p, axis=-1, keepdims=True)
        pb = p.astype(BF)
        o = jnp.einsum("rhtj,rjd->rthd", pb, v, preferred_element_type=F32)
        o = o.astype(BF).reshape(2 * T, DH)
        if aligned:
            order.mark(o)
            out_gather.pass_on(order)
            w_out = jnp.concatenate(out_gather.pieces)
        order.mark(w_out, cot_z)
        o_w, w_up_z = order(o, w_up.reshape(C * Z * R, F))
        up_gather = ChipGather(w_up_z, square)
        away = swap_core(mm(o_w[T:], w_out))
        mid = x + bo + mm(o_w[:T], w_out) + away

        xhat2, rstd2 = ln_stats(mid)
        h2 = turn((xhat2 * g2 + b2).astype(BF), me)
        h2_z = gather(h2, "ctx").reshape(Z * T, D)

        order.mark(h2)
        up_gather.pass_on(order)
        half = Z * T
        cot_z, down_pieces = order(cot_z, down_gather.pieces)
        cots = [cot_z, swap_core(cot_z)]
        if square:
            w_down = jnp.zeros((F, D), BF)
            places = [(0, 0), (1, 0), (2, 0), (3, 0), (3, 1)]
            for part, (block, j) in zip(down_pieces, places):
                at = (me ^ block) * F0 + j * (F0 // 2)
                w_down = lax.dynamic_update_slice_in_dim(w_down, part, at, 0)
        else:
            w_down = jnp.concatenate(down_pieces)
        dacts = [mm_nt(part, w_down) for part in cots]
        w_up = jnp.concatenate(up_gather.pieces)
        order.mark(dacts, w_up)
        h2_z = order(h2_z)
        h2s = [h2_z, swap_core(h2_z)]
        acts, dpres = [], []
        for part, dact in zip(h2s, dacts):
            pre = mm(part, w_up) + bu
            th = jnp.tanh(GELU_K * (pre + GELU_C * pre * pre * pre))
            slope = 1.0 - th * th
            dgelu = 0.5 * (1.0 + th) + 0.5 * pre * slope * GELU_K * (1.0 + 3.0 * GELU_C * pre * pre)
            acts.append((0.5 * pre * (1.0 + th)).astype(BF))
            dpres.append((dact * dgelu).astype(BF))
        away = swap_core(mm_nt(dpres[1], w_up).astype(BF))
        dh2_part = (mm_nt(after(dpres[0], away), w_up) + away.astype(F32)).astype(BF).reshape(Z, T, D)
        order.mark(dh2_part)
        dh2 = turn(scatter(dh2_part, "ctx").astype(F32), me)
        dpre_w, act_w, h2_all, cot_all = (jnp.concatenate(order(*pair)) for pair in (dpres, acts, h2s, cots))

        def down_term(*parts):
            half = F0 // 2
            cols = [
                lax.dynamic_slice_in_dim(act_w, (me ^ i if square else i) * F0 + j * half, half, axis=1)
                for i, j in parts
            ]
            return mm_tn(jnp.concatenate(cols, axis=1), cot_all)

        down_sum = ChipSum(down_term, square, AB)
        order.mark(down_sum.sent)
        up_sum = ChipSum(product(order(h2_all), dpre_w), square, AB)
        out_away = swap_core(mm(order(acts[1]), w_down).astype(BF))
        order.mark(up_sum.sent, out_away)
        down_sum.pass_on(order)
        order.mark(down_sum.sent)
        mlp = (mm(order(acts[0]), w_down) + out_away.astype(F32)).astype(BF).reshape(Z, T, D)
        order.mark(mlp)
        mlp = scatter(mlp, "ctx")

        dh2 = order(dh2)
        order.mark(dh2)
        dmid = cotangent[0].astype(F32) + ln_back(dh2, g2, xhat2, rstd2)
        db = dmid.astype(BF)
        db = jnp.concatenate([db, swap_core(db)])
        do = mm_nt(db, w_out).astype(BF)
        order.mark(do)
        do_h = order(do).reshape(2, T, HH, HD)
        dp = jnp.einsum("rthd,rjd->rhtj", do_h, v, preferred_element_type=F32)
        ds = (p * (dp - jnp.sum(p * dp, axis=-1, keepdims=True))).astype(BF)
        dk = jnp.einsum("rhtj,rthd->rjd", ds, q, preferred_element_type=F32) * HD**-0.5
        dv = jnp.einsum("rhtj,rthd->rjd", pb, do_h, preferred_element_type=F32)
        dkv_away = swap_core(jnp.where(c == 0, dv, dk).astype(BF))
        dkv = jnp.where(c == 0, dk, dv) + dkv_away[::-1].astype(F32)
        dkv = dkv.astype(BF).reshape(2, Z, T, HD).transpose(1, 0, 2, 3)
        order.mark(dkv, down_sum.far)
        dkv = lax.all_to_all(dkv, "ctx", 0, 0, tiled=True)
        up_sum.pass_on(order)
        order.mark(up_sum.sent)
        ds_w, db_w = order(ds, db)
        dq = jnp.einsum("rhtj,rjd->rthd", ds_w, k, preferred_element_type=F32) * HD**-0.5
        dq = dq.astype(BF).reshape(2 * T, DH)
        if aligned:
            dq = turn(dq, me)
            out_sum = ChipSum(product(o, db_w), square, AB)
            order.mark(out_sum.sent, dq)
        dkv = order(dkv)
        dkv = jnp.sum(dkv.astype(F32), axis=0).astype(BF).reshape(2 * T, HD)
        dq_ext = jnp.concatenate([dq, dkv], axis=1)
        ext_sum = ChipSum(product(h1, dq_ext), square, AB)
        order.mark(ext_sum.sent)
        g_up = up_sum.finish(order).astype(BF).reshape(C * Z, R, F)
        order.mark(g_up)
        g_up = lax.all_to_all(g_up, ("core", "ctx"), 0, 0, tiled=True)
        if aligned:
            out_sum.pass_on(order)
            order.mark(out_sum.sent)
        ext_sum.pass_on(order)
        order.mark(ext_sum.sent)
        dq_w = order(dq_ext)
        dh1_away = swap_core(mm_nt(dq_w[T:], w_ext))
        dh1 = turn(mm_nt(dq_w[:T], w_ext) + dh1_away, me)

        if aligned:
            g_out = out_sum.finish(order).astype(BF).reshape(Z, R, D)
            order.mark(g_out)
            g_out = lax.all_to_all(g_out, "ctx", 0, 0, tiled=True)
            g_out = jnp.sum(g_out.astype(F32), axis=0)
        else:
            g_out = mm_tn(o, order(db)).astype(BF)
            full = jnp.where(lax.broadcasted_iota(jnp.int32, (2, 1, 1), 0) == c, g_out[None], 0)
            g_out = scatter(full.reshape(N, R, D), EVERY).astype(F32)
        order.mark(ext_sum.far, g_up)
        g_ext = ext_sum.finish(order).astype(BF).reshape(2, Z, R, E)
        g_ext = g_ext.transpose(1, 0, 2, 3).reshape(Z, 2 * R, E)
        order.mark(g_ext)
        g_ext = scatter(g_ext, "ctx").reshape(2, R, E)
        g_down = down_sum.finish(order)
        dx = dmid + ln_back(order(dh1), g1, xhat1, rstd1)
        first, second = g_ext[0], g_ext[1]
        mate = swap_core(jnp.where(c == 0, second, first))
        mine = jnp.where(c == 0, first, second)
        first, second = jnp.where(c == 0, mine, mate), jnp.where(c == 0, mate, mine)
        g_q = [h[:, g * W0 : (g + 1) * W0] for g in range(G) for h in (first, second)]
        g_q = jnp.concatenate(g_q, axis=1).astype(F32)
        g_kv = jnp.concatenate([first[:, DH:], second[:, DH:]], axis=1).astype(F32)
        g_up = order(g_up)
        g_up = g_up.reshape(C * Z, R, AB, F0).transpose(1, 2, 0, 3).reshape(R, FF).astype(F32)
        result = mid + order(mlp).astype(F32) + bd

        own_core = (lax.broadcasted_iota(jnp.int32, (1, 2, 1), 1) == c).astype(F32)
        own_cz = (lax.broadcasted_iota(jnp.int32, (1, C * Z, 1), 1) == c * Z + z).astype(F32)
        dh2_late, dpre_late, cot_late, dq_late, db_late = order(dh2, dpre_w, cotangent[0], dq_ext, db[:T])
        gb_up = jnp.sum(dpre_late.astype(F32), axis=0)
        gb_ext = jnp.sum(dq_late.astype(F32), axis=0)
        wide = [
            jnp.sum(dh1 * xhat1, axis=0),
            jnp.sum(dh1, axis=0),
            (gb_ext[:DH].reshape(G, 1, W0) * own_core).reshape(D),
            jnp.sum(db_late.astype(F32), axis=0),
            jnp.sum(dh2_late * xhat2, axis=0),
            jnp.sum(dh2_late, axis=0),
            jnp.sum(cot_late.astype(F32), axis=0),
        ]
        packed = jnp.concatenate(
            [w.reshape(N, R) for w in wide]
            + [
                (gb_up.reshape(AB, 1, F0) * own_cz).reshape(N, F0),
                jnp.where(c == 1, gb_ext[DH:], 0.0).reshape(N, vb0),
            ],
            axis=1,
        )
        packed = jnp.sum(lax.all_to_all(packed, EVERY, 0, 0, tiled=True), axis=0)
        vecs = [packed[i * R : (i + 1) * R] for i in range(7)]
        gb_up = packed[7 * R : 7 * R + F0]
        gb_v = packed[7 * R + F0 :]
        return (
            result.astype(BF)[None], dx.astype(BF)[None],
            vecs[0], vecs[1], g_q, vecs[2], g_kv, gb_v, g_out, vecs[3],
            vecs[4], vecs[5], g_up, gb_up, g_down, vecs[6],
        )

    return local


def solution(mesh):
    dp, ctx = mesh.shape["dp"], mesh.shape["ctx"]
    chips = dp // 2
    a = next(i for i in range(int(chips**0.5), 0, -1) if chips % i == 0)
    b = chips // a
    fine = Mesh(mesh.devices.reshape(a, b, 2, ctx), EVERY)
    tok = P(("a", "b", "core"), "ctx", None)
    vec = P(EVERY)
    mat = P(EVERY, None)
    in_specs = (
        tok, P(("a", "b", "core"), None),
        vec, vec, mat, vec, mat, vec, mat, vec, vec, vec, mat, vec, mat, vec, tok,
    )
    out_specs = (tok, tok, vec, vec, mat, vec, mat, vec, mat, vec, vec, vec, mat, vec, mat, vec)
    return jax.shard_map(
        make_local(a, b, ctx), mesh=fine, in_specs=in_specs, out_specs=out_specs, check_vma=False
    )
```

time: 869 us -> 552 us (0.64)
  waiting for transfers between devices: 601 us -> 227 us
  blocking collectives: 77.6 us -> 16.6 us
  local copies, waits for them, and re-layouts: 29 us -> 81.9 us
  starting transfers between devices: 19.2 us -> 60.4 us
  matrix products: 82.9 us -> 106 us
    all_gather x8 -> x4, waiting for transfers between devices: 268 us -> 33 us  [gather(): return lax.all_gather(x, axes, axis=0, tiled=False)]
    unnamed x21 -> x7, waiting for transfers between devices: 208 us -> 0.8 us
    ppermute x11 -> x45, waiting for transfers between devices: 18.3 us -> 148 us  [the longest x16 67.6 us: over_b(): return lax.ppermute(x, 'b', MATES)]
    reduce_scatter x3, waiting for transfers between devices: 93.8 us -> 0.02 us  [scatter(): return lax.psum_scatter(x, axes, scatter_dimension=0, tiled=False)]
    all_to_all x3 -> x0, blocking collectives: 63.7 us -> none  [the longest x1 55 us: local(): w_up = lax.all_to_all(w_up, ('core', 'ctx'), 0, 0, tiled=True)]
    ppermute x11 -> x45, starting transfers between devices: 1.25 us -> 36.2 us  [the longest x16 20.3 us: over_b(): return lax.ppermute(x, 'b', MATES)]
    unnamed x76 -> x226, local copies, waits for them, and re-layouts: 8.95 us -> 39.8 us
    dot_general x12 -> x34, matrix products: 78.2 us -> 102 us  [dot(): return lax.dot_general(a, b, (dims, ((), ())), preferred_element_type=F32)]
  transfers between devices with their start and end apart: 31 -> 58, of which waited for: 26 -> 30; matrix products, arithmetic and copies ran while one was open for 13% -> 31% of each run, Pallas kernels for 0% -> 0%
where the time goes in v2:
time: 552 us; the launch traced here: 545 us
  waiting for transfers between devices  227 us (41%)
  matrix products  106 us (19%)
  local copies, waits for them, and re-layouts  81.9 us (15%)
  starting transfers between devices  60.4 us (11%)
  other arithmetic  36.2 us (7%)
  blocking collectives  16.6 us (3%)
  between operations  16.4 us (3%)
    dot_general x34, matrix products, dot(): return lax.dot_general(a, b, (dims, ((), ())), preferred_element_type=F32)  102 us
    ppermute x16, waiting for transfers between devices, over_b(): return lax.ppermute(x, 'b', MATES)  67.6 us
    ppermute x16, waiting for transfers between devices, over_a(): return lax.ppermute(x, 'a', MATES)  67.5 us
    unnamed x226, local copies, waits for them, and re-layouts  39.8 us
    all_gather x4, waiting for transfers between devices, gather(): return lax.all_gather(x, axes, axis=0, tiled=False)  33 us
    ppermute x16, starting transfers between devices, over_b(): return lax.ppermute(x, 'b', MATES)  20.3 us
    all_to_all x1, waiting for transfers between devices, local(): g_out = lax.all_to_all(g_out, 'ctx', 0, 0, tiled=True)  20 us
    all_to_all x1, waiting for transfers between devices, local(): small = lax.all_to_all(small, EVERY, 0, 0, tiled=True).astype(F32)  17.2 us
  transfers between devices with their start and end apart: 58, of which 30 were waited for; matrix products, arithmetic and copies ran while one was open for 31% of the time, Pallas kernels for 0%

profile of v2, /device:TPU:0, one launch (start us, length us, event | category | flops | bytes accessed | tf_op | source)
XLA Modules:
  0.0 544.8 jit_solution(15953346331539670449)
XLA Ops:
  15.1 2.9 collective-permute-start.2
  21.9 4.0 all-to-all-start
  26.4 17.2 %all-to-all-done = bf16[32,2,354]{2,1,0:T(2,128)(2,1)S(1)} async-done(((bf16[32,2,354]{2,1,0:T(2,128)(2,1)}), bf16[32,2,354]{2,1,0:T(2,128)(2,1)S(1)}, u32[]{:S(2)}, u32[]{:S(2)}) %all-to-all-start) | async-done | bytes 45344 | tf_op jit(solution)/shard_map/all_to_all | solution.py:197
  61.0 4.9 all-to-all-start.1
  66.7 15.0 %collective-permute-done.4 = bf16[512,1152]{1,0:T(8,128)(2,1)} collective-permute-done((bf16[512,1152]{1,0:T(8,128)(2,1)S(1)}, bf16[512,1152]{1,0:T(8,128)(2,1)}, u32[]{:S(2)}, u32[]{:S(2)}) %collective-permute-start.4) | collective-permute-done | bytes 1179680 | tf_op jit(solution)/shard_map/ppermute | solution.py:63
  88.4 2.4 constant_dynamic-update-slice_fusion.13
  90.8 2.4 constant_dynamic-update-slice_fusion.12
  93.2 4.9 collective-permute-done.6
  101.9 7.8 %all-gather.11.cloned.1.call-done = bf16[256,2048]{1,0:T(8,128)(2,1)} async-done(((bf16[64,2048]{1,0:T(8,128)(2,1)}), bf16[256,2048]{1,0:T(8,128)(2,1)}) %all-gather.11.cloned.1.call-update) | async-done | bytes 1048592 | tf_op jit(solution)/shard_map/all_gather | solution.py:67
  113.4 3.9 fusion.7
  117.3 16.6 %all_gather.31 = bf16[4,2,128,128]{3,2,1,0:T(8,128)(2,1)S(1)} all-gather(bf16[1,2,128,128]{3,2,1,0:T(8,128)(2,1)S(1)} %bitcast.250), channel_id=1, replica_groups=mesh['a'=2,'b'=2,'core'=2,'ctx'=4] {'ctx'}, dimensions={0}, use_global_device_ids=true | all-gather | bytes 327680 | tf_op jit(solution)/shard_map/all_gather | solution.py:67
  135.6 25.1 %all-gather.13.cloned.1.call-done = bf16[512,2048]{1,0:T(8,128)(2,1)} async-done(((bf16[128,2048]{1,0:T(8,128)(2,1)}), bf16[512,2048]{1,0:T(8,128)(2,1)}) %all-gather.13.cloned.1.call-update) | async-done | bytes 2097168 | tf_op jit(solution)/shard_map/all_gather | solution.py:67
  174.2 7.3 %collective-permute-done.12 = bf16[128,2048]{1,0:T(8,128)(2,1)S(1)} collective-permute-done((bf16[128,2048]{1,0:T(8,128)(2,1)S(1)}, bf16[128,2048]{1,0:T(8,128)(2,1)S(1)}, u32[]{:S(2)}, u32[]{:S(2)}) %collective-permute-start.12) | collective-permute-done | bytes 524320 | tf_op jit(solution)/shard_map/ppermute | solution.py:59
  181.6 2.3 collective-permute-done.13
  196.8 3.4 fusion.159
  202.1 28.0 %collective-permute-done.18 = bf16[512,1024]{1,0:T(8,128)(2,1)} collective-permute-done((bf16[512,1024]{1,0:T(8,128)(2,1)S(1)}, bf16[512,1024]{1,0:T(8,128)(2,1)}, u32[]{:S(2)}, u32[]{:S(2)}) %collective-permute-start.18) | collective-permute-done | bytes 1048608 | tf_op jit(solution)/shard_map/ppermute | solution.py:63
  242.5 3.7 fusion.160
  248.9 3.7 fusion.161
  252.7 4.4 collective-permute-done.22
  257.1 5.1 fusion.162
  262.3 6.6 %multiply_convert_fusion.1 = (bf16[512,1024]{1,0:T(8,128)(2,1)}, bf16[512,1024]{1,0:T(8,128)(2,1)}, bf16[512,1024]{1,0:T(8,128)(2,1)}, bf16[512,1024]{1,0:T(8,128)(2,1)S(1)}) fusion(f32[1024]{0:T(1024)S(1)} %bitcast.252, f32[512,1024]{1,0:T(8,128)S(1)} %copy-done.93, f32[512,1024]{1,0:T(8,128)S(1)} %fusion.162, f32[512,1024]{1,0:T(8,128)S(1)} %copy-done.94, ...), kind=kOutput, calls=%fused_computation.56 | convolution fusion | flops 2170552320 | bytes 16781312 | tf_op jit(solution)/shard_map/dot_general | solution.py:20
  268.9 3.7 convolution_convert_fusion.1
  272.7 4.4 collective-permute-done.23
  277.1 6.6 %add_convert_fusion.1 = bf16[512,2048]{1,0:T(8,128)(2,1)} fusion(bf16[512,2048]{1,0:T(8,128)(2,1)} %collective-permute-done.23, bf16[512,1024]{1,0:T(8,128)(2,1)S(1)} %copy-done.52, bf16[2048,1024]{1,0:T(8,128)(2,1)} %copy-done.60), kind=kOutput, calls=%fused_computation.10 | convolution fusion | flops 2150629376 | bytes 9437184 | tf_op jit(solution)/shard_map/dot_general | solution.py:20
  295.4 3.7 convolution_convert_fusion
  300.7 2.8 pad_maximum_fusion
  310.3 14.5 %collective-permute-done.25 = bf16[256,2048]{1,0:T(8,128)(2,1)S(1)} collective-permute-done((bf16[256,2048]{1,0:T(8,128)(2,1)}, bf16[256,2048]{1,0:T(8,128)(2,1)S(1)}, u32[]{:S(2)}, u32[]{:S(2)}) %collective-permute-start.25) | collective-permute-done | bytes 1048608 | tf_op jit(solution)/shard_map/ppermute | solution.py:59
  329.1 5.3 add_convert_fusion
  352.8 4.1 all-to-all-start.2
  356.9 8.6 %collective-permute-done.29 = bf16[512,1024]{1,0:T(8,128)(2,1)} collective-permute-done((bf16[512,1024]{1,0:T(8,128)(2,1)}, bf16[512,1024]{1,0:T(8,128)(2,1)}, u32[]{:S(2)}, u32[]{:S(2)}) %collective-permute-start.29) | collective-permute-done | bytes 1048608 | tf_op jit(solution)/shard_map/ppermute | solution.py:59
  367.5 10.5 %collective-permute-done.32 = bf16[128,2048]{1,0:T(8,128)(2,1)} collective-permute-done((bf16[128,2048]{1,0:T(8,128)(2,1)}, bf16[128,2048]{1,0:T(8,128)(2,1)}, u32[]{:S(2)}, u32[]{:S(2)}) %collective-permute-start.32) | collective-permute-done | bytes 524320 | tf_op jit(solution)/shard_map/ppermute | solution.py:63
  378.1 3.4 add_convert_fusion.8
  381.4 2.9 add_convert_fusion.9
  402.8 4.4 add_convert_fusion.2
  407.2 4.3 all-to-all-start.3
  411.9 11.1 %collective-permute-done.36 = bf16[256,2048]{1,0:T(8,128)(2,1)} collective-permute-done((bf16[256,2048]{1,0:T(8,128)(2,1)}, bf16[256,2048]{1,0:T(8,128)(2,1)}, u32[]{:S(2)}, u32[]{:S(2)}) %collective-permute-start.36) | collective-permute-done | bytes 1048608 | tf_op jit(solution)/shard_map/ppermute | solution.py:59
  429.5 18.8 %collective-permute-done.34 = bf16[512,1152]{1,0:T(8,128)(2,1)} collective-permute-done((bf16[512,1152]{1,0:T(8,128)(2,1)}, bf16[512,1152]{1,0:T(8,128)(2,1)}, u32[]{:S(2)}, u32[]{:S(2)}) %collective-permute-start.34) | collective-permute-done | bytes 1179680 | tf_op jit(solution)/shard_map/ppermute | solution.py:59
  459.4 5.0 fusion.84
  466.0 3.4 collective-permute-done.40
  474.0 2.6 fusion.149
  480.3 2.5 copy.104
  483.6 5.1 convolution_add_fusion.3
  488.7 4.3 convolution_add_fusion.7
  495.4 2.6 all-to-all-start.4
  498.3 7.6 %all-to-all-done.4 = f32[32,1,708]{2,1,0:T(1,128)S(1)} async-done(((f32[32,1,708]{2,1,0:T(1,128)}), f32[32,1,708]{2,1,0:T(1,128)S(1)}, u32[]{:S(2)}, u32[]{:S(2)}) %all-to-all-start.4) | async-done | bytes 90656 | tf_op jit(solution)/shard_map/all_to_all | solution.py:415
  505.9 3.5 all-to-all-start.5
  509.4 2.5 fusion.60
  514.9 20.0 %all-to-all-done.5 = bf16[4,64,2048]{2,1,0:T(8,128)(2,1)S(1)} async-done(((bf16[4,64,2048]{2,1,0:T(8,128)(2,1)}), bf16[4,64,2048]{2,1,0:T(8,128)(2,1)S(1)}, u32[]{:S(2)}, u32[]{:S(2)}) %all-to-all-start.5) | async-done | bytes 1048608 | tf_op jit(solution)/shard_map/all_to_all | solution.py:369
  (504 shorter events, 188.7 us)
Async XLA Ops:
  7.3 43.7 %all-gather.9.cloned.1.call-start = ((), (), s32[]{:S(2)}) async-start(), calls=%async_computation.12 | async-start | bytes 1474560 | tf_op jit(solution)/shard_map/all_gather | solution.py:67
  15.1 35.9 %collective-permute-start.2 = (bf16[256,2048]{1,0:T(8,128)(2,1)}, bf16[256,2048]{1,0:T(8,128)(2,1)S(1)}, u32[]{:S(2)}, u32[]{:S(2)}) collective-permute-start(bf16[256,2048]{1,0:T(8,128)(2,1)} %param.31), channel_id=1, source_target_pairs={{0,8},{8,0},{1,9},{9,1},{2,10},{10,2},{3,11},{11,3},{4,12},{12,4},... | collective-permute-start | bytes 3145736 | tf_op jit(solution)/shard_map/ppermute | solution.py:63
  17.9 33.0 %collective-permute-start.3 = (bf16[256,2048]{1,0:T(8,128)(2,1)}, bf16[256,2048]{1,0:T(8,128)(2,1)S(1)}, u32[]{:S(2)}, u32[]{:S(2)}) collective-permute-start(bf16[256,2048]{1,0:T(8,128)(2,1)} %param.31), channel_id=1, source_target_pairs={{0,16},{16,0},{1,17},{17,1},{2,18},{18,2},{3,19},{19,3},{4,20},{20... | collective-permute-start | bytes 3145736 | tf_op jit(solution)/shard_map/ppermute | solution.py:59
  21.9 21.7 %all-to-all-start = ((bf16[32,2,354]{2,1,0:T(2,128)(2,1)}), bf16[32,2,354]{2,1,0:T(2,128)(2,1)S(1)}, u32[]{:S(2)}, u32[]{:S(2)}) async-start(bf16[32,2,354]{2,1,0:T(2,128)(2,1)} %reshape.308), calls=%async_computation | async-start | bytes 98304 | tf_op jit(solution)/shard_map/all_to_all | solution.py:197
  53.4 28.2 %collective-permute-start.4 = (bf16[512,1152]{1,0:T(8,128)(2,1)S(1)}, bf16[512,1152]{1,0:T(8,128)(2,1)}, u32[]{:S(2)}, u32[]{:S(2)}) collective-permute-start(bf16[512,1152]{1,0:T(8,128)(2,1)S(1)} %bitcast.214), channel_id=1, source_target_pairs={{0,8},{8,0},{1,9},{9,1},{2,10},{10,2},{3,11},{11,3},{4,12},{12,4},... | collective-permute-start | bytes 3538952 | tf_op jit(solution)/shard_map/ppermute | solution.py:63
  54.7 28.0 %collective-permute-start.5 = (bf16[512,1152]{1,0:T(8,128)(2,1)S(1)}, bf16[512,1152]{1,0:T(8,128)(2,1)}, u32[]{:S(2)}, u32[]{:S(2)}) collective-permute-start(bf16[512,1152]{1,0:T(8,128)(2,1)S(1)} %bitcast.215), channel_id=1, source_target_pairs={{0,16},{16,0},{1,17},{17,1},{2,18},{18,2},{3,19},{19,3},{4,20},{20... | collective-permute-start | bytes 3538952 | tf_op jit(solution)/shard_map/ppermute | solution.py:59
  61.0 48.7 %all-to-all-start.1 = ((bf16[8,64,1024]{2,1,0:T(8,128)(2,1)}), bf16[8,64,1024]{2,1,0:T(8,128)(2,1)S(1)}, u32[]{:S(2)}, u32[]{:S(2)}) async-start(bf16[8,64,1024]{2,1,0:T(8,128)(2,1)} %fusion.111), calls=%async_computation.1 | async-start | bytes 2097152 | tf_op jit(solution)/shard_map/all_to_all | solution.py:231
  65.9 43.8 %all-gather.11.cloned.1.call-start = ((), (), s32[]{:S(2)}) async-start(), calls=%async_computation.13 | async-start | bytes 1310720 | tf_op jit(solution)/shard_map/all_gather | solution.py:67
  66.6 94.1 %all-gather.13.cloned.1.call-start = ((), (), s32[]{:S(2)}) async-start(), calls=%async_computation.14 | async-start | bytes 2621440 | tf_op jit(solution)/shard_map/all_gather | solution.py:67
  83.7 14.4 %collective-permute-start.6 = (bf16[256,1152]{1,0:T(8,128)(2,1)S(1)}, bf16[256,1152]{1,0:T(8,128)(2,1)S(1)}, u32[]{:S(2)}, u32[]{:S(2)}) collective-permute-start(bf16[256,1152]{1,0:T(8,128)(2,1)S(1)} %slice.510), channel_id=1, source_target_pairs={{0,16},{16,0},{1,17},{17,1},{2,18},{18,2},{3,19},{19,3},{4,20},{20... | collective-permute-start | bytes 1769480 | tf_op jit(solution)/shard_map/ppermute | solution.py:59
  86.8 14.1 %collective-permute-start.7 = (bf16[256,1152]{1,0:T(8,128)(2,1)S(1)}, bf16[256,1152]{1,0:T(8,128)(2,1)S(1)}, u32[]{:S(2)}, u32[]{:S(2)}) collective-permute-start(bf16[256,1152]{1,0:T(8,128)(2,1)S(1)} %slice.511), channel_id=1, source_target_pairs={{0,8},{8,0},{1,9},{9,1},{2,10},{10,2},{3,11},{11,3},{4,12},{12,4},... | collective-permute-start | bytes 1769480 | tf_op jit(solution)/shard_map/ppermute | solution.py:63
  109.7 142.8 %all-gather.15.cloned.1.call-start = ((), (), s32[]{:S(2)}) async-start(), calls=%async_computation.15 | async-start | bytes 2621440 | tf_op jit(solution)/shard_map/all_gather | solution.py:67
  111.3 55.1 %collective-permute-start.10 = (bf16[256,2048]{1,0:T(8,128)(2,1)}, bf16[256,2048]{1,0:T(8,128)(2,1)}, u32[]{:S(2)}, u32[]{:S(2)}) collective-permute-start(bf16[256,2048]{1,0:T(8,128)(2,1)} %all-gather.11.cloned.1.call-done), channel_id=1, source_target_pairs={{0,8},{8,0},{1,9},{9,1},{2,10},{10,2},{3,11},{11,3},{4,12},{12,4},... | collective-permute-start | bytes 3145736 | tf_op jit(solution)/shard_map/ppermute | solution.py:63
  112.9 53.5 %collective-permute-start.11 = (bf16[256,2048]{1,0:T(8,128)(2,1)}, bf16[256,2048]{1,0:T(8,128)(2,1)}, u32[]{:S(2)}, u32[]{:S(2)}) collective-permute-start(bf16[256,2048]{1,0:T(8,128)(2,1)} %all-gather.11.cloned.1.call-done), channel_id=1, source_target_pairs={{0,16},{16,0},{1,17},{17,1},{2,18},{18,2},{3,19},{19,3},{4,20},{20... | collective-permute-start | bytes 3145736 | tf_op jit(solution)/shard_map/ppermute | solution.py:59
  167.7 13.9 %collective-permute-start.12 = (bf16[128,2048]{1,0:T(8,128)(2,1)S(1)}, bf16[128,2048]{1,0:T(8,128)(2,1)S(1)}, u32[]{:S(2)}, u32[]{:S(2)}) collective-permute-start(bf16[128,2048]{1,0:T(8,128)(2,1)S(1)} %slice.517), channel_id=1, source_target_pairs={{0,16},{16,0},{1,17},{17,1},{2,18},{18,2},{3,19},{19,3},{4,20},{20... | collective-permute-start | bytes 1572872 | tf_op jit(solution)/shard_map/ppermute | solution.py:59
  170.4 13.6 %collective-permute-start.13 = (bf16[128,2048]{1,0:T(8,128)(2,1)S(1)}, bf16[128,2048]{1,0:T(8,128)(2,1)S(1)}, u32[]{:S(2)}, u32[]{:S(2)}) collective-permute-start(bf16[128,2048]{1,0:T(8,128)(2,1)S(1)} %slice.518), channel_id=1, source_target_pairs={{0,8},{8,0},{1,9},{9,1},{2,10},{10,2},{3,11},{11,3},{4,12},{12,4},... | collective-permute-start | bytes 1572872 | tf_op jit(solution)/shard_map/ppermute | solution.py:63
  192.8 42.3 %collective-permute-start.15 = (bf16[128,2048]{1,0:T(8,128)(2,1)}, bf16[128,2048]{1,0:T(8,128)(2,1)}, u32[]{:S(2)}, u32[]{:S(2)}) collective-permute-start(bf16[128,2048]{1,0:T(8,128)(2,1)} %slice.527), channel_id=1, source_target_pairs={{0,16},{16,0},{1,17},{17,1},{2,18},{18,2},{3,19},{19,3},{4,20},{20... | collective-permute-start | bytes 1572872 | tf_op jit(solution)/shard_map/ppermute | solution.py:59
  193.4 41.7 %collective-permute-start.16 = (bf16[128,2048]{1,0:T(8,128)(2,1)}, bf16[128,2048]{1,0:T(8,128)(2,1)}, u32[]{:S(2)}, u32[]{:S(2)}) collective-permute-start(bf16[128,2048]{1,0:T(8,128)(2,1)} %slice.528), channel_id=1, source_target_pairs={{0,8},{8,0},{1,9},{9,1},{2,10},{10,2},{3,11},{11,3},{4,12},{12,4},... | collective-permute-start | bytes 1572872 | tf_op jit(solution)/shard_map/ppermute | solution.py:63
  194.6 35.5 %collective-permute-start.18 = (bf16[512,1024]{1,0:T(8,128)(2,1)S(1)}, bf16[512,1024]{1,0:T(8,128)(2,1)}, u32[]{:S(2)}, u32[]{:S(2)}) collective-permute-start(bf16[512,1024]{1,0:T(8,128)(2,1)S(1)} %bitcast.221), channel_id=1, source_target_pairs={{0,8},{8,0},{1,9},{9,1},{2,10},{10,2},{3,11},{11,3},{4,12},{12,4},... | collective-permute-start | bytes 3145736 | tf_op jit(solution)/shard_map/ppermute | solution.py:63
  195.4 34.7 %collective-permute-start.19 = (bf16[512,1024]{1,0:T(8,128)(2,1)S(1)}, bf16[512,1024]{1,0:T(8,128)(2,1)}, u32[]{:S(2)}, u32[]{:S(2)}) collective-permute-start(bf16[512,1024]{1,0:T(8,128)(2,1)S(1)} %bitcast.222), channel_id=1, source_target_pairs={{0,16},{16,0},{1,17},{17,1},{2,18},{18,2},{3,19},{19,3},{4,20},{20... | collective-permute-start | bytes 3145736 | tf_op jit(solution)/shard_map/ppermute | solution.py:59
  201.8 132.6 %reduce-scatter.6.cloned.1.call-start = ((), (), s32[]{:S(2)}) async-start(), calls=%async_computation.10 | async-start | bytes 2621440 | tf_op jit(solution)/shard_map/reduce_scatter | solution.py:71
  231.2 14.9 %collective-permute-start.20 = (bf16[256,1024]{1,0:T(8,128)(2,1)S(1)}, bf16[256,1024]{1,0:T(8,128)(2,1)S(1)}, u32[]{:S(2)}, u32[]{:S(2)}) collective-permute-start(bf16[256,1024]{1,0:T(8,128)(2,1)S(1)} %slice.529), channel_id=1, source_target_pairs={{0,16},{16,0},{1,17},{17,1},{2,18},{18,2},{3,19},{19,3},{4,20},{20... | collective-permute-start | bytes 1572872 | tf_op jit(solution)/shard_map/ppermute | solution.py:59
  233.8 12.9 %collective-permute-start.21 = (bf16[256,1024]{1,0:T(8,128)(2,1)S(1)}, bf16[256,1024]{1,0:T(8,128)(2,1)S(1)}, u32[]{:S(2)}, u32[]{:S(2)}) collective-permute-start(bf16[256,1024]{1,0:T(8,128)(2,1)S(1)} %slice.530), channel_id=1, source_target_pairs={{0,8},{8,0},{1,9},{9,1},{2,10},{10,2},{3,11},{11,3},{4,12},{12,4},... | collective-permute-start | bytes 1572872 | tf_op jit(solution)/shard_map/ppermute | solution.py:63
  235.1 11.7 %collective-permute-start.17 = (bf16[512,2048]{1,0:T(8,128)(2,1)S(1)}, bf16[512,2048]{1,0:T(8,128)(2,1)S(1)}, u32[]{:S(2)}, u32[]{:S(2)}) collective-permute-start(bf16[512,2048]{1,0:T(8,128)(2,1)S(1)} %copy-done.40), channel_id=1, source_target_pairs={{0,4},{4,0},{1,5},{5,1},{2,6},{6,2},{3,7},{7,3},{8,12},{12,8},{9,1... | collective-permute-start | bytes 6291464 | tf_op jit(solution)/shard_map/ppermute | solution.py:55
  283.7 190.2 %reduce-scatter.4.cloned.1.call-start = ((), (), s32[]{:S(2)}) async-start(), calls=%async_computation.9 | async-start | bytes 2621440 | tf_op jit(solution)/shard_map/reduce_scatter | solution.py:71
  299.0 25.8 %collective-permute-start.26 = (bf16[512,2048]{1,0:T(8,128)(2,1)}, bf16[512,2048]{1,0:T(8,128)(2,1)}, u32[]{:S(2)}, u32[]{:S(2)}) collective-permute-start(bf16[512,2048]{1,0:T(8,128)(2,1)} %convolution_convert_fusion), channel_id=1, source_target_pairs={{0,4},{4,0},{1,5},{5,1},{2,6},{6,2},{3,7},{7,3},{8,12},{12,8},{9,1... | collective-permute-start | bytes 6291464 | tf_op jit(solution)/shard_map/ppermute | solution.py:55
  299.2 25.6 %collective-permute-start.25 = (bf16[256,2048]{1,0:T(8,128)(2,1)}, bf16[256,2048]{1,0:T(8,128)(2,1)S(1)}, u32[]{:S(2)}, u32[]{:S(2)}) collective-permute-start(bf16[256,2048]{1,0:T(8,128)(2,1)} %convolution_convert_fusion.6), channel_id=1, source_target_pairs={{0,16},{16,0},{1,17},{17,1},{2,18},{18,2},{3,19},{19,3},{4,20},{20... | collective-permute-start | bytes 3145736 | tf_op jit(solution)/shard_map/ppermute | solution.py:59
  299.5 25.4 %collective-permute-start.24 = (bf16[256,2048]{1,0:T(8,128)(2,1)}, bf16[256,2048]{1,0:T(8,128)(2,1)S(1)}, u32[]{:S(2)}, u32[]{:S(2)}) collective-permute-start(bf16[256,2048]{1,0:T(8,128)(2,1)} %convolution_convert_fusion.7), channel_id=1, source_target_pairs={{0,8},{8,0},{1,9},{9,1},{2,10},{10,2},{3,11},{11,3},{4,12},{12,4},... | collective-permute-start | bytes 3145736 | tf_op jit(solution)/shard_map/ppermute | solution.py:63
  339.2 26.3 %collective-permute-start.29 = (bf16[512,1024]{1,0:T(8,128)(2,1)}, bf16[512,1024]{1,0:T(8,128)(2,1)}, u32[]{:S(2)}, u32[]{:S(2)}) collective-permute-start(bf16[512,1024]{1,0:T(8,128)(2,1)} %convolution_convert_fusion.8), channel_id=1, source_target_pairs={{0,16},{16,0},{1,17},{17,1},{2,18},{18,2},{3,19},{19,3},{4,20},{20... | collective-permute-start | bytes 3145736 | tf_op jit(solution)/shard_map/ppermute | solution.py:59
  341.0 26.5 %collective-permute-start.28 = (bf16[512,1024]{1,0:T(8,128)(2,1)}, bf16[512,1024]{1,0:T(8,128)(2,1)}, u32[]{:S(2)}, u32[]{:S(2)}) collective-permute-start(bf16[512,1024]{1,0:T(8,128)(2,1)} %convolution_convert_fusion.9), channel_id=1, source_target_pairs={{0,8},{8,0},{1,9},{9,1},{2,10},{10,2},{3,11},{11,3},{4,12},{12,4},... | collective-permute-start | bytes 3145736 | tf_op jit(solution)/shard_map/ppermute | solution.py:63
  342.3 35.8 %collective-permute-start.32 = (bf16[128,2048]{1,0:T(8,128)(2,1)}, bf16[128,2048]{1,0:T(8,128)(2,1)}, u32[]{:S(2)}, u32[]{:S(2)}) collective-permute-start(bf16[128,2048]{1,0:T(8,128)(2,1)} %fusion.10), channel_id=1, source_target_pairs={{0,8},{8,0},{1,9},{9,1},{2,10},{10,2},{3,11},{11,3},{4,12},{12,4},... | collective-permute-start | bytes 1572872 | tf_op jit(solution)/shard_map/ppermute | solution.py:63
  343.2 34.8 %collective-permute-start.31 = (bf16[128,2048]{1,0:T(8,128)(2,1)}, bf16[128,2048]{1,0:T(8,128)(2,1)}, u32[]{:S(2)}, u32[]{:S(2)}) collective-permute-start(bf16[128,2048]{1,0:T(8,128)(2,1)} %fusion.9), channel_id=1, source_target_pairs={{0,16},{16,0},{1,17},{17,1},{2,18},{18,2},{3,19},{19,3},{4,20},{20... | collective-permute-start | bytes 1572872 | tf_op jit(solution)/shard_map/ppermute | solution.py:59
  352.8 40.0 %all-to-all-start.2 = ((bf16[4,2,128,128]{3,2,1,0:T(8,128)(2,1)}), bf16[4,2,128,128]{3,2,1,0:T(8,128)(2,1)}, u32[]{:S(2)}, u32[]{:S(2)}) async-start(bf16[4,2,128,128]{3,2,1,0:T(8,128)(2,1)} %bitcast.199), calls=%async_computation.4 | async-start | bytes 524288 | tf_op jit(solution)/shard_map/all_to_all | solution.py:339
  384.3 15.2 %collective-permute-start.38 = (bf16[256,1024]{1,0:T(8,128)(2,1)}, bf16[256,1024]{1,0:T(8,128)(2,1)}, u32[]{:S(2)}, u32[]{:S(2)}) collective-permute-start(bf16[256,1024]{1,0:T(8,128)(2,1)} %add_convert_fusion.8), channel_id=1, source_target_pairs={{0,8},{8,0},{1,9},{9,1},{2,10},{10,2},{3,11},{11,3},{4,12},{12,4},... | collective-permute-start | bytes 1572872 | tf_op jit(solution)/shard_map/ppermute | solution.py:63
  385.4 17.4 %collective-permute-start.37 = (bf16[256,1024]{1,0:T(8,128)(2,1)}, bf16[256,1024]{1,0:T(8,128)(2,1)}, u32[]{:S(2)}, u32[]{:S(2)}) collective-permute-start(bf16[256,1024]{1,0:T(8,128)(2,1)} %add_convert_fusion.9), channel_id=1, source_target_pairs={{0,16},{16,0},{1,17},{17,1},{2,18},{18,2},{3,19},{19,3},{4,20},{20... | collective-permute-start | bytes 1572872 | tf_op jit(solution)/shard_map/ppermute | solution.py:59
  388.7 34.3 %collective-permute-start.36 = (bf16[256,2048]{1,0:T(8,128)(2,1)}, bf16[256,2048]{1,0:T(8,128)(2,1)}, u32[]{:S(2)}, u32[]{:S(2)}) collective-permute-start(bf16[256,2048]{1,0:T(8,128)(2,1)} %convolution_convert_fusion.4), channel_id=1, source_target_pairs={{0,16},{16,0},{1,17},{17,1},{2,18},{18,2},{3,19},{19,3},{4,20},{20... | collective-permute-start | bytes 3145736 | tf_op jit(solution)/shard_map/ppermute | solution.py:59
  391.7 31.3 %collective-permute-start.35 = (bf16[256,2048]{1,0:T(8,128)(2,1)}, bf16[256,2048]{1,0:T(8,128)(2,1)}, u32[]{:S(2)}, u32[]{:S(2)}) collective-permute-start(bf16[256,2048]{1,0:T(8,128)(2,1)} %convolution_convert_fusion.5), channel_id=1, source_target_pairs={{0,8},{8,0},{1,9},{9,1},{2,10},{10,2},{3,11},{11,3},{4,12},{12,4},... | collective-permute-start | bytes 3145736 | tf_op jit(solution)/shard_map/ppermute | solution.py:63
  395.5 52.9 %collective-permute-start.34 = (bf16[512,1152]{1,0:T(8,128)(2,1)}, bf16[512,1152]{1,0:T(8,128)(2,1)}, u32[]{:S(2)}, u32[]{:S(2)}) collective-permute-start(bf16[512,1152]{1,0:T(8,128)(2,1)} %convolution_convert_fusion.2), channel_id=1, source_target_pairs={{0,16},{16,0},{1,17},{17,1},{2,18},{18,2},{3,19},{19,3},{4,20},{20... | collective-permute-start | bytes 3538952 | tf_op jit(solution)/shard_map/ppermute | solution.py:59
  399.5 48.8 %collective-permute-start.33 = (bf16[512,1152]{1,0:T(8,128)(2,1)}, bf16[512,1152]{1,0:T(8,128)(2,1)}, u32[]{:S(2)}, u32[]{:S(2)}) collective-permute-start(bf16[512,1152]{1,0:T(8,128)(2,1)} %convolution_convert_fusion.3), channel_id=1, source_target_pairs={{0,8},{8,0},{1,9},{9,1},{2,10},{10,2},{3,11},{11,3},{4,12},{12,4},... | collective-permute-start | bytes 3538952 | tf_op jit(solution)/shard_map/ppermute | solution.py:63
  407.2 63.1 %all-to-all-start.3 = ((bf16[8,64,1024]{2,1,0:T(8,128)(2,1)}), bf16[8,64,1024]{2,1,0:T(8,128)(2,1)}, u32[]{:S(2)}, u32[]{:S(2)}) async-start(bf16[8,64,1024]{2,1,0:T(8,128)(2,1)} %bitcast.239), calls=%async_computation.5 | async-start | bytes 2097152 | tf_op jit(solution)/shard_map/all_to_all | solution.py:356
  411.5 102.3 %reduce-scatter.8.cloned.1.call-start = ((), (), s32[]{:S(2)}) async-start(), calls=%async_computation.11 | async-start | bytes 1474560 | tf_op jit(solution)/shard_map/reduce_scatter | solution.py:71
  425.5 32.8 %collective-permute-start.44 = (bf16[128,2048]{1,0:T(8,128)(2,1)S(1)}, bf16[128,2048]{1,0:T(8,128)(2,1)S(1)}, u32[]{:S(2)}, u32[]{:S(2)}) collective-permute-start(bf16[128,2048]{1,0:T(8,128)(2,1)S(1)} %add_convert_fusion.6), channel_id=1, source_target_pairs={{0,8},{8,0},{1,9},{9,1},{2,10},{10,2},{3,11},{11,3},{4,12},{12,4},... | collective-permute-start | bytes 1572872 | tf_op jit(solution)/shard_map/ppermute | solution.py:63
  429.0 30.4 %collective-permute-start.43 = (bf16[128,2048]{1,0:T(8,128)(2,1)S(1)}, bf16[128,2048]{1,0:T(8,128)(2,1)S(1)}, u32[]{:S(2)}, u32[]{:S(2)}) collective-permute-start(bf16[128,2048]{1,0:T(8,128)(2,1)S(1)} %add_convert_fusion.7), channel_id=1, source_target_pairs={{0,16},{16,0},{1,17},{17,1},{2,18},{18,2},{3,19},{19,3},{4,20},{20... | collective-permute-start | bytes 1572872 | tf_op jit(solution)/shard_map/ppermute | solution.py:59
  451.8 17.6 %collective-permute-start.40 = (bf16[256,1152]{1,0:T(8,128)(2,1)S(1)}, bf16[256,1152]{1,0:T(8,128)(2,1)S(1)}, u32[]{:S(2)}, u32[]{:S(2)}) collective-permute-start(bf16[256,1152]{1,0:T(8,128)(2,1)S(1)} %add_convert_fusion.3), channel_id=1, source_target_pairs={{0,8},{8,0},{1,9},{9,1},{2,10},{10,2},{3,11},{11,3},{4,12},{12,4},... | collective-permute-start | bytes 1769480 | tf_op jit(solution)/shard_map/ppermute | solution.py:63
  456.2 14.1 %collective-permute-start.39 = (bf16[256,1152]{1,0:T(8,128)(2,1)S(1)}, bf16[256,1152]{1,0:T(8,128)(2,1)}, u32[]{:S(2)}, u32[]{:S(2)}) collective-permute-start(bf16[256,1152]{1,0:T(8,128)(2,1)S(1)} %add_convert_fusion.4), channel_id=1, source_target_pairs={{0,16},{16,0},{1,17},{17,1},{2,18},{18,2},{3,19},{19,3},{4,20},{20... | collective-permute-start | bytes 1769480 | tf_op jit(solution)/shard_map/ppermute | solution.py:59
  464.4 24.3 %collective-permute-start.41 = (f32[128,2048]{1,0:T(8,128)}, f32[128,2048]{1,0:T(8,128)}, u32[]{:S(2)}, u32[]{:S(2)}) collective-permute-start(f32[128,2048]{1,0:T(8,128)} %fusion.84), channel_id=1, source_target_pairs={{0,4},{4,0},{1,5},{5,1},{2,6},{6,2},{3,7},{7,3},{8,12},{12,8},{9,1... | collective-permute-start | bytes 3145736 | tf_op jit(solution)/shard_map/ppermute | solution.py:55
  505.9 29.1 %all-to-all-start.5 = ((bf16[4,64,2048]{2,1,0:T(8,128)(2,1)}), bf16[4,64,2048]{2,1,0:T(8,128)(2,1)S(1)}, u32[]{:S(2)}, u32[]{:S(2)}) async-start(bf16[4,64,2048]{2,1,0:T(8,128)(2,1)} %bitcast.238), calls=%async_computation.8 | async-start | bytes 2097152 | tf_op jit(solution)/shard_map/all_to_all | solution.py:369
  514.9 21.1 %collective-permute-start.42 = (bf16[64,1152]{1,0:T(8,128)(2,1)S(1)}, bf16[64,1152]{1,0:T(8,128)(2,1)S(1)}, u32[]{:S(2)}, u32[]{:S(2)}) collective-permute-start(bf16[64,1152]{1,0:T(8,128)(2,1)S(1)} %select_bitcast_fusion), channel_id=1, source_target_pairs={{0,4},{4,0},{1,5},{5,1},{2,6},{6,2},{3,7},{7,3},{8,12},{12,8},{9,1... | collective-permute-start | bytes 442376 | tf_op jit(solution)/shard_map/ppermute | solution.py:55
  (107 other events, 1079.2 us)
Sparse Core Ops, SparseCore 0:
  19.6 30.6 all-gather.8
  68.3 41.3 all-gather.10
  111.3 49.4 all-gather.12
  201.9 43.9 all-gather.14
  283.8 41.8 reduce-scatter.5
  349.9 47.0 reduce-scatter.3
  474.0 26.7 reduce-scatter.7

commit v3 on v2

--- a/solution.py
+++ b/solution.py
@@ -1,6 +1,8 @@
 import jax
 import jax.numpy as jnp
 from jax import lax
+from jax.experimental import pallas as pl
+from jax.experimental.pallas import tpu as pltpu
 from jax.sharding import Mesh, PartitionSpec as P
 
 HEADS = 16
@@ -30,6 +32,63 @@
 
 def mm_tn(a, b):
     return dot(a, b, ((0,), (0,)))
+
+
+def side(a, b, ca, cb, out=F32):
+    count, cols, depth = a.shape[1 - ca], b.shape[1 - cb], a.shape[ca]
+    tile = next((t for t in (512, 384, 256, 128) if cols % t == 0), cols)
+
+    def kernel(a_ref, b_ref, o_ref):
+        o_ref[...] = lax.dot_general(
+            a_ref[...], b_ref[...], (((ca,), (cb,)), ((), ())), preferred_element_type=F32
+        ).astype(out)
+
+    return pl.pallas_call(
+        kernel,
+        out_shape=jax.ShapeDtypeStruct((count, cols), out),
+        grid=(cols // tile,),
+        in_specs=[
+            pl.BlockSpec(a.shape, lambda j: (0, 0)),
+            pl.BlockSpec((depth, tile), lambda j: (0, j)) if cb == 0 else pl.BlockSpec((tile, depth), lambda j: (j, 0)),
+        ],
+        out_specs=pl.BlockSpec((count, tile), lambda j: (0, j)),
+        compiler_params=pltpu.CompilerParams(vmem_limit_bytes=24 << 20),
+        cost_estimate=pl.CostEstimate(flops=0, bytes_accessed=0, transcendentals=0),
+        name="side",
+    )(a, b)
+
+
+def hidden(h, w_up, bias, dact):
+    count, depth = h.shape
+    units = w_up.shape[1]
+    tile = next((t for t in (256, 128) if units % t == 0), units)
+
+    def kernel(h_ref, w_ref, b_ref, d_ref, act_ref, dpre_ref):
+        pre = jnp.dot(h_ref[...], w_ref[...], preferred_element_type=F32) + b_ref[...]
+        square = pre * pre
+        th = jnp.tanh(GELU_K * pre * (1.0 + GELU_C * square))
+        half = 0.5 * (1.0 + th)
+        act_ref[...] = (pre * half).astype(BF)
+        slope = half + 0.5 * GELU_K * pre * (1.0 - th * th) * (1.0 + 3.0 * GELU_C * square)
+        dpre_ref[...] = (d_ref[...] * slope).astype(BF)
+
+    return pl.pallas_call(
+        kernel,
+        out_shape=[jax.ShapeDtypeStruct((count, units), BF)] * 2,
+        grid=(units // tile,),
+        in_specs=[
+            pl.BlockSpec((count, depth), lambda j: (0, 0)),
+            pl.BlockSpec((depth, tile), lambda j: (0, j)),
+            pl.BlockSpec((1, tile), lambda j: (0, j)),
+            pl.BlockSpec((count, tile), lambda j: (0, j)),
+        ],
+        out_specs=[pl.BlockSpec((count, tile), lambda j: (0, j))] * 2,
+        compiler_params=pltpu.CompilerParams(vmem_limit_bytes=24 << 20),
+        cost_estimate=pl.CostEstimate(
+            flops=2 * count * depth * units, bytes_accessed=2 * (count + units) * depth, transcendentals=count * units
+        ),
+        name="hidden",
+    )(h, w_up, bias.reshape(1, units), dact)
 
 
 def ln_stats(x):
@@ -91,16 +150,17 @@
             return
         self.pieces = [x, over_b(x), over_a(x)]
 
-    def pass_on(self, order):
+    def pass_on(self, *joint):
         if self.square:
             x, x1, x2 = self.pieces
-            x1, x2 = order(x1, x2)
+            (x1, x2), joint = lax.optimization_barrier(((x1, x2), joint))
             half = x.shape[0] // 2
             self.pieces = [x, x1, x2, over_a(x1[:half]), over_b(x2[half:])]
+        return joint
 
 
 class ChipSum:
-    def __init__(self, term, square, count):
+    def __init__(self, term, square, count, gate=()):
         self.square, self.term = square, term
         self.far = []
         if not square:
@@ -111,6 +171,8 @@
         u = term((3, 0), (1, 0)).astype(BF)
         w = term((3, 1), (2, 1)).astype(BF)
         self.sent = [u, w]
+        if gate:
+            u, w = after((u, w), *gate)
         self.near = [over_b(u), over_a(w)]
 
     def pass_on(self, order):
@@ -146,11 +208,15 @@
         cols = [x[:, i * w : (i + 1) * w] for i in range(AB)]
         return jnp.concatenate([lax.select_n(me ^ i, *cols) for i in range(AB)], axis=1)
 
-    def product(left, right):
+    def product(left, right, multiply=None):
         half = left.shape[1] // AB // 2
-        return lambda *parts: mm_tn(
-            jnp.concatenate([left[:, (2 * i + j) * half : (2 * i + j + 1) * half] for i, j in parts], axis=1), right
-        )
+
+        def term(*parts):
+            cols = [left[:, (2 * i + j) * half : (2 * i + j + 1) * half] for i, j in parts]
+            cols = jnp.concatenate(cols, axis=1)
+            return mm_tn(cols, right) if multiply is None else multiply(cols, right, 0, 0)
+
+        return term
 
     def local(
         activations, segment_ids,
@@ -211,10 +277,6 @@
         q_at = start + jnp.arange(T, dtype=jnp.int32)
         k_at = jnp.arange(S, dtype=jnp.int32)
         allowed = (k_at[None, None, :] <= q_at[None, :, None]) & (seg[:, None, :] == seg_q[:, :, None])
-        order.mark(b_ext)
-        down_gather.pass_on(order)
-        order.mark(h1, down_gather.pieces[1:3])
-
         out_in = after(out_weight, w_ext_z)
         up_in = after(up_weight, w_ext_z)
         w_ext_z = order(w_ext_z)
@@ -229,11 +291,13 @@
             for j in range(C * Z)
         ]
         w_up = lax.all_to_all(jnp.stack(up_cols), ("core", "ctx"), 0, 0, tiled=True)
-        ext_gather.pass_on(order)
+        w_out_z, down_gather.pieces = ext_gather.pass_on(w_out_z, down_gather.pieces)
+        down_gather.pass_on()
+        ext_gather.pieces, w_up = lax.optimization_barrier((ext_gather.pieces, w_up))
 
         w_ext = jnp.concatenate(ext_gather.pieces)
         order.mark(w_ext)
-        w_out_z, h1, w_up = order(w_out_z, h1, w_up)
+        h1 = order(h1)
         if aligned:
             out_gather = ChipGather(w_out_z, square)
         cot_z = gather(after(cotangent[0], w_out_z), "ctx").reshape(Z * T, D)
@@ -247,21 +311,23 @@
         k = jnp.where(c == 0, kv, kv_mate)
         v = jnp.where(c == 0, kv_mate, kv)
         order.mark(kv)
-        q, k, cot_z = order(q, k, cot_z)
+        if aligned:
+            out_gather.pass_on()
+        q, k = order(q, k)
         s = jnp.einsum("rthd,rjd->rhtj", q, k, preferred_element_type=F32) * HD**-0.5
         s = jnp.where(allowed[:, None], s, -1e30)
         p = jnp.exp(s - jnp.max(s, axis=-1, keepdims=True))
         p = p / jnp.sum(p, axis=-1, keepdims=True)
+        if aligned:
+            p, pieces, cot_z, down_gather.pieces = lax.optimization_barrier(
+                (p, out_gather.pieces, cot_z, down_gather.pieces)
+            )
+            w_out = jnp.concatenate(pieces)
         pb = p.astype(BF)
         o = jnp.einsum("rhtj,rjd->rthd", pb, v, preferred_element_type=F32)
         o = o.astype(BF).reshape(2 * T, DH)
-        if aligned:
-            order.mark(o)
-            out_gather.pass_on(order)
-            w_out = jnp.concatenate(out_gather.pieces)
         order.mark(w_out, cot_z)
-        o_w, w_up_z = order(o, w_up.reshape(C * Z * R, F))
-        up_gather = ChipGather(w_up_z, square)
+        o_w = order(o)
         away = swap_core(mm(o_w[T:], w_out))
         mid = x + bo + mm(o_w[:T], w_out) + away
 
@@ -270,7 +336,7 @@
         h2_z = gather(h2, "ctx").reshape(Z * T, D)
 
         order.mark(h2)
-        up_gather.pass_on(order)
+        up_gather = ChipGather(order(w_up.reshape(C * Z * R, F)), square)
         half = Z * T
         cot_z, down_pieces = order(cot_z, down_gather.pieces)
         cots = [cot_z, swap_core(cot_z)]
@@ -282,21 +348,21 @@
                 w_down = lax.dynamic_update_slice_in_dim(w_down, part, at, 0)
         else:
             w_down = jnp.concatenate(down_pieces)
-        dacts = [mm_nt(part, w_down) for part in cots]
-        w_up = jnp.concatenate(up_gather.pieces)
+        order.mark(w_down)
+        up_gather.pass_on()
+        dacts = [side(part, w_down, 1, 1) for part in cots]
+        w_up = jnp.concatenate(after(up_gather.pieces, dacts))
         order.mark(dacts, w_up)
         h2_z = order(h2_z)
         h2s = [h2_z, swap_core(h2_z)]
         acts, dpres = [], []
         for part, dact in zip(h2s, dacts):
-            pre = mm(part, w_up) + bu
-            th = jnp.tanh(GELU_K * (pre + GELU_C * pre * pre * pre))
-            slope = 1.0 - th * th
-            dgelu = 0.5 * (1.0 + th) + 0.5 * pre * slope * GELU_K * (1.0 + 3.0 * GELU_C * pre * pre)
-            acts.append((0.5 * pre * (1.0 + th)).astype(BF))
-            dpres.append((dact * dgelu).astype(BF))
-        away = swap_core(mm_nt(dpres[1], w_up).astype(BF))
-        dh2_part = (mm_nt(after(dpres[0], away), w_up) + away.astype(F32)).astype(BF).reshape(Z, T, D)
+            act, dpre = hidden(part, w_up, bu, dact)
+            acts.append(act)
+            dpres.append(dpre)
+        away = swap_core(side(dpres[1], w_up, 1, 1, BF))
+        dh2_part, away = lax.optimization_barrier((side(dpres[0], w_up, 1, 1), away))
+        dh2_part = (dh2_part + away.astype(F32)).astype(BF).reshape(Z, T, D)
         order.mark(dh2_part)
         dh2 = turn(scatter(dh2_part, "ctx").astype(F32), me)
         dpre_w, act_w, h2_all, cot_all = (jnp.concatenate(order(*pair)) for pair in (dpres, acts, h2s, cots))
@@ -316,10 +382,6 @@
         order.mark(up_sum.sent, out_away)
         down_sum.pass_on(order)
         order.mark(down_sum.sent)
-        mlp = (mm(order(acts[0]), w_down) + out_away.astype(F32)).astype(BF).reshape(Z, T, D)
-        order.mark(mlp)
-        mlp = scatter(mlp, "ctx")
-
         dh2 = order(dh2)
         order.mark(dh2)
         dmid = cotangent[0].astype(F32) + ln_back(dh2, g2, xhat2, rstd2)
@@ -330,66 +392,61 @@
         do_h = order(do).reshape(2, T, HH, HD)
         dp = jnp.einsum("rthd,rjd->rhtj", do_h, v, preferred_element_type=F32)
         ds = (p * (dp - jnp.sum(p * dp, axis=-1, keepdims=True))).astype(BF)
+        order.mark(ds, down_sum.far)
+        ds = order(ds)
         dk = jnp.einsum("rhtj,rthd->rjd", ds, q, preferred_element_type=F32) * HD**-0.5
         dv = jnp.einsum("rhtj,rthd->rjd", pb, do_h, preferred_element_type=F32)
         dkv_away = swap_core(jnp.where(c == 0, dv, dk).astype(BF))
         dkv = jnp.where(c == 0, dk, dv) + dkv_away[::-1].astype(F32)
         dkv = dkv.astype(BF).reshape(2, Z, T, HD).transpose(1, 0, 2, 3)
-        order.mark(dkv, down_sum.far)
+        order.mark(dkv)
         dkv = lax.all_to_all(dkv, "ctx", 0, 0, tiled=True)
-        up_sum.pass_on(order)
-        order.mark(up_sum.sent)
-        ds_w, db_w = order(ds, db)
+        mlp, out_away = lax.optimization_barrier((side(order(acts[0]), w_down, 1, 0), out_away))
+        mlp = (mlp + out_away.astype(F32)).astype(BF).reshape(Z, T, D)
+        order.mark(mlp)
+        mlp = scatter(mlp, "ctx")
+        ds_w = order(ds)
         dq = jnp.einsum("rhtj,rjd->rthd", ds_w, k, preferred_element_type=F32) * HD**-0.5
         dq = dq.astype(BF).reshape(2 * T, DH)
         if aligned:
             dq = turn(dq, me)
-            out_sum = ChipSum(product(o, db_w), square, AB)
-            order.mark(out_sum.sent, dq)
+        order.mark(dq)
         dkv = order(dkv)
         dkv = jnp.sum(dkv.astype(F32), axis=0).astype(BF).reshape(2 * T, HD)
         dq_ext = jnp.concatenate([dq, dkv], axis=1)
         ext_sum = ChipSum(product(h1, dq_ext), square, AB)
         order.mark(ext_sum.sent)
+
+        dq_w = order(dq_ext)
+        dh1_away = swap_core(side(dq_w[T:], w_ext, 1, 1))
+        dh1 = turn(side(dq_w[:T], w_ext, 1, 1) + dh1_away, me)
+        up_sum.pass_on(order)
+        order.mark(up_sum.sent, dh1)
+        ext_sum.pass_on(order)
+        order.mark(ext_sum.sent)
+        if aligned:
+            out_sum = ChipSum(product(o, order(db), side), square, AB, ext_sum.far)
+            order.mark(out_sum.sent)
+        g_ext = ext_sum.finish(order).astype(BF).reshape(2, Z, R, E)
+        g_ext = g_ext.transpose(1, 0, 2, 3).reshape(Z, 2 * R, E)
+        g_ext, mlp = lax.optimization_barrier((g_ext, mlp))
+        order.mark(g_ext)
+        g_ext = scatter(g_ext, "ctx").reshape(2, R, E)
         g_up = up_sum.finish(order).astype(BF).reshape(C * Z, R, F)
         order.mark(g_up)
         g_up = lax.all_to_all(g_up, ("core", "ctx"), 0, 0, tiled=True)
         if aligned:
             out_sum.pass_on(order)
             order.mark(out_sum.sent)
-        ext_sum.pass_on(order)
-        order.mark(ext_sum.sent)
-        dq_w = order(dq_ext)
-        dh1_away = swap_core(mm_nt(dq_w[T:], w_ext))
-        dh1 = turn(mm_nt(dq_w[:T], w_ext) + dh1_away, me)
-
-        if aligned:
             g_out = out_sum.finish(order).astype(BF).reshape(Z, R, D)
             order.mark(g_out)
-            g_out = lax.all_to_all(g_out, "ctx", 0, 0, tiled=True)
-            g_out = jnp.sum(g_out.astype(F32), axis=0)
+            g_out = scatter(g_out, "ctx").astype(F32)
         else:
             g_out = mm_tn(o, order(db)).astype(BF)
             full = jnp.where(lax.broadcasted_iota(jnp.int32, (2, 1, 1), 0) == c, g_out[None], 0)
             g_out = scatter(full.reshape(N, R, D), EVERY).astype(F32)
-        order.mark(ext_sum.far, g_up)
-        g_ext = ext_sum.finish(order).astype(BF).reshape(2, Z, R, E)
-        g_ext = g_ext.transpose(1, 0, 2, 3).reshape(Z, 2 * R, E)
-        order.mark(g_ext)
-        g_ext = scatter(g_ext, "ctx").reshape(2, R, E)
-        g_down = down_sum.finish(order)
-        dx = dmid + ln_back(order(dh1), g1, xhat1, rstd1)
-        first, second = g_ext[0], g_ext[1]
-        mate = swap_core(jnp.where(c == 0, second, first))
-        mine = jnp.where(c == 0, first, second)
-        first, second = jnp.where(c == 0, mine, mate), jnp.where(c == 0, mate, mine)
-        g_q = [h[:, g * W0 : (g + 1) * W0] for g in range(G) for h in (first, second)]
-        g_q = jnp.concatenate(g_q, axis=1).astype(F32)
-        g_kv = jnp.concatenate([first[:, DH:], second[:, DH:]], axis=1).astype(F32)
-        g_up = order(g_up)
-        g_up = g_up.reshape(C * Z, R, AB, F0).transpose(1, 2, 0, 3).reshape(R, FF).astype(F32)
-        result = mid + order(mlp).astype(F32) + bd
-
+        g_ext, g_up = order(g_ext, g_up)
+        order.mark(g_ext, g_up)
         own_core = (lax.broadcasted_iota(jnp.int32, (1, 2, 1), 1) == c).astype(F32)
         own_cz = (lax.broadcasted_iota(jnp.int32, (1, C * Z, 1), 1) == c * Z + z).astype(F32)
         dh2_late, dpre_late, cot_late, dq_late, db_late = order(dh2, dpre_w, cotangent[0], dq_ext, db[:T])
@@ -413,6 +470,18 @@
             axis=1,
         )
         packed = jnp.sum(lax.all_to_all(packed, EVERY, 0, 0, tiled=True), axis=0)
+        g_down = down_sum.finish(order)
+        dx = dmid + ln_back(order(dh1), g1, xhat1, rstd1)
+        first, second = g_ext[0], g_ext[1]
+        mate = swap_core(jnp.where(c == 0, second, first))
+        mine = jnp.where(c == 0, first, second)
+        first, second = jnp.where(c == 0, mine, mate), jnp.where(c == 0, mate, mine)
+        g_q = [h[:, g * W0 : (g + 1) * W0] for g in range(G) for h in (first, second)]
+        g_q = jnp.concatenate(g_q, axis=1).astype(F32)
+        g_kv = jnp.concatenate([first[:, DH:], second[:, DH:]], axis=1).astype(F32)
+        g_up = g_up.reshape(C * Z, R, AB, F0).transpose(1, 2, 0, 3).reshape(R, FF).astype(F32)
+        result = order(mid) + mlp.astype(F32) + bd
+
         vecs = [packed[i * R : (i + 1) * R] for i in range(7)]
         gb_up = packed[7 * R : 7 * R + F0]
         gb_v = packed[7 * R + F0 :]

time: 552 us -> 538 us (0.975)
  waiting for transfers between devices: 227 us -> 150 us
  matrix products: 106 us -> 52.9 us
  Pallas kernels: 0 us -> 39.1 us
  other arithmetic: 36.2 us -> 68.3 us
  local copies, waits for them, and re-layouts: 81.9 us -> 111 us
  starting transfers between devices: 60.4 us -> 69.7 us
    dot_general x34 -> x20, matrix products: 102 us -> 44.8 us  [dot(): return lax.dot_general(a, b, (dims, ((), ())), preferred_element_type=F32)]
    pallas_call x0 -> x14, Pallas kernels: none -> 39.1 us  [the longest x12 28.1 us: side(): pl.pallas_call(kernel, out_shape=jax.ShapeDtypeStruct((count, cols), out)...]
    all_gather x4, waiting for transfers between devices: 33 us -> 10.2 us  [gather(): return lax.all_gather(x, axes, axis=0, tiled=False)]
    ppermute x16, waiting for transfers between devices: 67.5 us -> 45.3 us  [over_a(): return lax.ppermute(x, 'a', MATES)]
    all_to_all x1 -> x0, waiting for transfers between devices: 20 us -> none  [local(): g_out = lax.all_to_all(g_out, 'ctx', 0, 0, tiled=True)]
    convert_element_type x1 -> x8, other arithmetic: 0.78 us -> 18.1 us  [the longest x1 3.74 us: local(): mlp = (mlp + out_away.astype(F32)).astype(BF).reshape(Z, T, D)]
    unnamed x226 -> x240, local copies, waits for them, and re-layouts: 39.8 us -> 48.3 us
    div x0 -> x1, other arithmetic: none -> 7.93 us  [local(): p = p / jnp.sum(p, axis=-1, keepdims=True)]
  transfers between devices with their start and end apart: 58 -> 58, of which waited for: 30 -> 27; matrix products, arithmetic and copies ran while one was open for 31% -> 32% of each run, Pallas kernels for 0% -> 5%
where the time goes in v3:
time: 538 us; the launch traced here: 529 us
  waiting for transfers between devices  150 us (28%)
  local copies, waits for them, and re-layouts  111 us (21%)
  starting transfers between devices  69.7 us (13%)
  other arithmetic  68.3 us (13%)
  matrix products  52.9 us (10%)
  Pallas kernels  39.1 us (7%)
  blocking collectives  21.2 us (4%)
  between operations  16.5 us (3%)
    ppermute x16, waiting for transfers between devices, over_b(): return lax.ppermute(x, 'b', MATES)  65.8 us
    unnamed x240, local copies, waits for them, and re-layouts  48.3 us
    ppermute x16, waiting for transfers between devices, over_a(): return lax.ppermute(x, 'a', MATES)  45.3 us
    dot_general x20, matrix products, dot(): return lax.dot_general(a, b, (dims, ((), ())), preferred_element_type=F32)  44.8 us
    pallas_call x12, Pallas kernels, side(): pl.pallas_call(kernel, out_shape=jax.ShapeDtypeStruct((count, cols), out)...  28.1 us
    ppermute x16, starting transfers between devices, over_b(): return lax.ppermute(x, 'b', MATES)  27.5 us
    all_gather x1, blocking collectives, gather(): return lax.all_gather(x, axes, axis=0, tiled=False)  21.2 us
    ppermute x16, starting transfers between devices, over_a(): return lax.ppermute(x, 'a', MATES)  18.8 us
  transfers between devices with their start and end apart: 58, of which 27 were waited for; matrix products, arithmetic and copies ran while one was open for 32% of the time, Pallas kernels for 5%

profile of v3, /device:TPU:0, one launch (start us, length us, event | category | flops | bytes accessed | tf_op | source)
XLA Modules:
  0.0 528.8 jit_solution(5060630530768944136)
XLA Ops:
  16.5 2.9 collective-permute-start.4
  23.3 4.0 all-to-all-start
  27.8 17.3 %all-to-all-done = bf16[32,2,354]{2,1,0:T(2,128)(2,1)S(1)} async-done(((bf16[32,2,354]{2,1,0:T(2,128)(2,1)}), bf16[32,2,354]{2,1,0:T(2,128)(2,1)S(1)}, u32[]{:S(2)}, u32[]{:S(2)}) %all-to-all-start) | async-done | bytes 45344 | tf_op jit(solution)/shard_map/all_to_all | solution.py:263
  46.1 3.5 all-gather.9.cloned.1.call-done
  64.0 3.6 all-to-all-start.1
  70.2 8.5 %collective-permute-done.2 = bf16[512,1152]{1,0:T(8,128)(2,1)} collective-permute-done((bf16[512,1152]{1,0:T(8,128)(2,1)S(1)}, bf16[512,1152]{1,0:T(8,128)(2,1)}, u32[]{:S(2)}, u32[]{:S(2)}) %collective-permute-start.2) | collective-permute-done | bytes 1179680 | tf_op jit(solution)/shard_map/ppermute | solution.py:122
  79.9 6.7 %all-gather.11.cloned.1.call-done = bf16[256,2048]{1,0:T(8,128)(2,1)} async-done(((bf16[64,2048]{1,0:T(8,128)(2,1)}), bf16[256,2048]{1,0:T(8,128)(2,1)}) %all-gather.11.cloned.1.call-update) | async-done | bytes 1048592 | tf_op jit(solution)/shard_map/all_gather | solution.py:126
  88.5 3.0 collective-permute-start.6
  93.5 4.4 collective-permute-start.7
  106.2 4.3 collective-permute-start.15
  120.2 21.2 %all_gather.31 = bf16[4,2,128,128]{3,2,1,0:T(8,128)(2,1)S(1)} all-gather(bf16[1,2,128,128]{3,2,1,0:T(8,128)(2,1)S(1)} %bitcast.239), channel_id=1, replica_groups=mesh['a'=2,'b'=2,'core'=2,'ctx'=4] {'ctx'}, dimensions={0}, use_global_device_ids=true | all-gather | bytes 327680 | tf_op jit(solution)/shard_map/all_gather | solution.py:126
  149.1 2.8 fusion.70
  151.9 7.9 %fusion.8 = f32[2,8,128,512]{2,3,1,0:T(8,128)} fusion(f32[2,512,128,8]{2,1,3,0:T(8,128)} %fusion.70, pred[2,128,512]{1,2,0:T(8,128)(4,1)} %compare_and_fusion), kind=kOutput, calls=%fused_computation.24 | output fusion | flops 6296574 | bytes 8519680 | tf_op jit(solution)/shard_map/div | solution.py:320
  162.5 2.7 fusion.23
  165.6 2.6 constant_dynamic-update-slice_fusion.18
  174.3 3.9 fusion.85
  181.1 3.1 fusion.127
  193.8 18.9 %collective-permute-done.18 = bf16[512,1024]{1,0:T(8,128)(2,1)} collective-permute-done((bf16[512,1024]{1,0:T(8,128)(2,1)S(1)}, bf16[512,1024]{1,0:T(8,128)(2,1)}, u32[]{:S(2)}, u32[]{:S(2)}) %collective-permute-start.18) | collective-permute-done | bytes 1048608 | tf_op jit(solution)/shard_map/ppermute | solution.py:122
  222.0 2.7 side.12.d_ref
  226.0 4.3 side.13.d_ref
  235.9 4.4 collective-permute-done.22.h_ref
  244.1 6.2 %hidden.3 = (bf16[512,1024]{1,0:T(8,128)(2,1)S(1)}, bf16[512,1024]{1,0:T(8,128)(2,1)S(1)}) custom-call(bf16[512,2048]{1,0:T(8,128)(2,1)} %collective-permute-done.22.h_ref, bf16[2048,1024]{1,0:T(8,128)(2,1)S(1)} %copy-done.1, f32[1,1024]{1,0:T(1,128)S(1)} %bitcast.187, f32[512,1024]{1,0:T(8,128)S(1)} %copy-done.15), custom_call_target="tpu_custom_call" | custom-call | flops 2147483648 | bytes 6291456 | tf_op jit(solution)/shard_map/hidden/pallas_call | solution.py:75
  250.3 3.9 side.15
  259.6 4.8 hidden.2
  264.4 3.4 side.14
  267.9 3.7 add_convert_fusion.1
  280.3 3.7 convolution_convert_fusion
  295.8 14.0 %collective-permute-done.24 = bf16[256,2048]{1,0:T(8,128)(2,1)S(1)} collective-permute-done((bf16[256,2048]{1,0:T(8,128)(2,1)}, bf16[256,2048]{1,0:T(8,128)(2,1)S(1)}, u32[]{:S(2)}, u32[]{:S(2)}) %collective-permute-start.24) | collective-permute-done | bytes 1048608 | tf_op jit(solution)/shard_map/ppermute | solution.py:122
  311.4 2.7 fusion.10
  314.1 2.5 fusion.11
  328.0 7.5 %collective-permute-done.28 = bf16[128,2048]{1,0:T(8,128)(2,1)S(1)} collective-permute-done((bf16[128,2048]{1,0:T(8,128)(2,1)}, bf16[128,2048]{1,0:T(8,128)(2,1)S(1)}, u32[]{:S(2)}, u32[]{:S(2)}) %collective-permute-start.28) | collective-permute-done | bytes 524320 | tf_op jit(solution)/shard_map/ppermute | solution.py:118
  341.6 4.2 all-to-all-start.2
  348.0 3.4 side.16
  351.4 3.7 add_convert_fusion
  365.4 2.7 add_convert_fusion.10
  370.3 2.7 add_convert_fusion.9
  375.4 15.7 %collective-permute-done.31 = bf16[512,1152]{1,0:T(8,128)(2,1)S(1)} collective-permute-done((bf16[512,1152]{1,0:T(8,128)(2,1)S(1)}, bf16[512,1152]{1,0:T(8,128)(2,1)S(1)}, u32[]{:S(2)}, u32[]{:S(2)}) %collective-permute-start.31) | collective-permute-done | bytes 1179680 | tf_op jit(solution)/shard_map/ppermute | solution.py:122
  399.6 8.0 %collective-permute-done.36 = bf16[256,1152]{1,0:T(8,128)(2,1)S(1)} collective-permute-done((bf16[256,1152]{1,0:T(8,128)(2,1)S(1)}, bf16[256,1152]{1,0:T(8,128)(2,1)S(1)}, u32[]{:S(2)}, u32[]{:S(2)}) %collective-permute-start.36) | collective-permute-done | bytes 589856 | tf_op jit(solution)/shard_map/ppermute | solution.py:118
  419.8 23.7 %collective-permute-done.38 = bf16[256,1024]{1,0:T(8,128)(2,1)} collective-permute-done((bf16[256,1024]{1,0:T(8,128)(2,1)}, bf16[256,1024]{1,0:T(8,128)(2,1)}, u32[]{:S(2)}, u32[]{:S(2)}) %collective-permute-start.38) | collective-permute-done | bytes 524320 | tf_op jit(solution)/shard_map/ppermute | solution.py:118
  443.5 4.7 add_convert_fusion.3
  448.2 5.1 all-to-all-start.3
  469.9 3.4 collective-permute-done.43
  473.3 2.7 add_convert_fusion.2
  476.0 3.5 all-to-all-done.3
  497.7 3.2 all-to-all-start.4
  503.6 2.5 fusion.48
  506.1 4.2 convolution_add_fusion.2
  513.6 2.5 copy.96
  (532 shorter events, 231.2 us)
Async XLA Ops:
  7.3 42.3 %all-gather.9.cloned.1.call-start = ((), (), s32[]{:S(2)}) async-start(), calls=%async_computation.13 | async-start | bytes 1474560 | tf_op jit(solution)/shard_map/all_gather | solution.py:126
  16.5 53.7 %collective-permute-start.4 = (bf16[256,2048]{1,0:T(8,128)(2,1)}, bf16[256,2048]{1,0:T(8,128)(2,1)}, u32[]{:S(2)}, u32[]{:S(2)}) collective-permute-start(bf16[256,2048]{1,0:T(8,128)(2,1)} %param.31), channel_id=1, source_target_pairs={{0,8},{8,0},{1,9},{9,1},{2,10},{10,2},{3,11},{11,3},{4,12},{12,4},... | collective-permute-start | bytes 3145736 | tf_op jit(solution)/shard_map/ppermute | solution.py:122
  19.4 50.8 %collective-permute-start.5 = (bf16[256,2048]{1,0:T(8,128)(2,1)}, bf16[256,2048]{1,0:T(8,128)(2,1)}, u32[]{:S(2)}, u32[]{:S(2)}) collective-permute-start(bf16[256,2048]{1,0:T(8,128)(2,1)} %param.31), channel_id=1, source_target_pairs={{0,16},{16,0},{1,17},{17,1},{2,18},{18,2},{3,19},{19,3},{4,20},{20... | collective-permute-start | bytes 3145736 | tf_op jit(solution)/shard_map/ppermute | solution.py:118
  23.3 21.8 %all-to-all-start = ((bf16[32,2,354]{2,1,0:T(2,128)(2,1)}), bf16[32,2,354]{2,1,0:T(2,128)(2,1)S(1)}, u32[]{:S(2)}, u32[]{:S(2)}) async-start(bf16[32,2,354]{2,1,0:T(2,128)(2,1)} %reshape.306), calls=%async_computation | async-start | bytes 98304 | tf_op jit(solution)/shard_map/all_to_all | solution.py:263
  27.3 59.3 %all-gather.11.cloned.1.call-start = ((), (), s32[]{:S(2)}) async-start(), calls=%async_computation.14 | async-start | bytes 1310720 | tf_op jit(solution)/shard_map/all_gather | solution.py:126
  51.0 27.7 %collective-permute-start.2 = (bf16[512,1152]{1,0:T(8,128)(2,1)S(1)}, bf16[512,1152]{1,0:T(8,128)(2,1)}, u32[]{:S(2)}, u32[]{:S(2)}) collective-permute-start(bf16[512,1152]{1,0:T(8,128)(2,1)S(1)} %bitcast.205), channel_id=1, source_target_pairs={{0,8},{8,0},{1,9},{9,1},{2,10},{10,2},{3,11},{11,3},{4,12},{12,4},... | collective-permute-start | bytes 3538952 | tf_op jit(solution)/shard_map/ppermute | solution.py:122
  52.5 27.4 %collective-permute-start.3 = (bf16[512,1152]{1,0:T(8,128)(2,1)S(1)}, bf16[512,1152]{1,0:T(8,128)(2,1)}, u32[]{:S(2)}, u32[]{:S(2)}) collective-permute-start(bf16[512,1152]{1,0:T(8,128)(2,1)S(1)} %bitcast.206), channel_id=1, source_target_pairs={{0,16},{16,0},{1,17},{17,1},{2,18},{18,2},{3,19},{19,3},{4,20},{20... | collective-permute-start | bytes 3538952 | tf_op jit(solution)/shard_map/ppermute | solution.py:118
  64.0 46.5 %all-to-all-start.1 = ((bf16[8,64,1024]{2,1,0:T(8,128)(2,1)}), bf16[8,64,1024]{2,1,0:T(8,128)(2,1)S(1)}, u32[]{:S(2)}, u32[]{:S(2)}) async-start(bf16[8,64,1024]{2,1,0:T(8,128)(2,1)} %fusion.95), calls=%async_computation.1 | async-start | bytes 2097152 | tf_op jit(solution)/shard_map/all_to_all | solution.py:293
  67.5 93.9 %all-gather.13.cloned.1.call-start = ((), (), s32[]{:S(2)}) async-start(), calls=%async_computation.15 | async-start | bytes 2621440 | tf_op jit(solution)/shard_map/all_gather | solution.py:126
  69.0 29.2 %collective-permute-start.1 = (bf16[128,2048]{1,0:T(8,128)(2,1)}, bf16[128,2048]{1,0:T(8,128)(2,1)}, u32[]{:S(2)}, u32[]{:S(2)}) collective-permute-start(bf16[128,2048]{1,0:T(8,128)(2,1)} %pad_maximum_fusion.5), channel_id=1, source_target_pairs={{0,4},{4,0},{1,5},{5,1},{2,6},{6,2},{3,7},{7,3},{8,12},{12,8},{9,1... | collective-permute-start | bytes 1572872 | tf_op jit(solution)/shard_map/ppermute | solution.py:114
  88.5 17.7 %collective-permute-start.6 = (bf16[256,1152]{1,0:T(8,128)(2,1)}, bf16[256,1152]{1,0:T(8,128)(2,1)}, u32[]{:S(2)}, u32[]{:S(2)}) collective-permute-start(bf16[256,1152]{1,0:T(8,128)(2,1)} %slice.474), channel_id=1, source_target_pairs={{0,16},{16,0},{1,17},{17,1},{2,18},{18,2},{3,19},{19,3},{4,20},{20... | collective-permute-start | bytes 1769480 | tf_op jit(solution)/shard_map/ppermute | solution.py:118
  93.5 18.9 %collective-permute-start.7 = (bf16[256,1152]{1,0:T(8,128)(2,1)}, bf16[256,1152]{1,0:T(8,128)(2,1)}, u32[]{:S(2)}, u32[]{:S(2)}) collective-permute-start(bf16[256,1152]{1,0:T(8,128)(2,1)} %slice.475), channel_id=1, source_target_pairs={{0,8},{8,0},{1,9},{9,1},{2,10},{10,2},{3,11},{11,3},{4,12},{12,4},... | collective-permute-start | bytes 1769480 | tf_op jit(solution)/shard_map/ppermute | solution.py:122
  100.3 42.9 %collective-permute-start.10 = (bf16[256,2048]{1,0:T(8,128)(2,1)}, bf16[256,2048]{1,0:T(8,128)(2,1)}, u32[]{:S(2)}, u32[]{:S(2)}) collective-permute-start(bf16[256,2048]{1,0:T(8,128)(2,1)} %all-gather.11.cloned.1.call-done), channel_id=1, source_target_pairs={{0,8},{8,0},{1,9},{9,1},{2,10},{10,2},{3,11},{11,3},{4,12},{12,4},... | collective-permute-start | bytes 3145736 | tf_op jit(solution)/shard_map/ppermute | solution.py:122
  100.3 42.9 %collective-permute-start.11 = (bf16[256,2048]{1,0:T(8,128)(2,1)}, bf16[256,2048]{1,0:T(8,128)(2,1)}, u32[]{:S(2)}, u32[]{:S(2)}) collective-permute-start(bf16[256,2048]{1,0:T(8,128)(2,1)} %all-gather.11.cloned.1.call-done), channel_id=1, source_target_pairs={{0,16},{16,0},{1,17},{17,1},{2,18},{18,2},{3,19},{19,3},{4,20},{20... | collective-permute-start | bytes 3145736 | tf_op jit(solution)/shard_map/ppermute | solution.py:118
  100.3 135.5 %all-gather.15.cloned.1.call-start = ((), (), s32[]{:S(2)}) async-start(), calls=%async_computation.16 | async-start | bytes 2621440 | tf_op jit(solution)/shard_map/all_gather | solution.py:126
  102.3 57.5 %collective-permute-start.14 = (bf16[128,2048]{1,0:T(8,128)(2,1)}, bf16[128,2048]{1,0:T(8,128)(2,1)}, u32[]{:S(2)}, u32[]{:S(2)}) collective-permute-start(bf16[128,2048]{1,0:T(8,128)(2,1)} %slice.517), channel_id=1, source_target_pairs={{0,16},{16,0},{1,17},{17,1},{2,18},{18,2},{3,19},{19,3},{4,20},{20... | collective-permute-start | bytes 1572872 | tf_op jit(solution)/shard_map/ppermute | solution.py:118
  106.2 53.6 %collective-permute-start.15 = (bf16[128,2048]{1,0:T(8,128)(2,1)}, bf16[128,2048]{1,0:T(8,128)(2,1)}, u32[]{:S(2)}, u32[]{:S(2)}) collective-permute-start(bf16[128,2048]{1,0:T(8,128)(2,1)} %slice.518), channel_id=1, source_target_pairs={{0,8},{8,0},{1,9},{9,1},{2,10},{10,2},{3,11},{11,3},{4,12},{12,4},... | collective-permute-start | bytes 1572872 | tf_op jit(solution)/shard_map/ppermute | solution.py:122
  145.2 14.6 %collective-permute-start.12 = (bf16[128,2048]{1,0:T(8,128)(2,1)}, bf16[128,2048]{1,0:T(8,128)(2,1)}, u32[]{:S(2)}, u32[]{:S(2)}) collective-permute-start(bf16[128,2048]{1,0:T(8,128)(2,1)} %slice.515), channel_id=1, source_target_pairs={{0,16},{16,0},{1,17},{17,1},{2,18},{18,2},{3,19},{19,3},{4,20},{20... | collective-permute-start | bytes 1572872 | tf_op jit(solution)/shard_map/ppermute | solution.py:118
  147.3 14.2 %collective-permute-start.13 = (bf16[128,2048]{1,0:T(8,128)(2,1)}, bf16[128,2048]{1,0:T(8,128)(2,1)}, u32[]{:S(2)}, u32[]{:S(2)}) collective-permute-start(bf16[128,2048]{1,0:T(8,128)(2,1)} %slice.516), channel_id=1, source_target_pairs={{0,8},{8,0},{1,9},{9,1},{2,10},{10,2},{3,11},{11,3},{4,12},{12,4},... | collective-permute-start | bytes 1572872 | tf_op jit(solution)/shard_map/ppermute | solution.py:122
  186.3 130.2 %reduce-scatter.5.cloned.1.call-start = ((), (), s32[]{:S(2)}) async-start(), calls=%async_computation.9 | async-start | bytes 2621440 | tf_op jit(solution)/shard_map/reduce_scatter | solution.py:130
  186.9 39.1 %collective-permute-start.17 = (bf16[512,2048]{1,0:T(8,128)(2,1)S(1)}, bf16[512,2048]{1,0:T(8,128)(2,1)}, u32[]{:S(2)}, u32[]{:S(2)}) collective-permute-start(bf16[512,2048]{1,0:T(8,128)(2,1)S(1)} %copy-done.9), channel_id=1, source_target_pairs={{0,4},{4,0},{1,5},{5,1},{2,6},{6,2},{3,7},{7,3},{8,12},{12,8},{9,1... | collective-permute-start | bytes 6291464 | tf_op jit(solution)/shard_map/ppermute | solution.py:114
  187.1 25.5 %collective-permute-start.18 = (bf16[512,1024]{1,0:T(8,128)(2,1)S(1)}, bf16[512,1024]{1,0:T(8,128)(2,1)}, u32[]{:S(2)}, u32[]{:S(2)}) collective-permute-start(bf16[512,1024]{1,0:T(8,128)(2,1)S(1)} %bitcast.218), channel_id=1, source_target_pairs={{0,8},{8,0},{1,9},{9,1},{2,10},{10,2},{3,11},{11,3},{4,12},{12,4},... | collective-permute-start | bytes 3145736 | tf_op jit(solution)/shard_map/ppermute | solution.py:122
  188.9 25.2 %collective-permute-start.19 = (bf16[512,1024]{1,0:T(8,128)(2,1)S(1)}, bf16[512,1024]{1,0:T(8,128)(2,1)}, u32[]{:S(2)}, u32[]{:S(2)}) collective-permute-start(bf16[512,1024]{1,0:T(8,128)(2,1)S(1)} %bitcast.219), channel_id=1, source_target_pairs={{0,16},{16,0},{1,17},{17,1},{2,18},{18,2},{3,19},{19,3},{4,20},{20... | collective-permute-start | bytes 3145736 | tf_op jit(solution)/shard_map/ppermute | solution.py:118
  215.2 15.1 %collective-permute-start.20 = (bf16[256,1024]{1,0:T(8,128)(2,1)S(1)}, bf16[256,1024]{1,0:T(8,128)(2,1)S(1)}, u32[]{:S(2)}, u32[]{:S(2)}) collective-permute-start(bf16[256,1024]{1,0:T(8,128)(2,1)S(1)} %slice.527), channel_id=1, source_target_pairs={{0,16},{16,0},{1,17},{17,1},{2,18},{18,2},{3,19},{19,3},{4,20},{20... | collective-permute-start | bytes 1572872 | tf_op jit(solution)/shard_map/ppermute | solution.py:118
  283.9 27.4 %collective-permute-start.26 = (bf16[512,2048]{1,0:T(8,128)(2,1)}, bf16[512,2048]{1,0:T(8,128)(2,1)}, u32[]{:S(2)}, u32[]{:S(2)}) collective-permute-start(bf16[512,2048]{1,0:T(8,128)(2,1)} %convolution_convert_fusion), channel_id=1, source_target_pairs={{0,4},{4,0},{1,5},{5,1},{2,6},{6,2},{3,7},{7,3},{8,12},{12,8},{9,1... | collective-permute-start | bytes 6291464 | tf_op jit(solution)/shard_map/ppermute | solution.py:114
  284.3 25.6 %collective-permute-start.24 = (bf16[256,2048]{1,0:T(8,128)(2,1)}, bf16[256,2048]{1,0:T(8,128)(2,1)S(1)}, u32[]{:S(2)}, u32[]{:S(2)}) collective-permute-start(bf16[256,2048]{1,0:T(8,128)(2,1)} %convolution_convert_fusion.4), channel_id=1, source_target_pairs={{0,8},{8,0},{1,9},{9,1},{2,10},{10,2},{3,11},{11,3},{4,12},{12,4},... | collective-permute-start | bytes 3145736 | tf_op jit(solution)/shard_map/ppermute | solution.py:122
  285.9 25.4 %collective-permute-start.25 = (bf16[256,2048]{1,0:T(8,128)(2,1)}, bf16[256,2048]{1,0:T(8,128)(2,1)S(1)}, u32[]{:S(2)}, u32[]{:S(2)}) collective-permute-start(bf16[256,2048]{1,0:T(8,128)(2,1)} %convolution_convert_fusion.3), channel_id=1, source_target_pairs={{0,16},{16,0},{1,17},{17,1},{2,18},{18,2},{3,19},{19,3},{4,20},{20... | collective-permute-start | bytes 3145736 | tf_op jit(solution)/shard_map/ppermute | solution.py:118
  320.9 14.5 %collective-permute-start.28 = (bf16[128,2048]{1,0:T(8,128)(2,1)}, bf16[128,2048]{1,0:T(8,128)(2,1)S(1)}, u32[]{:S(2)}, u32[]{:S(2)}) collective-permute-start(bf16[128,2048]{1,0:T(8,128)(2,1)} %fusion.10), channel_id=1, source_target_pairs={{0,16},{16,0},{1,17},{17,1},{2,18},{18,2},{3,19},{19,3},{4,20},{20... | collective-permute-start | bytes 1572872 | tf_op jit(solution)/shard_map/ppermute | solution.py:118
  321.8 14.2 %collective-permute-start.29 = (bf16[128,2048]{1,0:T(8,128)(2,1)}, bf16[128,2048]{1,0:T(8,128)(2,1)S(1)}, u32[]{:S(2)}, u32[]{:S(2)}) collective-permute-start(bf16[128,2048]{1,0:T(8,128)(2,1)} %fusion.11), channel_id=1, source_target_pairs={{0,8},{8,0},{1,9},{9,1},{2,10},{10,2},{3,11},{11,3},{4,12},{12,4},... | collective-permute-start | bytes 1572872 | tf_op jit(solution)/shard_map/ppermute | solution.py:122
  338.7 26.1 %collective-permute-start.33 = (bf16[512,1024]{1,0:T(8,128)(2,1)}, bf16[512,1024]{1,0:T(8,128)(2,1)}, u32[]{:S(2)}, u32[]{:S(2)}) collective-permute-start(bf16[512,1024]{1,0:T(8,128)(2,1)} %convolution_convert_fusion.6), channel_id=1, source_target_pairs={{0,8},{8,0},{1,9},{9,1},{2,10},{10,2},{3,11},{11,3},{4,12},{12,4},... | collective-permute-start | bytes 3145736 | tf_op jit(solution)/shard_map/ppermute | solution.py:122
  340.2 25.2 %collective-permute-start.34 = (bf16[512,1024]{1,0:T(8,128)(2,1)}, bf16[512,1024]{1,0:T(8,128)(2,1)}, u32[]{:S(2)}, u32[]{:S(2)}) collective-permute-start(bf16[512,1024]{1,0:T(8,128)(2,1)} %convolution_convert_fusion.5), channel_id=1, source_target_pairs={{0,16},{16,0},{1,17},{17,1},{2,18},{18,2},{3,19},{19,3},{4,20},{20... | collective-permute-start | bytes 3145736 | tf_op jit(solution)/shard_map/ppermute | solution.py:118
  341.6 14.9 %all-to-all-start.2 = ((bf16[4,2,128,128]{3,2,1,0:T(8,128)(2,1)}), bf16[4,2,128,128]{3,2,1,0:T(8,128)(2,1)S(1)}, u32[]{:S(2)}, u32[]{:S(2)}) async-start(bf16[4,2,128,128]{3,2,1,0:T(8,128)(2,1)} %bitcast.230), calls=%async_computation.3 | async-start | bytes 524288 | tf_op jit(solution)/shard_map/all_to_all | solution.py:403
  345.8 74.0 %reduce-scatter.7.cloned.1.call-start = ((), (), s32[]{:S(2)}) async-start(), calls=%async_computation.10 | async-start | bytes 2621440 | tf_op jit(solution)/shard_map/reduce_scatter | solution.py:130
  355.2 124.4 %reduce-scatter.9.cloned.1.call-start = ((), (), s32[]{:S(2)}) async-start(), calls=%async_computation.11 | async-start | bytes 1474560 | tf_op jit(solution)/shard_map/reduce_scatter | solution.py:130
  362.7 28.4 %collective-permute-start.31 = (bf16[512,1152]{1,0:T(8,128)(2,1)S(1)}, bf16[512,1152]{1,0:T(8,128)(2,1)S(1)}, u32[]{:S(2)}, u32[]{:S(2)}) collective-permute-start(bf16[512,1152]{1,0:T(8,128)(2,1)S(1)} %convolution_convert_fusion.2), channel_id=1, source_target_pairs={{0,8},{8,0},{1,9},{9,1},{2,10},{10,2},{3,11},{11,3},{4,12},{12,4},... | collective-permute-start | bytes 3538952 | tf_op jit(solution)/shard_map/ppermute | solution.py:122
  364.4 28.0 %collective-permute-start.32 = (bf16[512,1152]{1,0:T(8,128)(2,1)S(1)}, bf16[512,1152]{1,0:T(8,128)(2,1)S(1)}, u32[]{:S(2)}, u32[]{:S(2)}) collective-permute-start(bf16[512,1152]{1,0:T(8,128)(2,1)S(1)} %convolution_convert_fusion.1), channel_id=1, source_target_pairs={{0,16},{16,0},{1,17},{17,1},{2,18},{18,2},{3,19},{19,3},{4,20},{20... | collective-permute-start | bytes 3538952 | tf_op jit(solution)/shard_map/ppermute | solution.py:118
  392.8 14.7 %collective-permute-start.36 = (bf16[256,1152]{1,0:T(8,128)(2,1)S(1)}, bf16[256,1152]{1,0:T(8,128)(2,1)S(1)}, u32[]{:S(2)}, u32[]{:S(2)}) collective-permute-start(bf16[256,1152]{1,0:T(8,128)(2,1)S(1)} %add_convert_fusion.5), channel_id=1, source_target_pairs={{0,16},{16,0},{1,17},{17,1},{2,18},{18,2},{3,19},{19,3},{4,20},{20... | collective-permute-start | bytes 1769480 | tf_op jit(solution)/shard_map/ppermute | solution.py:118
  393.7 14.5 %collective-permute-start.37 = (bf16[256,1152]{1,0:T(8,128)(2,1)S(1)}, bf16[256,1152]{1,0:T(8,128)(2,1)S(1)}, u32[]{:S(2)}, u32[]{:S(2)}) collective-permute-start(bf16[256,1152]{1,0:T(8,128)(2,1)S(1)} %add_convert_fusion.4), channel_id=1, source_target_pairs={{0,8},{8,0},{1,9},{9,1},{2,10},{10,2},{3,11},{11,3},{4,12},{12,4},... | collective-permute-start | bytes 1769480 | tf_op jit(solution)/shard_map/ppermute | solution.py:122
  408.2 45.2 %collective-permute-start.40 = (bf16[256,2048]{1,0:T(8,128)(2,1)}, bf16[256,2048]{1,0:T(8,128)(2,1)}, u32[]{:S(2)}, u32[]{:S(2)}) collective-permute-start(bf16[256,2048]{1,0:T(8,128)(2,1)} %convert_element_type.287), channel_id=1, source_target_pairs={{0,8},{8,0},{1,9},{9,1},{2,10},{10,2},{3,11},{11,3},{4,12},{12,4},... | collective-permute-start | bytes 3145736 | tf_op jit(solution)/shard_map/ppermute | solution.py:122
  408.9 44.5 %collective-permute-start.41 = (bf16[256,2048]{1,0:T(8,128)(2,1)}, bf16[256,2048]{1,0:T(8,128)(2,1)}, u32[]{:S(2)}, u32[]{:S(2)}) collective-permute-start(bf16[256,2048]{1,0:T(8,128)(2,1)} %convert_element_type.288), channel_id=1, source_target_pairs={{0,16},{16,0},{1,17},{17,1},{2,18},{18,2},{3,19},{19,3},{4,20},{20... | collective-permute-start | bytes 3145736 | tf_op jit(solution)/shard_map/ppermute | solution.py:118
  410.4 33.1 %collective-permute-start.38 = (bf16[256,1024]{1,0:T(8,128)(2,1)}, bf16[256,1024]{1,0:T(8,128)(2,1)}, u32[]{:S(2)}, u32[]{:S(2)}) collective-permute-start(bf16[256,1024]{1,0:T(8,128)(2,1)} %add_convert_fusion.10), channel_id=1, source_target_pairs={{0,16},{16,0},{1,17},{17,1},{2,18},{18,2},{3,19},{19,3},{4,20},{20... | collective-permute-start | bytes 1572872 | tf_op jit(solution)/shard_map/ppermute | solution.py:118
  410.9 32.6 %collective-permute-start.39 = (bf16[256,1024]{1,0:T(8,128)(2,1)}, bf16[256,1024]{1,0:T(8,128)(2,1)}, u32[]{:S(2)}, u32[]{:S(2)}) collective-permute-start(bf16[256,1024]{1,0:T(8,128)(2,1)} %add_convert_fusion.9), channel_id=1, source_target_pairs={{0,8},{8,0},{1,9},{9,1},{2,10},{10,2},{3,11},{11,3},{4,12},{12,4},... | collective-permute-start | bytes 1572872 | tf_op jit(solution)/shard_map/ppermute | solution.py:122
  448.2 31.3 %all-to-all-start.3 = ((bf16[8,64,1024]{2,1,0:T(8,128)(2,1)}), bf16[8,64,1024]{2,1,0:T(8,128)(2,1)}, u32[]{:S(2)}, u32[]{:S(2)}) async-start(bf16[8,64,1024]{2,1,0:T(8,128)(2,1)} %bitcast.229), calls=%async_computation.6 | async-start | bytes 2097152 | tf_op jit(solution)/shard_map/all_to_all | solution.py:437
  453.3 66.4 %reduce-scatter.11.cloned.1.call-start = ((), (), s32[]{:S(2)}) async-start(), calls=%async_computation.12 | async-start | bytes 1310720 | tf_op jit(solution)/shard_map/reduce_scatter | solution.py:130
  455.3 14.6 %collective-permute-start.42 = (bf16[128,2048]{1,0:T(8,128)(2,1)}, bf16[128,2048]{1,0:T(8,128)(2,1)}, u32[]{:S(2)}, u32[]{:S(2)}) collective-permute-start(bf16[128,2048]{1,0:T(8,128)(2,1)} %add_convert_fusion.8), channel_id=1, source_target_pairs={{0,16},{16,0},{1,17},{17,1},{2,18},{18,2},{3,19},{19,3},{4,20},{20... | collective-permute-start | bytes 1572872 | tf_op jit(solution)/shard_map/ppermute | solution.py:118
  459.0 14.3 %collective-permute-start.43 = (bf16[128,2048]{1,0:T(8,128)(2,1)}, bf16[128,2048]{1,0:T(8,128)(2,1)}, u32[]{:S(2)}, u32[]{:S(2)}) collective-permute-start(bf16[128,2048]{1,0:T(8,128)(2,1)} %add_convert_fusion.7), channel_id=1, source_target_pairs={{0,8},{8,0},{1,9},{9,1},{2,10},{10,2},{3,11},{11,3},{4,12},{12,4},... | collective-permute-start | bytes 1572872 | tf_op jit(solution)/shard_map/ppermute | solution.py:122
  497.7 20.1 %all-to-all-start.4 = ((f32[32,1,708]{2,1,0:T(1,128)}), f32[32,1,708]{2,1,0:T(1,128)S(1)}, u32[]{:S(2)}, u32[]{:S(2)}) async-start(f32[32,1,708]{2,1,0:T(1,128)} %all_to_all.23), calls=%async_computation.7 | async-start | bytes 196608 | tf_op jit(solution)/shard_map/all_to_all | solution.py:472
  500.9 15.2 %collective-permute-start.44 = (bf16[64,1152]{1,0:T(8,128)(2,1)S(1)}, bf16[64,1152]{1,0:T(8,128)(2,1)S(1)}, u32[]{:S(2)}, u32[]{:S(2)}) collective-permute-start(bf16[64,1152]{1,0:T(8,128)(2,1)S(1)} %select_bitcast_fusion), channel_id=1, source_target_pairs={{0,4},{4,0},{1,5},{5,1},{2,6},{6,2},{3,7},{7,3},{8,12},{12,8},{9,1... | collective-permute-start | bytes 442376 | tf_op jit(solution)/shard_map/ppermute | solution.py:114
  (114 other events, 1469.4 us)
Sparse Core Ops, SparseCore 0:
  15.3 34.2 all-gather.8
  55.6 30.9 all-gather.10
  100.4 56.9 all-gather.12
  186.5 47.3 all-gather.14
  271.7 44.1 reduce-scatter.4
  355.3 44.5 reduce-scatter.6
  419.9 29.8 reduce-scatter.8
  476.2 26.9 reduce-scatter.10

commit v4 on v3

--- a/solution.py
+++ b/solution.py
@@ -184,13 +184,13 @@
             self.sent = [u, w]
             self.far = [over_a(u), over_b(w)]
 
-    def finish(self, order):
+    def finish(self, order, free=False):
         if not self.square:
             return self.result
         f0, f1 = order(*self.far)
         half = f0.shape[0]
         n0, n1 = self.near[0][half:], self.near[1][half:]
-        return self.term((0, 0), (0, 1)) + (
+        return self.term((0, 0), (0, 1), free=free) + (
             jnp.concatenate([n0, n1]).astype(F32) + jnp.concatenate([f0, f1]).astype(F32)
         )
 
@@ -211,10 +211,10 @@
     def product(left, right, multiply=None):
         half = left.shape[1] // AB // 2
 
-        def term(*parts):
+        def term(*parts, free=False):
             cols = [left[:, (2 * i + j) * half : (2 * i + j + 1) * half] for i, j in parts]
             cols = jnp.concatenate(cols, axis=1)
-            return mm_tn(cols, right) if multiply is None else multiply(cols, right, 0, 0)
+            return side(cols, right, 0, 0) if free or multiply is not None else mm_tn(cols, right)
 
         return term
 
@@ -367,13 +367,14 @@
         dh2 = turn(scatter(dh2_part, "ctx").astype(F32), me)
         dpre_w, act_w, h2_all, cot_all = (jnp.concatenate(order(*pair)) for pair in (dpres, acts, h2s, cots))
 
-        def down_term(*parts):
+        def down_term(*parts, free=False):
             half = F0 // 2
             cols = [
                 lax.dynamic_slice_in_dim(act_w, (me ^ i if square else i) * F0 + j * half, half, axis=1)
                 for i, j in parts
             ]
-            return mm_tn(jnp.concatenate(cols, axis=1), cot_all)
+            cols = jnp.concatenate(cols, axis=1)
+            return side(cols, cot_all, 0, 0) if free else mm_tn(cols, cot_all)
 
         down_sum = ChipSum(down_term, square, AB)
         order.mark(down_sum.sent)
@@ -427,17 +428,31 @@
         if aligned:
             out_sum = ChipSum(product(o, order(db), side), square, AB, ext_sum.far)
             order.mark(out_sum.sent)
+        dx = (dmid + ln_back(dh1, g1, xhat1, rstd1)).astype(BF)
+        result = (mid + mlp.astype(F32) + bd).astype(BF)
+        ext_sum.far, dx, result = lax.optimization_barrier((ext_sum.far, dx, result))
         g_ext = ext_sum.finish(order).astype(BF).reshape(2, Z, R, E)
         g_ext = g_ext.transpose(1, 0, 2, 3).reshape(Z, 2 * R, E)
-        g_ext, mlp = lax.optimization_barrier((g_ext, mlp))
         order.mark(g_ext)
         g_ext = scatter(g_ext, "ctx").reshape(2, R, E)
         g_up = up_sum.finish(order).astype(BF).reshape(C * Z, R, F)
         order.mark(g_up)
         g_up = lax.all_to_all(g_up, ("core", "ctx"), 0, 0, tiled=True)
-        if aligned:
+        first, second = g_ext[0], g_ext[1]
+        mate = swap_core(jnp.where(c == 0, second, first))
+        mine = jnp.where(c == 0, first, second)
+        first, second = jnp.where(c == 0, mine, mate), jnp.where(c == 0, mate, mine)
+        g_q = [h[:, g * W0 : (g + 1) * W0] for g in range(G) for h in (first, second)]
+        g_q = jnp.concatenate(g_q, axis=1).astype(F32)
+        g_kv = jnp.concatenate([first[:, DH:], second[:, DH:]], axis=1).astype(F32)
+        g_down = down_sum.finish(order, free=True)
+        if aligned:
+            if square:
+                out_sum.near, g_down = lax.optimization_barrier((out_sum.near, g_down))
             out_sum.pass_on(order)
             order.mark(out_sum.sent)
+            if square:
+                out_sum.far, g_q, g_kv = lax.optimization_barrier((out_sum.far, g_q, g_kv))
             g_out = out_sum.finish(order).astype(BF).reshape(Z, R, D)
             order.mark(g_out)
             g_out = scatter(g_out, "ctx").astype(F32)
@@ -445,8 +460,6 @@
             g_out = mm_tn(o, order(db)).astype(BF)
             full = jnp.where(lax.broadcasted_iota(jnp.int32, (2, 1, 1), 0) == c, g_out[None], 0)
             g_out = scatter(full.reshape(N, R, D), EVERY).astype(F32)
-        g_ext, g_up = order(g_ext, g_up)
-        order.mark(g_ext, g_up)
         own_core = (lax.broadcasted_iota(jnp.int32, (1, 2, 1), 1) == c).astype(F32)
         own_cz = (lax.broadcasted_iota(jnp.int32, (1, C * Z, 1), 1) == c * Z + z).astype(F32)
         dh2_late, dpre_late, cot_late, dq_late, db_late = order(dh2, dpre_w, cotangent[0], dq_ext, db[:T])
@@ -470,23 +483,13 @@
             axis=1,
         )
         packed = jnp.sum(lax.all_to_all(packed, EVERY, 0, 0, tiled=True), axis=0)
-        g_down = down_sum.finish(order)
-        dx = dmid + ln_back(order(dh1), g1, xhat1, rstd1)
-        first, second = g_ext[0], g_ext[1]
-        mate = swap_core(jnp.where(c == 0, second, first))
-        mine = jnp.where(c == 0, first, second)
-        first, second = jnp.where(c == 0, mine, mate), jnp.where(c == 0, mate, mine)
-        g_q = [h[:, g * W0 : (g + 1) * W0] for g in range(G) for h in (first, second)]
-        g_q = jnp.concatenate(g_q, axis=1).astype(F32)
-        g_kv = jnp.concatenate([first[:, DH:], second[:, DH:]], axis=1).astype(F32)
         g_up = g_up.reshape(C * Z, R, AB, F0).transpose(1, 2, 0, 3).reshape(R, FF).astype(F32)
-        result = order(mid) + mlp.astype(F32) + bd
 
         vecs = [packed[i * R : (i + 1) * R] for i in range(7)]
         gb_up = packed[7 * R : 7 * R + F0]
         gb_v = packed[7 * R + F0 :]
         return (
-            result.astype(BF)[None], dx.astype(BF)[None],
+            result[None], dx[None],
             vecs[0], vecs[1], g_q, vecs[2], g_kv, gb_v, g_out, vecs[3],
             vecs[4], vecs[5], g_up, gb_up, g_down, vecs[6],
         )

time: 538 us -> 527 us (0.980)
  waiting for transfers between devices: 150 us -> 139 us
    ppermute x16, waiting for transfers between devices: 45.3 us -> 15.5 us  [over_a(): return lax.ppermute(x, 'a', MATES)]
    ppermute x16, waiting for transfers between devices: 65.8 us -> 78.7 us  [over_b(): return lax.ppermute(x, 'b', MATES)]
    reduce_scatter x4, waiting for transfers between devices: 0.01 us -> 6.34 us  [scatter(): return lax.psum_scatter(x, axes, scatter_dimension=0, tiled=False)]
    unnamed x240 -> x226, local copies, waits for them, and re-layouts: 48.3 us -> 52.9 us
    pallas_call x12 -> x13, Pallas kernels: 28.1 us -> 30.5 us  [side(): pl.pallas_call(kernel, out_shape=jax.ShapeDtypeStruct((count, cols), out)...]
    dot_general x20 -> x19, matrix products: 44.8 us -> 43.2 us  [dot(): return lax.dot_general(a, b, (dims, ((), ())), preferred_element_type=F32)]
  transfers between devices with their start and end apart: 58 -> 58, of which waited for: 27 -> 28; matrix products, arithmetic and copies ran while one was open for 32% -> 30% of each run, Pallas kernels for 5% -> 6%
where the time goes in v4:
time: 527 us; the launch traced here: 518 us
  waiting for transfers between devices  139 us (26%)
  local copies, waits for them, and re-layouts  108 us (20%)
  starting transfers between devices  72.9 us (14%)
  other arithmetic  66 us (13%)
  matrix products  52.9 us (10%)
  Pallas kernels  41.4 us (8%)
  blocking collectives  21.3 us (4%)
  between operations  16.6 us (3%)
    ppermute x16, waiting for transfers between devices, over_b(): return lax.ppermute(x, 'b', MATES)  78.7 us
    unnamed x226, local copies, waits for them, and re-layouts  52.9 us
    dot_general x19, matrix products, dot(): return lax.dot_general(a, b, (dims, ((), ())), preferred_element_type=F32)  43.2 us
    pallas_call x13, Pallas kernels, side(): pl.pallas_call(kernel, out_shape=jax.ShapeDtypeStruct((count, cols), out)...  30.5 us
    ppermute x16, starting transfers between devices, over_b(): return lax.ppermute(x, 'b', MATES)  27.3 us
    all_gather x1, blocking collectives, gather(): return lax.all_gather(x, axes, axis=0, tiled=False)  21.3 us
    ppermute x16, starting transfers between devices, over_a(): return lax.ppermute(x, 'a', MATES)  20.6 us
    all_to_all x1, waiting for transfers between devices, local(): small = lax.all_to_all(small, EVERY, 0, 0, tiled=True).astype(F32)  17.3 us
  transfers between devices with their start and end apart: 58, of which 28 were waited for; matrix products, arithmetic and copies ran while one was open for 30% of the time, Pallas kernels for 6%

profile of v4, /device:TPU:0, one launch (start us, length us, event | category | flops | bytes accessed | tf_op | source)
XLA Modules:
  0.0 518.4 jit_solution(14193093976143861024)
XLA Ops:
  16.5 2.9 collective-permute-start.4
  23.3 4.0 all-to-all-start
  27.8 17.3 %all-to-all-done = bf16[32,2,354]{2,1,0:T(2,128)(2,1)S(1)} async-done(((bf16[32,2,354]{2,1,0:T(2,128)(2,1)}), bf16[32,2,354]{2,1,0:T(2,128)(2,1)S(1)}, u32[]{:S(2)}, u32[]{:S(2)}) %all-to-all-start) | async-done | bytes 45344 | tf_op jit(solution)/shard_map/all_to_all | solution.py:263
  46.1 3.5 all-gather.9.cloned.1.call-done
  64.0 3.6 all-to-all-start.1
  70.2 8.5 %collective-permute-done.2 = bf16[512,1152]{1,0:T(8,128)(2,1)} collective-permute-done((bf16[512,1152]{1,0:T(8,128)(2,1)S(1)}, bf16[512,1152]{1,0:T(8,128)(2,1)}, u32[]{:S(2)}, u32[]{:S(2)}) %collective-permute-start.2) | collective-permute-done | bytes 1179680 | tf_op jit(solution)/shard_map/ppermute | solution.py:122
  79.9 6.7 %all-gather.11.cloned.1.call-done = bf16[256,2048]{1,0:T(8,128)(2,1)} async-done(((bf16[64,2048]{1,0:T(8,128)(2,1)}), bf16[256,2048]{1,0:T(8,128)(2,1)}) %all-gather.11.cloned.1.call-update) | async-done | bytes 1048592 | tf_op jit(solution)/shard_map/all_gather | solution.py:126
  88.5 3.0 collective-permute-start.6
  93.5 4.4 collective-permute-start.7
  106.2 4.3 collective-permute-start.15
  120.1 21.3 %all_gather.31 = bf16[4,2,128,128]{3,2,1,0:T(8,128)(2,1)S(1)} all-gather(bf16[1,2,128,128]{3,2,1,0:T(8,128)(2,1)S(1)} %bitcast.234), channel_id=1, replica_groups=mesh['a'=2,'b'=2,'core'=2,'ctx'=4] {'ctx'}, dimensions={0}, use_global_device_ids=true | all-gather | bytes 327680 | tf_op jit(solution)/shard_map/all_gather | solution.py:126
  149.0 2.8 fusion.67
  151.8 7.9 %fusion.8 = f32[2,8,128,512]{2,3,1,0:T(8,128)} fusion(f32[2,512,128,8]{2,1,3,0:T(8,128)} %fusion.67, pred[2,128,512]{1,2,0:T(8,128)(4,1)} %compare_and_fusion), kind=kOutput, calls=%fused_computation.23 | output fusion | flops 6296574 | bytes 8519680 | tf_op jit(solution)/shard_map/div | solution.py:320
  162.5 2.7 fusion.23
  165.6 2.6 constant_dynamic-update-slice_fusion.18
  174.3 3.9 fusion.82
  181.2 3.1 fusion.123
  194.4 18.6 %collective-permute-done.18 = bf16[512,1024]{1,0:T(8,128)(2,1)} collective-permute-done((bf16[512,1024]{1,0:T(8,128)(2,1)S(1)}, bf16[512,1024]{1,0:T(8,128)(2,1)}, u32[]{:S(2)}, u32[]{:S(2)}) %collective-permute-start.18) | collective-permute-done | bytes 1048608 | tf_op jit(solution)/shard_map/ppermute | solution.py:122
  222.3 2.7 side.13.d_ref
  226.4 4.3 side.14.d_ref
  236.3 4.4 collective-permute-done.22.h_ref
  244.5 6.2 %hidden.3 = (bf16[512,1024]{1,0:T(8,128)(2,1)S(1)}, bf16[512,1024]{1,0:T(8,128)(2,1)S(1)}) custom-call(bf16[512,2048]{1,0:T(8,128)(2,1)} %collective-permute-done.22.h_ref, bf16[2048,1024]{1,0:T(8,128)(2,1)S(1)} %copy-done.1, f32[1,1024]{1,0:T(1,128)S(1)} %bitcast.185, f32[512,1024]{1,0:T(8,128)S(1)} %copy-done.20), custom_call_target="tpu_custom_call" | custom-call | flops 2147483648 | bytes 6291456 | tf_op jit(solution)/shard_map/hidden/pallas_call | solution.py:75
  250.7 3.9 side.16
  260.1 4.8 hidden.2
  264.9 3.4 side.15
  268.3 3.7 add_convert_fusion.1
  280.5 3.7 convolution_convert_fusion
  296.1 14.1 %collective-permute-done.24 = bf16[256,2048]{1,0:T(8,128)(2,1)S(1)} collective-permute-done((bf16[256,2048]{1,0:T(8,128)(2,1)}, bf16[256,2048]{1,0:T(8,128)(2,1)S(1)}, u32[]{:S(2)}, u32[]{:S(2)}) %collective-permute-start.24) | collective-permute-done | bytes 1048608 | tf_op jit(solution)/shard_map/ppermute | solution.py:122
  328.2 6.7 %collective-permute-done.28 = bf16[128,2048]{1,0:T(8,128)(2,1)S(1)} collective-permute-done((bf16[128,2048]{1,0:T(8,128)(2,1)S(1)}, bf16[128,2048]{1,0:T(8,128)(2,1)S(1)}, u32[]{:S(2)}, u32[]{:S(2)}) %collective-permute-start.28) | collective-permute-done | bytes 524320 | tf_op jit(solution)/shard_map/ppermute | solution.py:118
  343.3 3.4 all-to-all-start.2
  349.0 3.4 side.17
  352.4 3.7 add_convert_fusion
  362.9 2.4 side.19
  367.7 2.8 add_convert_fusion.9
  370.5 2.7 add_convert_fusion.8
  377.1 17.1 %collective-permute-done.31 = bf16[512,1152]{1,0:T(8,128)(2,1)S(1)} collective-permute-done((bf16[512,1152]{1,0:T(8,128)(2,1)S(1)}, bf16[512,1152]{1,0:T(8,128)(2,1)S(1)}, u32[]{:S(2)}, u32[]{:S(2)}) %collective-permute-start.31) | collective-permute-done | bytes 1179680 | tf_op jit(solution)/shard_map/ppermute | solution.py:122
  411.7 3.0 collective-permute-done.37
  435.9 3.9 add_convert_fusion.3
  439.8 5.2 all-to-all-start.4
  445.0 2.9 add_add_fusion
  448.0 5.7 %collective-permute-done.38 = bf16[256,2048]{1,0:T(8,128)(2,1)} collective-permute-done((bf16[256,2048]{1,0:T(8,128)(2,1)}, bf16[256,2048]{1,0:T(8,128)(2,1)}, u32[]{:S(2)}, u32[]{:S(2)}) %collective-permute-start.38) | collective-permute-done | bytes 1048608 | tf_op jit(solution)/shard_map/ppermute | solution.py:122
  467.0 3.6 collective-permute-done.42
  470.6 6.7 %collective-permute-done.43 = bf16[128,2048]{1,0:T(8,128)(2,1)S(1)} collective-permute-done((bf16[128,2048]{1,0:T(8,128)(2,1)S(1)}, bf16[128,2048]{1,0:T(8,128)(2,1)S(1)}, u32[]{:S(2)}, u32[]{:S(2)}) %collective-permute-start.43) | collective-permute-done | bytes 524320 | tf_op jit(solution)/shard_map/ppermute | solution.py:122
  477.3 2.5 add_convert_fusion.2
  487.0 5.4 %all-to-all-start.3 = ((f32[32,1,708]{2,1,0:T(1,128)}), f32[32,1,708]{2,1,0:T(1,128)S(1)}, u32[]{:S(2)}, u32[]{:S(2)}) async-start(f32[32,1,708]{2,1,0:T(1,128)} %all_to_all.22), calls=%async_computation.6 | async-start | bytes 196608 | tf_op jit(solution)/shard_map/all_to_all | solution.py:485
  495.7 2.5 copy.97
  498.2 3.7 all-to-all-done.3
  503.8 5.4 %reduce-scatter.11.cloned.1.call-done = bf16[1,64,2048]{2,1,0:T(8,128)(2,1)} async-done(((bf16[4,64,2048]{2,1,0:T(8,128)(2,1)}), bf16[1,64,2048]{2,1,0:T(8,128)(2,1)}) %reduce-scatter.11.cloned.1.call-update) | async-done | bytes 262160 | tf_op jit(solution)/shard_map/reduce_scatter | solution.py:130
  (519 shorter events, 236.9 us)
Async XLA Ops:
  7.3 42.3 %all-gather.9.cloned.1.call-start = ((), (), s32[]{:S(2)}) async-start(), calls=%async_computation.13 | async-start | bytes 1474560 | tf_op jit(solution)/shard_map/all_gather | solution.py:126
  16.5 53.7 %collective-permute-start.4 = (bf16[256,2048]{1,0:T(8,128)(2,1)}, bf16[256,2048]{1,0:T(8,128)(2,1)}, u32[]{:S(2)}, u32[]{:S(2)}) collective-permute-start(bf16[256,2048]{1,0:T(8,128)(2,1)} %param.31), channel_id=1, source_target_pairs={{0,8},{8,0},{1,9},{9,1},{2,10},{10,2},{3,11},{11,3},{4,12},{12,4},... | collective-permute-start | bytes 3145736 | tf_op jit(solution)/shard_map/ppermute | solution.py:122
  19.4 50.8 %collective-permute-start.5 = (bf16[256,2048]{1,0:T(8,128)(2,1)}, bf16[256,2048]{1,0:T(8,128)(2,1)}, u32[]{:S(2)}, u32[]{:S(2)}) collective-permute-start(bf16[256,2048]{1,0:T(8,128)(2,1)} %param.31), channel_id=1, source_target_pairs={{0,16},{16,0},{1,17},{17,1},{2,18},{18,2},{3,19},{19,3},{4,20},{20... | collective-permute-start | bytes 3145736 | tf_op jit(solution)/shard_map/ppermute | solution.py:118
  23.3 21.8 %all-to-all-start = ((bf16[32,2,354]{2,1,0:T(2,128)(2,1)}), bf16[32,2,354]{2,1,0:T(2,128)(2,1)S(1)}, u32[]{:S(2)}, u32[]{:S(2)}) async-start(bf16[32,2,354]{2,1,0:T(2,128)(2,1)} %reshape.313), calls=%async_computation | async-start | bytes 98304 | tf_op jit(solution)/shard_map/all_to_all | solution.py:263
  27.3 59.3 %all-gather.11.cloned.1.call-start = ((), (), s32[]{:S(2)}) async-start(), calls=%async_computation.14 | async-start | bytes 1310720 | tf_op jit(solution)/shard_map/all_gather | solution.py:126
  51.0 27.7 %collective-permute-start.2 = (bf16[512,1152]{1,0:T(8,128)(2,1)S(1)}, bf16[512,1152]{1,0:T(8,128)(2,1)}, u32[]{:S(2)}, u32[]{:S(2)}) collective-permute-start(bf16[512,1152]{1,0:T(8,128)(2,1)S(1)} %bitcast.202), channel_id=1, source_target_pairs={{0,8},{8,0},{1,9},{9,1},{2,10},{10,2},{3,11},{11,3},{4,12},{12,4},... | collective-permute-start | bytes 3538952 | tf_op jit(solution)/shard_map/ppermute | solution.py:122
  52.5 27.4 %collective-permute-start.3 = (bf16[512,1152]{1,0:T(8,128)(2,1)S(1)}, bf16[512,1152]{1,0:T(8,128)(2,1)}, u32[]{:S(2)}, u32[]{:S(2)}) collective-permute-start(bf16[512,1152]{1,0:T(8,128)(2,1)S(1)} %bitcast.203), channel_id=1, source_target_pairs={{0,16},{16,0},{1,17},{17,1},{2,18},{18,2},{3,19},{19,3},{4,20},{20... | collective-permute-start | bytes 3538952 | tf_op jit(solution)/shard_map/ppermute | solution.py:118
  64.0 46.5 %all-to-all-start.1 = ((bf16[8,64,1024]{2,1,0:T(8,128)(2,1)}), bf16[8,64,1024]{2,1,0:T(8,128)(2,1)S(1)}, u32[]{:S(2)}, u32[]{:S(2)}) async-start(bf16[8,64,1024]{2,1,0:T(8,128)(2,1)} %fusion.92), calls=%async_computation.1 | async-start | bytes 2097152 | tf_op jit(solution)/shard_map/all_to_all | solution.py:293
  67.5 93.9 %all-gather.13.cloned.1.call-start = ((), (), s32[]{:S(2)}) async-start(), calls=%async_computation.15 | async-start | bytes 2621440 | tf_op jit(solution)/shard_map/all_gather | solution.py:126
  69.0 29.2 %collective-permute-start.1 = (bf16[128,2048]{1,0:T(8,128)(2,1)}, bf16[128,2048]{1,0:T(8,128)(2,1)}, u32[]{:S(2)}, u32[]{:S(2)}) collective-permute-start(bf16[128,2048]{1,0:T(8,128)(2,1)} %pad_maximum_fusion.5), channel_id=1, source_target_pairs={{0,4},{4,0},{1,5},{5,1},{2,6},{6,2},{3,7},{7,3},{8,12},{12,8},{9,1... | collective-permute-start | bytes 1572872 | tf_op jit(solution)/shard_map/ppermute | solution.py:114
  88.5 17.7 %collective-permute-start.6 = (bf16[256,1152]{1,0:T(8,128)(2,1)}, bf16[256,1152]{1,0:T(8,128)(2,1)}, u32[]{:S(2)}, u32[]{:S(2)}) collective-permute-start(bf16[256,1152]{1,0:T(8,128)(2,1)} %slice.475), channel_id=1, source_target_pairs={{0,16},{16,0},{1,17},{17,1},{2,18},{18,2},{3,19},{19,3},{4,20},{20... | collective-permute-start | bytes 1769480 | tf_op jit(solution)/shard_map/ppermute | solution.py:118
  93.5 18.9 %collective-permute-start.7 = (bf16[256,1152]{1,0:T(8,128)(2,1)}, bf16[256,1152]{1,0:T(8,128)(2,1)}, u32[]{:S(2)}, u32[]{:S(2)}) collective-permute-start(bf16[256,1152]{1,0:T(8,128)(2,1)} %slice.476), channel_id=1, source_target_pairs={{0,8},{8,0},{1,9},{9,1},{2,10},{10,2},{3,11},{11,3},{4,12},{12,4},... | collective-permute-start | bytes 1769480 | tf_op jit(solution)/shard_map/ppermute | solution.py:122
  100.3 42.9 %collective-permute-start.10 = (bf16[256,2048]{1,0:T(8,128)(2,1)}, bf16[256,2048]{1,0:T(8,128)(2,1)}, u32[]{:S(2)}, u32[]{:S(2)}) collective-permute-start(bf16[256,2048]{1,0:T(8,128)(2,1)} %all-gather.11.cloned.1.call-done), channel_id=1, source_target_pairs={{0,8},{8,0},{1,9},{9,1},{2,10},{10,2},{3,11},{11,3},{4,12},{12,4},... | collective-permute-start | bytes 3145736 | tf_op jit(solution)/shard_map/ppermute | solution.py:122
  100.3 42.9 %collective-permute-start.11 = (bf16[256,2048]{1,0:T(8,128)(2,1)}, bf16[256,2048]{1,0:T(8,128)(2,1)}, u32[]{:S(2)}, u32[]{:S(2)}) collective-permute-start(bf16[256,2048]{1,0:T(8,128)(2,1)} %all-gather.11.cloned.1.call-done), channel_id=1, source_target_pairs={{0,16},{16,0},{1,17},{17,1},{2,18},{18,2},{3,19},{19,3},{4,20},{20... | collective-permute-start | bytes 3145736 | tf_op jit(solution)/shard_map/ppermute | solution.py:118
  100.3 135.9 %all-gather.15.cloned.1.call-start = ((), (), s32[]{:S(2)}) async-start(), calls=%async_computation.16 | async-start | bytes 2621440 | tf_op jit(solution)/shard_map/all_gather | solution.py:126
  102.3 57.5 %collective-permute-start.14 = (bf16[128,2048]{1,0:T(8,128)(2,1)}, bf16[128,2048]{1,0:T(8,128)(2,1)}, u32[]{:S(2)}, u32[]{:S(2)}) collective-permute-start(bf16[128,2048]{1,0:T(8,128)(2,1)} %slice.519), channel_id=1, source_target_pairs={{0,16},{16,0},{1,17},{17,1},{2,18},{18,2},{3,19},{19,3},{4,20},{20... | collective-permute-start | bytes 1572872 | tf_op jit(solution)/shard_map/ppermute | solution.py:118
  106.2 53.6 %collective-permute-start.15 = (bf16[128,2048]{1,0:T(8,128)(2,1)}, bf16[128,2048]{1,0:T(8,128)(2,1)}, u32[]{:S(2)}, u32[]{:S(2)}) collective-permute-start(bf16[128,2048]{1,0:T(8,128)(2,1)} %slice.520), channel_id=1, source_target_pairs={{0,8},{8,0},{1,9},{9,1},{2,10},{10,2},{3,11},{11,3},{4,12},{12,4},... | collective-permute-start | bytes 1572872 | tf_op jit(solution)/shard_map/ppermute | solution.py:122
  145.1 14.6 %collective-permute-start.12 = (bf16[128,2048]{1,0:T(8,128)(2,1)}, bf16[128,2048]{1,0:T(8,128)(2,1)}, u32[]{:S(2)}, u32[]{:S(2)}) collective-permute-start(bf16[128,2048]{1,0:T(8,128)(2,1)} %slice.517), channel_id=1, source_target_pairs={{0,16},{16,0},{1,17},{17,1},{2,18},{18,2},{3,19},{19,3},{4,20},{20... | collective-permute-start | bytes 1572872 | tf_op jit(solution)/shard_map/ppermute | solution.py:118
  147.2 14.2 %collective-permute-start.13 = (bf16[128,2048]{1,0:T(8,128)(2,1)}, bf16[128,2048]{1,0:T(8,128)(2,1)}, u32[]{:S(2)}, u32[]{:S(2)}) collective-permute-start(bf16[128,2048]{1,0:T(8,128)(2,1)} %slice.518), channel_id=1, source_target_pairs={{0,8},{8,0},{1,9},{9,1},{2,10},{10,2},{3,11},{11,3},{4,12},{12,4},... | collective-permute-start | bytes 1572872 | tf_op jit(solution)/shard_map/ppermute | solution.py:122
  186.5 129.8 %reduce-scatter.5.cloned.1.call-start = ((), (), s32[]{:S(2)}) async-start(), calls=%async_computation.9 | async-start | bytes 2621440 | tf_op jit(solution)/shard_map/reduce_scatter | solution.py:130
  187.1 39.2 %collective-permute-start.17 = (bf16[512,2048]{1,0:T(8,128)(2,1)S(1)}, bf16[512,2048]{1,0:T(8,128)(2,1)}, u32[]{:S(2)}, u32[]{:S(2)}) collective-permute-start(bf16[512,2048]{1,0:T(8,128)(2,1)S(1)} %copy-done.14), channel_id=1, source_target_pairs={{0,4},{4,0},{1,5},{5,1},{2,6},{6,2},{3,7},{7,3},{8,12},{12,8},{9,1... | collective-permute-start | bytes 6291464 | tf_op jit(solution)/shard_map/ppermute | solution.py:114
  187.7 25.3 %collective-permute-start.18 = (bf16[512,1024]{1,0:T(8,128)(2,1)S(1)}, bf16[512,1024]{1,0:T(8,128)(2,1)}, u32[]{:S(2)}, u32[]{:S(2)}) collective-permute-start(bf16[512,1024]{1,0:T(8,128)(2,1)S(1)} %bitcast.215), channel_id=1, source_target_pairs={{0,8},{8,0},{1,9},{9,1},{2,10},{10,2},{3,11},{11,3},{4,12},{12,4},... | collective-permute-start | bytes 3145736 | tf_op jit(solution)/shard_map/ppermute | solution.py:122
  189.4 25.0 %collective-permute-start.19 = (bf16[512,1024]{1,0:T(8,128)(2,1)S(1)}, bf16[512,1024]{1,0:T(8,128)(2,1)}, u32[]{:S(2)}, u32[]{:S(2)}) collective-permute-start(bf16[512,1024]{1,0:T(8,128)(2,1)S(1)} %bitcast.216), channel_id=1, source_target_pairs={{0,16},{16,0},{1,17},{17,1},{2,18},{18,2},{3,19},{19,3},{4,20},{20... | collective-permute-start | bytes 3145736 | tf_op jit(solution)/shard_map/ppermute | solution.py:118
  215.5 15.2 %collective-permute-start.20 = (bf16[256,1024]{1,0:T(8,128)(2,1)S(1)}, bf16[256,1024]{1,0:T(8,128)(2,1)S(1)}, u32[]{:S(2)}, u32[]{:S(2)}) collective-permute-start(bf16[256,1024]{1,0:T(8,128)(2,1)S(1)} %slice.530), channel_id=1, source_target_pairs={{0,16},{16,0},{1,17},{17,1},{2,18},{18,2},{3,19},{19,3},{4,20},{20... | collective-permute-start | bytes 1572872 | tf_op jit(solution)/shard_map/ppermute | solution.py:118
  218.4 12.5 %collective-permute-start.21 = (bf16[256,1024]{1,0:T(8,128)(2,1)S(1)}, bf16[256,1024]{1,0:T(8,128)(2,1)S(1)}, u32[]{:S(2)}, u32[]{:S(2)}) collective-permute-start(bf16[256,1024]{1,0:T(8,128)(2,1)S(1)} %slice.531), channel_id=1, source_target_pairs={{0,8},{8,0},{1,9},{9,1},{2,10},{10,2},{3,11},{11,3},{4,12},{12,4},... | collective-permute-start | bytes 1572872 | tf_op jit(solution)/shard_map/ppermute | solution.py:122
  254.5 13.8 %collective-permute-start.23 = (bf16[512,2048]{1,0:T(8,128)(2,1)}, bf16[512,2048]{1,0:T(8,128)(2,1)}, u32[]{:S(2)}, u32[]{:S(2)}) collective-permute-start(bf16[512,2048]{1,0:T(8,128)(2,1)} %side.16), channel_id=1, source_target_pairs={{0,4},{4,0},{1,5},{5,1},{2,6},{6,2},{3,7},{7,3},{8,12},{12,8},{9,1... | collective-permute-start | bytes 6291464 | tf_op jit(solution)/shard_map/ppermute | solution.py:114
  284.2 27.5 %collective-permute-start.26 = (bf16[512,2048]{1,0:T(8,128)(2,1)}, bf16[512,2048]{1,0:T(8,128)(2,1)}, u32[]{:S(2)}, u32[]{:S(2)}) collective-permute-start(bf16[512,2048]{1,0:T(8,128)(2,1)} %convolution_convert_fusion), channel_id=1, source_target_pairs={{0,4},{4,0},{1,5},{5,1},{2,6},{6,2},{3,7},{7,3},{8,12},{12,8},{9,1... | collective-permute-start | bytes 6291464 | tf_op jit(solution)/shard_map/ppermute | solution.py:114
  284.5 25.7 %collective-permute-start.24 = (bf16[256,2048]{1,0:T(8,128)(2,1)}, bf16[256,2048]{1,0:T(8,128)(2,1)S(1)}, u32[]{:S(2)}, u32[]{:S(2)}) collective-permute-start(bf16[256,2048]{1,0:T(8,128)(2,1)} %convolution_convert_fusion.4), channel_id=1, source_target_pairs={{0,8},{8,0},{1,9},{9,1},{2,10},{10,2},{3,11},{11,3},{4,12},{12,4},... | collective-permute-start | bytes 3145736 | tf_op jit(solution)/shard_map/ppermute | solution.py:122
  286.2 25.4 %collective-permute-start.25 = (bf16[256,2048]{1,0:T(8,128)(2,1)}, bf16[256,2048]{1,0:T(8,128)(2,1)S(1)}, u32[]{:S(2)}, u32[]{:S(2)}) collective-permute-start(bf16[256,2048]{1,0:T(8,128)(2,1)} %convolution_convert_fusion.3), channel_id=1, source_target_pairs={{0,16},{16,0},{1,17},{17,1},{2,18},{18,2},{3,19},{19,3},{4,20},{20... | collective-permute-start | bytes 3145736 | tf_op jit(solution)/shard_map/ppermute | solution.py:118
  320.5 14.3 %collective-permute-start.28 = (bf16[128,2048]{1,0:T(8,128)(2,1)S(1)}, bf16[128,2048]{1,0:T(8,128)(2,1)S(1)}, u32[]{:S(2)}, u32[]{:S(2)}) collective-permute-start(bf16[128,2048]{1,0:T(8,128)(2,1)S(1)} %fusion.10), channel_id=1, source_target_pairs={{0,16},{16,0},{1,17},{17,1},{2,18},{18,2},{3,19},{19,3},{4,20},{20... | collective-permute-start | bytes 1572872 | tf_op jit(solution)/shard_map/ppermute | solution.py:118
  322.1 14.0 %collective-permute-start.29 = (bf16[128,2048]{1,0:T(8,128)(2,1)S(1)}, bf16[128,2048]{1,0:T(8,128)(2,1)S(1)}, u32[]{:S(2)}, u32[]{:S(2)}) collective-permute-start(bf16[128,2048]{1,0:T(8,128)(2,1)S(1)} %fusion.11), channel_id=1, source_target_pairs={{0,8},{8,0},{1,9},{9,1},{2,10},{10,2},{3,11},{11,3},{4,12},{12,4},... | collective-permute-start | bytes 1572872 | tf_op jit(solution)/shard_map/ppermute | solution.py:122
  339.6 28.1 %collective-permute-start.33 = (bf16[512,1024]{1,0:T(8,128)(2,1)}, bf16[512,1024]{1,0:T(8,128)(2,1)}, u32[]{:S(2)}, u32[]{:S(2)}) collective-permute-start(bf16[512,1024]{1,0:T(8,128)(2,1)} %convolution_convert_fusion.6), channel_id=1, source_target_pairs={{0,8},{8,0},{1,9},{9,1},{2,10},{10,2},{3,11},{11,3},{4,12},{12,4},... | collective-permute-start | bytes 3145736 | tf_op jit(solution)/shard_map/ppermute | solution.py:122
  340.9 26.8 %collective-permute-start.34 = (bf16[512,1024]{1,0:T(8,128)(2,1)}, bf16[512,1024]{1,0:T(8,128)(2,1)}, u32[]{:S(2)}, u32[]{:S(2)}) collective-permute-start(bf16[512,1024]{1,0:T(8,128)(2,1)} %convolution_convert_fusion.5), channel_id=1, source_target_pairs={{0,16},{16,0},{1,17},{17,1},{2,18},{18,2},{3,19},{19,3},{4,20},{20... | collective-permute-start | bytes 3145736 | tf_op jit(solution)/shard_map/ppermute | solution.py:118
  343.3 15.8 %all-to-all-start.2 = ((bf16[4,2,128,128]{3,2,1,0:T(8,128)(2,1)}), bf16[4,2,128,128]{3,2,1,0:T(8,128)(2,1)S(1)}, u32[]{:S(2)}, u32[]{:S(2)}) async-start(bf16[4,2,128,128]{3,2,1,0:T(8,128)(2,1)} %bitcast.181), calls=%async_computation.3 | async-start | bytes 524288 | tf_op jit(solution)/shard_map/all_to_all | solution.py:404
  346.8 62.4 %reduce-scatter.7.cloned.1.call-start = ((), (), s32[]{:S(2)}) async-start(), calls=%async_computation.10 | async-start | bytes 2621440 | tf_op jit(solution)/shard_map/reduce_scatter | solution.py:130
  356.2 104.4 %reduce-scatter.9.cloned.1.call-start = ((), (), s32[]{:S(2)}) async-start(), calls=%async_computation.11 | async-start | bytes 1474560 | tf_op jit(solution)/shard_map/reduce_scatter | solution.py:130
  365.7 28.4 %collective-permute-start.31 = (bf16[512,1152]{1,0:T(8,128)(2,1)S(1)}, bf16[512,1152]{1,0:T(8,128)(2,1)S(1)}, u32[]{:S(2)}, u32[]{:S(2)}) collective-permute-start(bf16[512,1152]{1,0:T(8,128)(2,1)S(1)} %convolution_convert_fusion.2), channel_id=1, source_target_pairs={{0,8},{8,0},{1,9},{9,1},{2,10},{10,2},{3,11},{11,3},{4,12},{12,4},... | collective-permute-start | bytes 3538952 | tf_op jit(solution)/shard_map/ppermute | solution.py:122
  366.5 28.1 %collective-permute-start.32 = (bf16[512,1152]{1,0:T(8,128)(2,1)S(1)}, bf16[512,1152]{1,0:T(8,128)(2,1)S(1)}, u32[]{:S(2)}, u32[]{:S(2)}) collective-permute-start(bf16[512,1152]{1,0:T(8,128)(2,1)S(1)} %convolution_convert_fusion.1), channel_id=1, source_target_pairs={{0,16},{16,0},{1,17},{17,1},{2,18},{18,2},{3,19},{19,3},{4,20},{20... | collective-permute-start | bytes 3538952 | tf_op jit(solution)/shard_map/ppermute | solution.py:118
  396.7 15.0 %collective-permute-start.36 = (bf16[256,1152]{1,0:T(8,128)(2,1)}, bf16[256,1152]{1,0:T(8,128)(2,1)}, u32[]{:S(2)}, u32[]{:S(2)}) collective-permute-start(bf16[256,1152]{1,0:T(8,128)(2,1)} %add_convert_fusion.5), channel_id=1, source_target_pairs={{0,16},{16,0},{1,17},{17,1},{2,18},{18,2},{3,19},{19,3},{4,20},{20... | collective-permute-start | bytes 1769480 | tf_op jit(solution)/shard_map/ppermute | solution.py:118
  400.0 14.8 %collective-permute-start.37 = (bf16[256,1152]{1,0:T(8,128)(2,1)}, bf16[256,1152]{1,0:T(8,128)(2,1)}, u32[]{:S(2)}, u32[]{:S(2)}) collective-permute-start(bf16[256,1152]{1,0:T(8,128)(2,1)} %add_convert_fusion.4), channel_id=1, source_target_pairs={{0,8},{8,0},{1,9},{9,1},{2,10},{10,2},{3,11},{11,3},{4,12},{12,4},... | collective-permute-start | bytes 1769480 | tf_op jit(solution)/shard_map/ppermute | solution.py:122
  418.1 17.8 %collective-permute-start.40 = (bf16[256,1024]{1,0:T(8,128)(2,1)}, bf16[256,1024]{1,0:T(8,128)(2,1)S(1)}, u32[]{:S(2)}, u32[]{:S(2)}) collective-permute-start(bf16[256,1024]{1,0:T(8,128)(2,1)} %add_convert_fusion.9), channel_id=1, source_target_pairs={{0,16},{16,0},{1,17},{17,1},{2,18},{18,2},{3,19},{19,3},{4,20},{20... | collective-permute-start | bytes 1572872 | tf_op jit(solution)/shard_map/ppermute | solution.py:118
  419.0 16.9 %collective-permute-start.41 = (bf16[256,1024]{1,0:T(8,128)(2,1)}, bf16[256,1024]{1,0:T(8,128)(2,1)S(1)}, u32[]{:S(2)}, u32[]{:S(2)}) collective-permute-start(bf16[256,1024]{1,0:T(8,128)(2,1)} %add_convert_fusion.8), channel_id=1, source_target_pairs={{0,8},{8,0},{1,9},{9,1},{2,10},{10,2},{3,11},{11,3},{4,12},{12,4},... | collective-permute-start | bytes 1572872 | tf_op jit(solution)/shard_map/ppermute | solution.py:122
  421.2 32.4 %collective-permute-start.38 = (bf16[256,2048]{1,0:T(8,128)(2,1)}, bf16[256,2048]{1,0:T(8,128)(2,1)}, u32[]{:S(2)}, u32[]{:S(2)}) collective-permute-start(bf16[256,2048]{1,0:T(8,128)(2,1)} %convert_element_type.293), channel_id=1, source_target_pairs={{0,8},{8,0},{1,9},{9,1},{2,10},{10,2},{3,11},{11,3},{4,12},{12,4},... | collective-permute-start | bytes 3145736 | tf_op jit(solution)/shard_map/ppermute | solution.py:122
  422.0 31.6 %collective-permute-start.39 = (bf16[256,2048]{1,0:T(8,128)(2,1)}, bf16[256,2048]{1,0:T(8,128)(2,1)}, u32[]{:S(2)}, u32[]{:S(2)}) collective-permute-start(bf16[256,2048]{1,0:T(8,128)(2,1)} %convert_element_type.294), channel_id=1, source_target_pairs={{0,16},{16,0},{1,17},{17,1},{2,18},{18,2},{3,19},{19,3},{4,20},{20... | collective-permute-start | bytes 3145736 | tf_op jit(solution)/shard_map/ppermute | solution.py:118
  439.8 47.2 %all-to-all-start.4 = ((bf16[8,64,1024]{2,1,0:T(8,128)(2,1)}), bf16[8,64,1024]{2,1,0:T(8,128)(2,1)}, u32[]{:S(2)}, u32[]{:S(2)}) async-start(bf16[8,64,1024]{2,1,0:T(8,128)(2,1)} %bitcast.224), calls=%async_computation.8 | async-start | bytes 2097152 | tf_op jit(solution)/shard_map/all_to_all | solution.py:440
  445.0 64.3 %reduce-scatter.11.cloned.1.call-start = ((), (), s32[]{:S(2)}) async-start(), calls=%async_computation.12 | async-start | bytes 1310720 | tf_op jit(solution)/shard_map/reduce_scatter | solution.py:130
  462.9 14.4 %collective-permute-start.43 = (bf16[128,2048]{1,0:T(8,128)(2,1)S(1)}, bf16[128,2048]{1,0:T(8,128)(2,1)S(1)}, u32[]{:S(2)}, u32[]{:S(2)}) collective-permute-start(bf16[128,2048]{1,0:T(8,128)(2,1)S(1)} %add_convert_fusion.6), channel_id=1, source_target_pairs={{0,8},{8,0},{1,9},{9,1},{2,10},{10,2},{3,11},{11,3},{4,12},{12,4},... | collective-permute-start | bytes 1572872 | tf_op jit(solution)/shard_map/ppermute | solution.py:122
  487.0 14.9 %all-to-all-start.3 = ((f32[32,1,708]{2,1,0:T(1,128)}), f32[32,1,708]{2,1,0:T(1,128)S(1)}, u32[]{:S(2)}, u32[]{:S(2)}) async-start(f32[32,1,708]{2,1,0:T(1,128)} %all_to_all.22), calls=%async_computation.6 | async-start | bytes 196608 | tf_op jit(solution)/shard_map/all_to_all | solution.py:485
  (107 other events, 931.5 us)
Sparse Core Ops, SparseCore 0:
  15.3 34.2 all-gather.8
  55.6 30.9 all-gather.10
  100.5 56.9 all-gather.12
  186.6 47.4 all-gather.14
  272.2 44.0 reduce-scatter.4
  356.3 44.2 reduce-scatter.6
  418.2 29.6 reduce-scatter.8
  480.0 29.2 reduce-scatter.10

commit v5 on v4

--- a/solution.py
+++ b/solution.py
@@ -58,37 +58,119 @@
     )(a, b)
 
 
+def tile_of(cols, largest):
+    return next((t for t in (512, 384, 256, 128) if t <= largest and cols % t == 0), cols)
+
+
+def against(x, refs):
+    total, at = None, 0
+    for ref in refs:
+        depth = ref.shape[0]
+        part = jnp.dot(x[:, at : at + depth], ref[...], preferred_element_type=F32)
+        total, at = part if total is None else total + part, at + depth
+    return total
+
+
+def cost(count, depth, cols, special=0):
+    return pl.CostEstimate(
+        flops=2 * count * depth * cols, bytes_accessed=2 * (count + cols) * depth, transcendentals=special
+    )
+
+
+def mm_pieces(x, pieces, bias=None, out=F32):
+    count, depth = x.shape
+    cols = pieces[0].shape[1]
+    tile = tile_of(cols, 512)
+    bias = jnp.zeros((cols,), F32) if bias is None else bias
+
+    def kernel(x_ref, b_ref, *refs):
+        refs[-1][...] = (against(x_ref, refs[:-1]) + b_ref[...]).astype(out)
+
+    return pl.pallas_call(
+        kernel,
+        out_shape=jax.ShapeDtypeStruct((count, cols), out),
+        grid=(cols // tile,),
+        in_specs=[pl.BlockSpec((count, depth), lambda j: (0, 0)), pl.BlockSpec((1, tile), lambda j: (0, j))]
+        + [pl.BlockSpec((p.shape[0], tile), lambda j: (0, j)) for p in pieces],
+        out_specs=pl.BlockSpec((count, tile), lambda j: (0, j)),
+        compiler_params=pltpu.CompilerParams(vmem_limit_bytes=24 << 20),
+        cost_estimate=cost(count, depth, cols),
+        name="rows_product",
+    )(x, bias.reshape(1, cols), *pieces)
+
+
+def mm_nt_pieces(x, pieces, out=F32):
+    count, depth = x.shape
+    cols = sum(p.shape[0] for p in pieces)
+
+    def kernel(x_ref, *refs):
+        at = 0
+        for ref in refs[:-1]:
+            part = lax.dot_general(x_ref[...], ref[...], (((1,), (1,)), ((), ())), preferred_element_type=F32)
+            refs[-1][:, at : at + ref.shape[0]] = part.astype(out)
+            at += ref.shape[0]
+
+    return pl.pallas_call(
+        kernel,
+        out_shape=jax.ShapeDtypeStruct((count, cols), out),
+        compiler_params=pltpu.CompilerParams(vmem_limit_bytes=32 << 20),
+        cost_estimate=cost(count, depth, cols),
+        name="columns_product",
+    )(x, *pieces)
+
+
 def hidden(h, w_up, bias, dact):
     count, depth = h.shape
     units = w_up.shape[1]
-    tile = next((t for t in (256, 128) if units % t == 0), units)
+    tile = tile_of(units, 256)
 
     def kernel(h_ref, w_ref, b_ref, d_ref, act_ref, dpre_ref):
-        pre = jnp.dot(h_ref[...], w_ref[...], preferred_element_type=F32) + b_ref[...]
-        square = pre * pre
-        th = jnp.tanh(GELU_K * pre * (1.0 + GELU_C * square))
-        half = 0.5 * (1.0 + th)
-        act_ref[...] = (pre * half).astype(BF)
-        slope = half + 0.5 * GELU_K * pre * (1.0 - th * th) * (1.0 + 3.0 * GELU_C * square)
-        dpre_ref[...] = (d_ref[...] * slope).astype(BF)
-
+        @pl.loop(0, units // tile)
+        def _(step):
+            at = pl.ds(pl.multiple_of(step * tile, tile), tile)
+            pre = jnp.dot(h_ref[...], w_ref[:, at], preferred_element_type=F32) + b_ref[:, at]
+            square = pre * pre
+            th = jnp.tanh(GELU_K * pre * (1.0 + GELU_C * square))
+            half = 0.5 * (1.0 + th)
+            act_ref[:, at] = (pre * half).astype(BF)
+            slope = half + 0.5 * GELU_K * pre * (1.0 - th * th) * (1.0 + 3.0 * GELU_C * square)
+            dpre_ref[:, at] = (d_ref[:, at] * slope).astype(BF)
+
+    near = pl.BlockSpec(memory_space=pltpu.VMEM)
     return pl.pallas_call(
         kernel,
         out_shape=[jax.ShapeDtypeStruct((count, units), BF)] * 2,
-        grid=(units // tile,),
-        in_specs=[
-            pl.BlockSpec((count, depth), lambda j: (0, 0)),
-            pl.BlockSpec((depth, tile), lambda j: (0, j)),
-            pl.BlockSpec((1, tile), lambda j: (0, j)),
-            pl.BlockSpec((count, tile), lambda j: (0, j)),
-        ],
-        out_specs=[pl.BlockSpec((count, tile), lambda j: (0, j))] * 2,
-        compiler_params=pltpu.CompilerParams(vmem_limit_bytes=24 << 20),
-        cost_estimate=pl.CostEstimate(
-            flops=2 * count * depth * units, bytes_accessed=2 * (count + units) * depth, transcendentals=count * units
-        ),
+        in_specs=[near] * 4,
+        out_specs=[near] * 2,
+        compiler_params=pltpu.CompilerParams(vmem_limit_bytes=16 << 20),
+        cost_estimate=cost(count, depth, units, count * units),
         name="hidden",
     )(h, w_up, bias.reshape(1, units), dact)
+
+
+def near_nt(x, w, out):
+    count, depth = x.shape
+    cols = w.shape[0]
+    tile = tile_of(cols, 512)
+
+    def kernel(x_ref, w_ref, o_ref):
+        @pl.loop(0, cols // tile)
+        def _(step):
+            at = pl.ds(pl.multiple_of(step * tile, tile), tile)
+            o_ref[:, at] = lax.dot_general(
+                x_ref[...], w_ref[at, :], (((1,), (1,)), ((), ())), preferred_element_type=F32
+            ).astype(out)
+
+    near = pl.BlockSpec(memory_space=pltpu.VMEM)
+    return pl.pallas_call(
+        kernel,
+        out_shape=jax.ShapeDtypeStruct((count, cols), out),
+        in_specs=[near] * 2,
+        out_specs=near,
+        compiler_params=pltpu.CompilerParams(vmem_limit_bytes=16 << 20),
+        cost_estimate=cost(count, depth, cols),
+        name="near_product",
+    )(x, w)
 
 
 def ln_stats(x):
@@ -285,7 +367,8 @@
             w_out_z = gather(out_in, "ctx").reshape(Z * R, D)
         else:
             w_out = gather(out_in, EVERY).reshape(2, DH, D)
-            w_out = w_out_z = lax.dynamic_index_in_dim(w_out, c, 0, keepdims=False)
+            w_out_z = lax.dynamic_index_in_dim(w_out, c, 0, keepdims=False)
+            w_out = [w_out_z]
         up_cols = [
             jnp.concatenate([up_in[:, (i * C * Z + j) * F0 : (i * C * Z + j + 1) * F0] for i in range(AB)], axis=1)
             for j in range(C * Z)
@@ -322,14 +405,13 @@
             p, pieces, cot_z, down_gather.pieces = lax.optimization_barrier(
                 (p, out_gather.pieces, cot_z, down_gather.pieces)
             )
-            w_out = jnp.concatenate(pieces)
+            w_out = pieces
         pb = p.astype(BF)
         o = jnp.einsum("rhtj,rjd->rthd", pb, v, preferred_element_type=F32)
         o = o.astype(BF).reshape(2 * T, DH)
-        order.mark(w_out, cot_z)
         o_w = order(o)
-        away = swap_core(mm(o_w[T:], w_out))
-        mid = x + bo + mm(o_w[:T], w_out) + away
+        away = swap_core(mm_pieces(o_w[T:], w_out))
+        mid = x + bo + mm_pieces(o_w[:T], w_out) + away
 
         xhat2, rstd2 = ln_stats(mid)
         h2 = turn((xhat2 * g2 + b2).astype(BF), me)
@@ -354,14 +436,15 @@
         w_up = jnp.concatenate(after(up_gather.pieces, dacts))
         order.mark(dacts, w_up)
         h2_z = order(h2_z)
-        h2s = [h2_z, swap_core(h2_z)]
-        acts, dpres = [], []
-        for part, dact in zip(h2s, dacts):
-            act, dpre = hidden(part, w_up, bu, dact)
-            acts.append(act)
-            dpres.append(dpre)
-        away = swap_core(side(dpres[1], w_up, 1, 1, BF))
-        dh2_part, away = lax.optimization_barrier((side(dpres[0], w_up, 1, 1), away))
+        h2_mate = swap_core(h2_z)
+        act, dpre = hidden(h2_z, w_up, bu, dacts[0])
+        h2_mate, act, dpre = lax.optimization_barrier((h2_mate, act, dpre))
+        h2s, acts, dpres = [h2_z, h2_mate], [act], [dpre]
+        act, dpre = hidden(h2_mate, w_up, bu, dacts[1])
+        acts.append(act)
+        dpres.append(dpre)
+        away = swap_core(near_nt(dpres[1], w_up, BF))
+        dh2_part, away = lax.optimization_barrier((near_nt(dpres[0], w_up, F32), away))
         dh2_part = (dh2_part + away.astype(F32)).astype(BF).reshape(Z, T, D)
         order.mark(dh2_part)
         dh2 = turn(scatter(dh2_part, "ctx").astype(F32), me)
@@ -388,7 +471,7 @@
         dmid = cotangent[0].astype(F32) + ln_back(dh2, g2, xhat2, rstd2)
         db = dmid.astype(BF)
         db = jnp.concatenate([db, swap_core(db)])
-        do = mm_nt(db, w_out).astype(BF)
+        do = mm_nt_pieces(db, w_out, BF)
         order.mark(do)
         do_h = order(do).reshape(2, T, HH, HD)
         dp = jnp.einsum("rthd,rjd->rhtj", do_h, v, preferred_element_type=F32)

time: 527 us -> 520 us (0.987)
  waiting for transfers between devices: 139 us -> 128 us
  Pallas kernels: 41.4 us -> 51.3 us
    pallas_call x0 -> x5, Pallas kernels: none -> 18 us  [the longest x2 7.54 us: mm_pieces(): pl.pallas_call(kernel, out_shape=jax.ShapeDtypeStruct((count, cols), out)...]
    ppermute x16, waiting for transfers between devices: 78.7 us -> 69.4 us  [over_b(): return lax.ppermute(x, 'b', MATES)]
    pallas_call x13 -> x11, Pallas kernels: 30.5 us -> 23.2 us  [side(): pl.pallas_call(kernel, out_shape=jax.ShapeDtypeStruct((count, cols), out)...]
    dot_general x19 -> x16, matrix products: 43.2 us -> 38 us  [dot(): return lax.dot_general(a, b, (dims, ((), ())), preferred_element_type=F32)]
    unnamed x226 -> x234, local copies, waits for them, and re-layouts: 52.9 us -> 53.3 us
  transfers between devices with their start and end apart: 58 -> 58, of which waited for: 28 -> 27; matrix products, arithmetic and copies ran while one was open for 30% -> 31% of each run, Pallas kernels for 6% -> 7%
where the time goes in v5:
time: 520 us; the launch traced here: 511 us
  waiting for transfers between devices  128 us (25%)
  local copies, waits for them, and re-layouts  106 us (20%)
  starting transfers between devices  69.7 us (13%)
  other arithmetic  67.6 us (13%)
  Pallas kernels  51.3 us (10%)
  matrix products  47.7 us (9%)
  blocking collectives  24.2 us (5%)
  between operations  16.7 us (3%)
    ppermute x16, waiting for transfers between devices, over_b(): return lax.ppermute(x, 'b', MATES)  69.4 us
    unnamed x234, local copies, waits for them, and re-layouts  53.3 us
    dot_general x16, matrix products, dot(): return lax.dot_general(a, b, (dims, ((), ())), preferred_element_type=F32)  38 us
    all_gather x1, blocking collectives, gather(): return lax.all_gather(x, axes, axis=0, tiled=False)  24.2 us
    pallas_call x11, Pallas kernels, side(): pl.pallas_call(kernel, out_shape=jax.ShapeDtypeStruct((count, cols), out)...  23.2 us
    ppermute x16, starting transfers between devices, over_b(): return lax.ppermute(x, 'b', MATES)  22.2 us
    ppermute x16, starting transfers between devices, over_a(): return lax.ppermute(x, 'a', MATES)  22 us
    ppermute x16, waiting for transfers between devices, over_a(): return lax.ppermute(x, 'a', MATES)  18.2 us
  transfers between devices with their start and end apart: 58, of which 27 were waited for; matrix products, arithmetic and copies ran while one was open for 31% of the time, Pallas kernels for 7%

profile of v5, /device:TPU:0, one launch (start us, length us, event | category | flops | bytes accessed | tf_op | source)
XLA Modules:
  0.0 511.0 jit_solution(11604432708521547751)
XLA Ops:
  16.5 2.9 collective-permute-start.4
  23.3 4.0 all-to-all-start
  27.8 17.3 %all-to-all-done = bf16[32,2,354]{2,1,0:T(2,128)(2,1)S(1)} async-done(((bf16[32,2,354]{2,1,0:T(2,128)(2,1)}), bf16[32,2,354]{2,1,0:T(2,128)(2,1)S(1)}, u32[]{:S(2)}, u32[]{:S(2)}) %all-to-all-start) | async-done | bytes 45344 | tf_op jit(solution)/shard_map/all_to_all | solution.py:345
  46.1 3.5 all-gather.9.cloned.1.call-done
  66.9 4.3 all-to-all-start.1
  73.8 4.8 collective-permute-done.2
  79.9 7.1 %all-gather.11.cloned.1.call-done.refs_0_ = bf16[256,2048]{1,0:T(8,128)(2,1)} async-done(((bf16[64,2048]{1,0:T(8,128)(2,1)}), bf16[256,2048]{1,0:T(8,128)(2,1)}) %all-gather.11.cloned.1.call-update) | async-done | bytes 1048592 | tf_op jit(solution)/shard_map/all_gather | solution.py:208
  89.1 3.0 collective-permute-start.6
  106.6 2.4 collective-permute-start.15
  118.6 24.2 %all_gather.31 = bf16[4,2,128,128]{3,2,1,0:T(8,128)(2,1)S(1)} all-gather(bf16[1,2,128,128]{3,2,1,0:T(8,128)(2,1)S(1)} %bitcast.225), channel_id=1, replica_groups=mesh['a'=2,'b'=2,'core'=2,'ctx'=4] {'ctx'}, dimensions={0}, use_global_device_ids=true | all-gather | bytes 327680 | tf_op jit(solution)/shard_map/all_gather | solution.py:208
  148.4 2.8 fusion.68
  151.2 7.8 %fusion.8 = f32[2,8,128,512]{2,3,1,0:T(8,128)} fusion(f32[2,512,128,8]{2,1,3,0:T(8,128)} %fusion.68, pred[2,128,512]{1,2,0:T(8,128)(4,1)} %compare_and_fusion), kind=kOutput, calls=%fused_computation.23 | output fusion | flops 6296574 | bytes 8519680 | tf_op jit(solution)/shard_map/div | solution.py:403
  160.9 3.5 fusion.22
  168.4 4.2 rows_product.3
  174.9 3.3 rows_product.2
  189.4 18.7 %collective-permute-done.18 = bf16[512,1024]{1,0:T(8,128)(2,1)S(1)} collective-permute-done((bf16[512,1024]{1,0:T(8,128)(2,1)}, bf16[512,1024]{1,0:T(8,128)(2,1)S(1)}, u32[]{:S(2)}, u32[]{:S(2)}) %collective-permute-start.18) | collective-permute-done | bytes 1048608 | tf_op jit(solution)/shard_map/ppermute | solution.py:204
  216.8 2.7 side.11.d_ref
  220.8 4.3 side.12.d_ref
  236.2 3.9 hidden.2
  240.2 6.2 %hidden.3 = (bf16[512,1024]{1,0:T(8,128)(2,1)S(1)}, bf16[512,1024]{1,0:T(8,128)(2,1)S(1)}) custom-call(bf16[512,2048]{1,0:T(8,128)(2,1)} %collective-permute-done.22.h_ref, bf16[2048,1024]{1,0:T(8,128)(2,1)S(1)} %copy-done.8, f32[1,1024]{1,0:T(1,128)S(1)} %bitcast.182, f32[512,1024]{1,0:T(8,128)S(1)} %copy-done.20), custom_call_target="tpu_custom_call" | custom-call | flops 2147483648 | bytes 6291456 | tf_op jit(solution)/shard_map/hidden/pallas_call | solution.py:140
  246.4 4.3 near_product.3
  254.6 3.2 near_product.2
  257.8 3.7 add_convert_fusion.1
  271.4 3.7 convolution_convert_fusion
  277.4 2.8 pad_maximum_fusion
  287.1 13.7 %collective-permute-done.24 = bf16[256,2048]{1,0:T(8,128)(2,1)S(1)} collective-permute-done((bf16[256,2048]{1,0:T(8,128)(2,1)}, bf16[256,2048]{1,0:T(8,128)(2,1)S(1)}, u32[]{:S(2)}, u32[]{:S(2)}) %collective-permute-start.24) | collective-permute-done | bytes 1048608 | tf_op jit(solution)/shard_map/ppermute | solution.py:204
  302.0 2.7 fusion.9
  304.7 2.5 fusion.10
  314.6 3.0 columns_product.1
  320.8 5.3 %collective-permute-done.28 = bf16[128,2048]{1,0:T(8,128)(2,1)S(1)} collective-permute-done((bf16[128,2048]{1,0:T(8,128)(2,1)}, bf16[128,2048]{1,0:T(8,128)(2,1)S(1)}, u32[]{:S(2)}, u32[]{:S(2)}) %collective-permute-start.28) | collective-permute-done | bytes 524320 | tf_op jit(solution)/shard_map/ppermute | solution.py:200
  332.8 4.0 all-to-all-start.2
  339.1 3.4 side.13
  342.5 3.7 add_convert_fusion
  357.5 2.4 side.15
  364.4 3.4 add_convert_fusion.9
  367.8 2.7 add_convert_fusion.8
  378.0 11.9 %collective-permute-done.31 = bf16[512,1152]{1,0:T(8,128)(2,1)S(1)} collective-permute-done((bf16[512,1152]{1,0:T(8,128)(2,1)}, bf16[512,1152]{1,0:T(8,128)(2,1)S(1)}, u32[]{:S(2)}, u32[]{:S(2)}) %collective-permute-start.31) | collective-permute-done | bytes 1179680 | tf_op jit(solution)/shard_map/ppermute | solution.py:204
  408.1 3.5 collective-permute-done.37
  432.7 3.8 add_convert_fusion.3
  436.5 5.2 %all-to-all-start.4 = ((bf16[8,64,1024]{2,1,0:T(8,128)(2,1)}), bf16[8,64,1024]{2,1,0:T(8,128)(2,1)}, u32[]{:S(2)}, u32[]{:S(2)}) async-start(bf16[8,64,1024]{2,1,0:T(8,128)(2,1)} %bitcast.216), calls=%async_computation.8 | async-start | bytes 2097152 | tf_op jit(solution)/shard_map/all_to_all | solution.py:523
  441.7 2.9 add_add_fusion
  444.7 5.4 %collective-permute-done.38 = bf16[256,2048]{1,0:T(8,128)(2,1)} collective-permute-done((bf16[256,2048]{1,0:T(8,128)(2,1)}, bf16[256,2048]{1,0:T(8,128)(2,1)}, u32[]{:S(2)}, u32[]{:S(2)}) %collective-permute-start.38) | collective-permute-done | bytes 1048608 | tf_op jit(solution)/shard_map/ppermute | solution.py:204
  459.9 4.6 collective-permute-done.42
  464.5 7.3 %collective-permute-done.43 = bf16[128,2048]{1,0:T(8,128)(2,1)S(1)} collective-permute-done((bf16[128,2048]{1,0:T(8,128)(2,1)S(1)}, bf16[128,2048]{1,0:T(8,128)(2,1)S(1)}, u32[]{:S(2)}, u32[]{:S(2)}) %collective-permute-start.43) | collective-permute-done | bytes 524320 | tf_op jit(solution)/shard_map/ppermute | solution.py:204
  480.6 4.4 all-to-all-start.3
  488.3 2.5 copy.97
  490.8 3.7 all-to-all-done.3
  496.4 5.5 %reduce-scatter.11.cloned.1.call-done = bf16[1,64,2048]{2,1,0:T(8,128)(2,1)} async-done(((bf16[4,64,2048]{2,1,0:T(8,128)(2,1)}), bf16[1,64,2048]{2,1,0:T(8,128)(2,1)}) %reduce-scatter.11.cloned.1.call-update) | async-done | bytes 262160 | tf_op jit(solution)/shard_map/reduce_scatter | solution.py:212
  (528 shorter events, 238.1 us)
Async XLA Ops:
  7.3 42.3 %all-gather.9.cloned.1.call-start = ((), (), s32[]{:S(2)}) async-start(), calls=%async_computation.13 | async-start | bytes 1474560 | tf_op jit(solution)/shard_map/all_gather | solution.py:208
  16.5 57.3 %collective-permute-start.4 = (bf16[256,2048]{1,0:T(8,128)(2,1)}, bf16[256,2048]{1,0:T(8,128)(2,1)}, u32[]{:S(2)}, u32[]{:S(2)}) collective-permute-start(bf16[256,2048]{1,0:T(8,128)(2,1)} %param.31), channel_id=1, source_target_pairs={{0,8},{8,0},{1,9},{9,1},{2,10},{10,2},{3,11},{11,3},{4,12},{12,4},... | collective-permute-start | bytes 3145736 | tf_op jit(solution)/shard_map/ppermute | solution.py:204
  19.4 54.5 %collective-permute-start.5 = (bf16[256,2048]{1,0:T(8,128)(2,1)}, bf16[256,2048]{1,0:T(8,128)(2,1)}, u32[]{:S(2)}, u32[]{:S(2)}) collective-permute-start(bf16[256,2048]{1,0:T(8,128)(2,1)} %param.31), channel_id=1, source_target_pairs={{0,16},{16,0},{1,17},{17,1},{2,18},{18,2},{3,19},{19,3},{4,20},{20... | collective-permute-start | bytes 3145736 | tf_op jit(solution)/shard_map/ppermute | solution.py:200
  23.3 21.8 %all-to-all-start = ((bf16[32,2,354]{2,1,0:T(2,128)(2,1)}), bf16[32,2,354]{2,1,0:T(2,128)(2,1)S(1)}, u32[]{:S(2)}, u32[]{:S(2)}) async-start(bf16[32,2,354]{2,1,0:T(2,128)(2,1)} %reshape.313), calls=%async_computation | async-start | bytes 98304 | tf_op jit(solution)/shard_map/all_to_all | solution.py:345
  27.3 59.8 %all-gather.11.cloned.1.call-start = ((), (), s32[]{:S(2)}) async-start(), calls=%async_computation.14 | async-start | bytes 1310720 | tf_op jit(solution)/shard_map/all_gather | solution.py:208
  51.0 27.6 %collective-permute-start.2 = (bf16[512,1152]{1,0:T(8,128)(2,1)S(1)}, bf16[512,1152]{1,0:T(8,128)(2,1)S(1)}, u32[]{:S(2)}, u32[]{:S(2)}) collective-permute-start(bf16[512,1152]{1,0:T(8,128)(2,1)S(1)} %bitcast.201), channel_id=1, source_target_pairs={{0,8},{8,0},{1,9},{9,1},{2,10},{10,2},{3,11},{11,3},{4,12},{12,4},... | collective-permute-start | bytes 3538952 | tf_op jit(solution)/shard_map/ppermute | solution.py:204
  52.5 27.4 %collective-permute-start.3 = (bf16[512,1152]{1,0:T(8,128)(2,1)S(1)}, bf16[512,1152]{1,0:T(8,128)(2,1)}, u32[]{:S(2)}, u32[]{:S(2)}) collective-permute-start(bf16[512,1152]{1,0:T(8,128)(2,1)S(1)} %bitcast.202), channel_id=1, source_target_pairs={{0,16},{16,0},{1,17},{17,1},{2,18},{18,2},{3,19},{19,3},{4,20},{20... | collective-permute-start | bytes 3538952 | tf_op jit(solution)/shard_map/ppermute | solution.py:200
  66.9 42.1 %all-to-all-start.1 = ((bf16[8,64,1024]{2,1,0:T(8,128)(2,1)}), bf16[8,64,1024]{2,1,0:T(8,128)(2,1)}, u32[]{:S(2)}, u32[]{:S(2)}) async-start(bf16[8,64,1024]{2,1,0:T(8,128)(2,1)} %fusion.90), calls=%async_computation.1 | async-start | bytes 2097152 | tf_op jit(solution)/shard_map/all_to_all | solution.py:376
  71.2 89.7 %all-gather.13.cloned.1.call-start = ((), (), s32[]{:S(2)}) async-start(), calls=%async_computation.15 | async-start | bytes 2621440 | tf_op jit(solution)/shard_map/all_gather | solution.py:208
  72.6 24.1 %collective-permute-start.1 = (bf16[128,2048]{1,0:T(8,128)(2,1)}, bf16[128,2048]{1,0:T(8,128)(2,1)}, u32[]{:S(2)}, u32[]{:S(2)}) collective-permute-start(bf16[128,2048]{1,0:T(8,128)(2,1)} %pad_maximum_fusion.5), channel_id=1, source_target_pairs={{0,4},{4,0},{1,5},{5,1},{2,6},{6,2},{3,7},{7,3},{8,12},{12,8},{9,1... | collective-permute-start | bytes 1572872 | tf_op jit(solution)/shard_map/ppermute | solution.py:196
  89.1 17.6 %collective-permute-start.6 = (bf16[256,1152]{1,0:T(8,128)(2,1)}, bf16[256,1152]{1,0:T(8,128)(2,1)}, u32[]{:S(2)}, u32[]{:S(2)}) collective-permute-start(bf16[256,1152]{1,0:T(8,128)(2,1)} %slice.475), channel_id=1, source_target_pairs={{0,16},{16,0},{1,17},{17,1},{2,18},{18,2},{3,19},{19,3},{4,20},{20... | collective-permute-start | bytes 1769480 | tf_op jit(solution)/shard_map/ppermute | solution.py:200
  94.0 16.9 %collective-permute-start.7 = (bf16[256,1152]{1,0:T(8,128)(2,1)}, bf16[256,1152]{1,0:T(8,128)(2,1)}, u32[]{:S(2)}, u32[]{:S(2)}) collective-permute-start(bf16[256,1152]{1,0:T(8,128)(2,1)} %slice.476), channel_id=1, source_target_pairs={{0,8},{8,0},{1,9},{9,1},{2,10},{10,2},{3,11},{11,3},{4,12},{12,4},... | collective-permute-start | bytes 1769480 | tf_op jit(solution)/shard_map/ppermute | solution.py:204
  98.9 45.7 %collective-permute-start.10 = (bf16[256,2048]{1,0:T(8,128)(2,1)S(1)}, bf16[256,2048]{1,0:T(8,128)(2,1)S(1)}, u32[]{:S(2)}, u32[]{:S(2)}) collective-permute-start(bf16[256,2048]{1,0:T(8,128)(2,1)S(1)} %copy-done.13), channel_id=1, source_target_pairs={{0,8},{8,0},{1,9},{9,1},{2,10},{10,2},{3,11},{11,3},{4,12},{12,4},... | collective-permute-start | bytes 3145736 | tf_op jit(solution)/shard_map/ppermute | solution.py:204
  98.9 45.7 %collective-permute-start.11 = (bf16[256,2048]{1,0:T(8,128)(2,1)S(1)}, bf16[256,2048]{1,0:T(8,128)(2,1)S(1)}, u32[]{:S(2)}, u32[]{:S(2)}) collective-permute-start(bf16[256,2048]{1,0:T(8,128)(2,1)S(1)} %copy-done.13), channel_id=1, source_target_pairs={{0,16},{16,0},{1,17},{17,1},{2,18},{18,2},{3,19},{19,3},{4,20},{20... | collective-permute-start | bytes 3145736 | tf_op jit(solution)/shard_map/ppermute | solution.py:200
  98.9 131.8 %all-gather.15.cloned.1.call-start = ((), (), s32[]{:S(2)}) async-start(), calls=%async_computation.16 | async-start | bytes 2621440 | tf_op jit(solution)/shard_map/all_gather | solution.py:208
  100.9 58.1 %collective-permute-start.14 = (bf16[128,2048]{1,0:T(8,128)(2,1)}, bf16[128,2048]{1,0:T(8,128)(2,1)}, u32[]{:S(2)}, u32[]{:S(2)}) collective-permute-start(bf16[128,2048]{1,0:T(8,128)(2,1)} %slice.519), channel_id=1, source_target_pairs={{0,16},{16,0},{1,17},{17,1},{2,18},{18,2},{3,19},{19,3},{4,20},{20... | collective-permute-start | bytes 1572872 | tf_op jit(solution)/shard_map/ppermute | solution.py:200
  106.6 52.4 %collective-permute-start.15 = (bf16[128,2048]{1,0:T(8,128)(2,1)}, bf16[128,2048]{1,0:T(8,128)(2,1)}, u32[]{:S(2)}, u32[]{:S(2)}) collective-permute-start(bf16[128,2048]{1,0:T(8,128)(2,1)} %slice.520), channel_id=1, source_target_pairs={{0,8},{8,0},{1,9},{9,1},{2,10},{10,2},{3,11},{11,3},{4,12},{12,4},... | collective-permute-start | bytes 1572872 | tf_op jit(solution)/shard_map/ppermute | solution.py:204
  145.6 14.3 %collective-permute-start.12 = (bf16[128,2048]{1,0:T(8,128)(2,1)}, bf16[128,2048]{1,0:T(8,128)(2,1)}, u32[]{:S(2)}, u32[]{:S(2)}) collective-permute-start(bf16[128,2048]{1,0:T(8,128)(2,1)} %slice.517), channel_id=1, source_target_pairs={{0,16},{16,0},{1,17},{17,1},{2,18},{18,2},{3,19},{19,3},{4,20},{20... | collective-permute-start | bytes 1572872 | tf_op jit(solution)/shard_map/ppermute | solution.py:200
  146.9 14.0 %collective-permute-start.13 = (bf16[128,2048]{1,0:T(8,128)(2,1)}, bf16[128,2048]{1,0:T(8,128)(2,1)}, u32[]{:S(2)}, u32[]{:S(2)}) collective-permute-start(bf16[128,2048]{1,0:T(8,128)(2,1)} %slice.518), channel_id=1, source_target_pairs={{0,8},{8,0},{1,9},{9,1},{2,10},{10,2},{3,11},{11,3},{4,12},{12,4},... | collective-permute-start | bytes 1572872 | tf_op jit(solution)/shard_map/ppermute | solution.py:204
  181.6 125.5 %reduce-scatter.5.cloned.1.call-start = ((), (), s32[]{:S(2)}) async-start(), calls=%async_computation.9 | async-start | bytes 2621440 | tf_op jit(solution)/shard_map/reduce_scatter | solution.py:212
  182.3 38.6 %collective-permute-start.17 = (bf16[512,2048]{1,0:T(8,128)(2,1)}, bf16[512,2048]{1,0:T(8,128)(2,1)}, u32[]{:S(2)}, u32[]{:S(2)}) collective-permute-start(bf16[512,2048]{1,0:T(8,128)(2,1)} %all-gather.13.cloned.1.call-done.a_ref), channel_id=1, source_target_pairs={{0,4},{4,0},{1,5},{5,1},{2,6},{6,2},{3,7},{7,3},{8,12},{12,8},{9,1... | collective-permute-start | bytes 6291464 | tf_op jit(solution)/shard_map/ppermute | solution.py:196
  182.8 25.4 %collective-permute-start.18 = (bf16[512,1024]{1,0:T(8,128)(2,1)}, bf16[512,1024]{1,0:T(8,128)(2,1)S(1)}, u32[]{:S(2)}, u32[]{:S(2)}) collective-permute-start(bf16[512,1024]{1,0:T(8,128)(2,1)} %bitcast.26), channel_id=1, source_target_pairs={{0,8},{8,0},{1,9},{9,1},{2,10},{10,2},{3,11},{11,3},{4,12},{12,4},... | collective-permute-start | bytes 3145736 | tf_op jit(solution)/shard_map/ppermute | solution.py:204
  184.5 25.2 %collective-permute-start.19 = (bf16[512,1024]{1,0:T(8,128)(2,1)}, bf16[512,1024]{1,0:T(8,128)(2,1)}, u32[]{:S(2)}, u32[]{:S(2)}) collective-permute-start(bf16[512,1024]{1,0:T(8,128)(2,1)} %bitcast.26), channel_id=1, source_target_pairs={{0,16},{16,0},{1,17},{17,1},{2,18},{18,2},{3,19},{19,3},{4,20},{20... | collective-permute-start | bytes 3145736 | tf_op jit(solution)/shard_map/ppermute | solution.py:200
  209.8 15.4 %collective-permute-start.20 = (bf16[256,1024]{1,0:T(8,128)(2,1)S(1)}, bf16[256,1024]{1,0:T(8,128)(2,1)S(1)}, u32[]{:S(2)}, u32[]{:S(2)}) collective-permute-start(bf16[256,1024]{1,0:T(8,128)(2,1)S(1)} %slice.530), channel_id=1, source_target_pairs={{0,16},{16,0},{1,17},{17,1},{2,18},{18,2},{3,19},{19,3},{4,20},{20... | collective-permute-start | bytes 1572872 | tf_op jit(solution)/shard_map/ppermute | solution.py:200
  212.6 12.5 %collective-permute-start.21 = (bf16[256,1024]{1,0:T(8,128)(2,1)S(1)}, bf16[256,1024]{1,0:T(8,128)(2,1)S(1)}, u32[]{:S(2)}, u32[]{:S(2)}) collective-permute-start(bf16[256,1024]{1,0:T(8,128)(2,1)S(1)} %slice.531), channel_id=1, source_target_pairs={{0,8},{8,0},{1,9},{9,1},{2,10},{10,2},{3,11},{11,3},{4,12},{12,4},... | collective-permute-start | bytes 1572872 | tf_op jit(solution)/shard_map/ppermute | solution.py:204
  275.0 26.9 %collective-permute-start.26 = (bf16[512,2048]{1,0:T(8,128)(2,1)}, bf16[512,2048]{1,0:T(8,128)(2,1)}, u32[]{:S(2)}, u32[]{:S(2)}) collective-permute-start(bf16[512,2048]{1,0:T(8,128)(2,1)} %convolution_convert_fusion), channel_id=1, source_target_pairs={{0,4},{4,0},{1,5},{5,1},{2,6},{6,2},{3,7},{7,3},{8,12},{12,8},{9,1... | collective-permute-start | bytes 6291464 | tf_op jit(solution)/shard_map/ppermute | solution.py:196
  275.2 25.7 %collective-permute-start.24 = (bf16[256,2048]{1,0:T(8,128)(2,1)}, bf16[256,2048]{1,0:T(8,128)(2,1)S(1)}, u32[]{:S(2)}, u32[]{:S(2)}) collective-permute-start(bf16[256,2048]{1,0:T(8,128)(2,1)} %convolution_convert_fusion.4), channel_id=1, source_target_pairs={{0,8},{8,0},{1,9},{9,1},{2,10},{10,2},{3,11},{11,3},{4,12},{12,4},... | collective-permute-start | bytes 3145736 | tf_op jit(solution)/shard_map/ppermute | solution.py:204
  276.7 25.2 %collective-permute-start.25 = (bf16[256,2048]{1,0:T(8,128)(2,1)S(1)}, bf16[256,2048]{1,0:T(8,128)(2,1)S(1)}, u32[]{:S(2)}, u32[]{:S(2)}) collective-permute-start(bf16[256,2048]{1,0:T(8,128)(2,1)S(1)} %convolution_convert_fusion.3), channel_id=1, source_target_pairs={{0,16},{16,0},{1,17},{17,1},{2,18},{18,2},{3,19},{19,3},{4,20},{20... | collective-permute-start | bytes 3145736 | tf_op jit(solution)/shard_map/ppermute | solution.py:200
  311.6 14.5 %collective-permute-start.28 = (bf16[128,2048]{1,0:T(8,128)(2,1)}, bf16[128,2048]{1,0:T(8,128)(2,1)S(1)}, u32[]{:S(2)}, u32[]{:S(2)}) collective-permute-start(bf16[128,2048]{1,0:T(8,128)(2,1)} %fusion.9), channel_id=1, source_target_pairs={{0,16},{16,0},{1,17},{17,1},{2,18},{18,2},{3,19},{19,3},{4,20},{20... | collective-permute-start | bytes 1572872 | tf_op jit(solution)/shard_map/ppermute | solution.py:200
  313.0 14.2 %collective-permute-start.29 = (bf16[128,2048]{1,0:T(8,128)(2,1)}, bf16[128,2048]{1,0:T(8,128)(2,1)S(1)}, u32[]{:S(2)}, u32[]{:S(2)}) collective-permute-start(bf16[128,2048]{1,0:T(8,128)(2,1)} %fusion.10), channel_id=1, source_target_pairs={{0,8},{8,0},{1,9},{9,1},{2,10},{10,2},{3,11},{11,3},{4,12},{12,4},... | collective-permute-start | bytes 1572872 | tf_op jit(solution)/shard_map/ppermute | solution.py:204
  330.0 34.4 %collective-permute-start.33 = (bf16[512,1024]{1,0:T(8,128)(2,1)}, bf16[512,1024]{1,0:T(8,128)(2,1)}, u32[]{:S(2)}, u32[]{:S(2)}) collective-permute-start(bf16[512,1024]{1,0:T(8,128)(2,1)} %convolution_convert_fusion.6), channel_id=1, source_target_pairs={{0,8},{8,0},{1,9},{9,1},{2,10},{10,2},{3,11},{11,3},{4,12},{12,4},... | collective-permute-start | bytes 3145736 | tf_op jit(solution)/shard_map/ppermute | solution.py:204
  331.4 33.0 %collective-permute-start.34 = (bf16[512,1024]{1,0:T(8,128)(2,1)}, bf16[512,1024]{1,0:T(8,128)(2,1)}, u32[]{:S(2)}, u32[]{:S(2)}) collective-permute-start(bf16[512,1024]{1,0:T(8,128)(2,1)} %convolution_convert_fusion.5), channel_id=1, source_target_pairs={{0,16},{16,0},{1,17},{17,1},{2,18},{18,2},{3,19},{19,3},{4,20},{20... | collective-permute-start | bytes 3145736 | tf_op jit(solution)/shard_map/ppermute | solution.py:200
  332.8 18.2 %all-to-all-start.2 = ((bf16[4,2,128,128]{3,2,1,0:T(8,128)(2,1)}), bf16[4,2,128,128]{3,2,1,0:T(8,128)(2,1)}, u32[]{:S(2)}, u32[]{:S(2)}) async-start(bf16[4,2,128,128]{3,2,1,0:T(8,128)(2,1)} %bitcast.178), calls=%async_computation.3 | async-start | bytes 524288 | tf_op jit(solution)/shard_map/all_to_all | solution.py:487
  336.8 68.4 %reduce-scatter.7.cloned.1.call-start = ((), (), s32[]{:S(2)}) async-start(), calls=%async_computation.10 | async-start | bytes 2621440 | tf_op jit(solution)/shard_map/reduce_scatter | solution.py:212
  346.3 108.8 %reduce-scatter.9.cloned.1.call-start = ((), (), s32[]{:S(2)}) async-start(), calls=%async_computation.11 | async-start | bytes 1474560 | tf_op jit(solution)/shard_map/reduce_scatter | solution.py:212
  360.0 15.1 %collective-permute-start.35 = (f32[128,2048]{1,0:T(8,128)S(1)}, f32[128,2048]{1,0:T(8,128)}, u32[]{:S(2)}, u32[]{:S(2)}) collective-permute-start(f32[128,2048]{1,0:T(8,128)S(1)} %side.15), channel_id=1, source_target_pairs={{0,4},{4,0},{1,5},{5,1},{2,6},{6,2},{3,7},{7,3},{8,12},{12,8},{9,1... | collective-permute-start | bytes 3145736 | tf_op jit(solution)/shard_map/ppermute | solution.py:196
  361.2 28.6 %collective-permute-start.31 = (bf16[512,1152]{1,0:T(8,128)(2,1)}, bf16[512,1152]{1,0:T(8,128)(2,1)S(1)}, u32[]{:S(2)}, u32[]{:S(2)}) collective-permute-start(bf16[512,1152]{1,0:T(8,128)(2,1)} %convolution_convert_fusion.2), channel_id=1, source_target_pairs={{0,8},{8,0},{1,9},{9,1},{2,10},{10,2},{3,11},{11,3},{4,12},{12,4},... | collective-permute-start | bytes 3538952 | tf_op jit(solution)/shard_map/ppermute | solution.py:204
  362.7 28.3 %collective-permute-start.32 = (bf16[512,1152]{1,0:T(8,128)(2,1)}, bf16[512,1152]{1,0:T(8,128)(2,1)S(1)}, u32[]{:S(2)}, u32[]{:S(2)}) collective-permute-start(bf16[512,1152]{1,0:T(8,128)(2,1)} %convolution_convert_fusion.1), channel_id=1, source_target_pairs={{0,16},{16,0},{1,17},{17,1},{2,18},{18,2},{3,19},{19,3},{4,20},{20... | collective-permute-start | bytes 3538952 | tf_op jit(solution)/shard_map/ppermute | solution.py:200
  393.1 15.0 %collective-permute-start.36 = (bf16[256,1152]{1,0:T(8,128)(2,1)}, bf16[256,1152]{1,0:T(8,128)(2,1)}, u32[]{:S(2)}, u32[]{:S(2)}) collective-permute-start(bf16[256,1152]{1,0:T(8,128)(2,1)} %add_convert_fusion.5), channel_id=1, source_target_pairs={{0,16},{16,0},{1,17},{17,1},{2,18},{18,2},{3,19},{19,3},{4,20},{20... | collective-permute-start | bytes 1769480 | tf_op jit(solution)/shard_map/ppermute | solution.py:200
  396.9 14.7 %collective-permute-start.37 = (bf16[256,1152]{1,0:T(8,128)(2,1)}, bf16[256,1152]{1,0:T(8,128)(2,1)}, u32[]{:S(2)}, u32[]{:S(2)}) collective-permute-start(bf16[256,1152]{1,0:T(8,128)(2,1)} %add_convert_fusion.4), channel_id=1, source_target_pairs={{0,8},{8,0},{1,9},{9,1},{2,10},{10,2},{3,11},{11,3},{4,12},{12,4},... | collective-permute-start | bytes 1769480 | tf_op jit(solution)/shard_map/ppermute | solution.py:204
  415.0 17.6 %collective-permute-start.40 = (bf16[256,1024]{1,0:T(8,128)(2,1)}, bf16[256,1024]{1,0:T(8,128)(2,1)S(1)}, u32[]{:S(2)}, u32[]{:S(2)}) collective-permute-start(bf16[256,1024]{1,0:T(8,128)(2,1)} %add_convert_fusion.9), channel_id=1, source_target_pairs={{0,16},{16,0},{1,17},{17,1},{2,18},{18,2},{3,19},{19,3},{4,20},{20... | collective-permute-start | bytes 1572872 | tf_op jit(solution)/shard_map/ppermute | solution.py:200
  415.4 17.2 %collective-permute-start.41 = (bf16[256,1024]{1,0:T(8,128)(2,1)}, bf16[256,1024]{1,0:T(8,128)(2,1)S(1)}, u32[]{:S(2)}, u32[]{:S(2)}) collective-permute-start(bf16[256,1024]{1,0:T(8,128)(2,1)} %add_convert_fusion.8), channel_id=1, source_target_pairs={{0,8},{8,0},{1,9},{9,1},{2,10},{10,2},{3,11},{11,3},{4,12},{12,4},... | collective-permute-start | bytes 1572872 | tf_op jit(solution)/shard_map/ppermute | solution.py:204
  416.9 33.2 %collective-permute-start.38 = (bf16[256,2048]{1,0:T(8,128)(2,1)}, bf16[256,2048]{1,0:T(8,128)(2,1)}, u32[]{:S(2)}, u32[]{:S(2)}) collective-permute-start(bf16[256,2048]{1,0:T(8,128)(2,1)} %convert_element_type.289), channel_id=1, source_target_pairs={{0,8},{8,0},{1,9},{9,1},{2,10},{10,2},{3,11},{11,3},{4,12},{12,4},... | collective-permute-start | bytes 3145736 | tf_op jit(solution)/shard_map/ppermute | solution.py:204
  418.4 31.6 %collective-permute-start.39 = (bf16[256,2048]{1,0:T(8,128)(2,1)}, bf16[256,2048]{1,0:T(8,128)(2,1)}, u32[]{:S(2)}, u32[]{:S(2)}) collective-permute-start(bf16[256,2048]{1,0:T(8,128)(2,1)} %convert_element_type.290), channel_id=1, source_target_pairs={{0,16},{16,0},{1,17},{17,1},{2,18},{18,2},{3,19},{19,3},{4,20},{20... | collective-permute-start | bytes 3145736 | tf_op jit(solution)/shard_map/ppermute | solution.py:200
  436.5 44.1 %all-to-all-start.4 = ((bf16[8,64,1024]{2,1,0:T(8,128)(2,1)}), bf16[8,64,1024]{2,1,0:T(8,128)(2,1)}, u32[]{:S(2)}, u32[]{:S(2)}) async-start(bf16[8,64,1024]{2,1,0:T(8,128)(2,1)} %bitcast.216), calls=%async_computation.8 | async-start | bytes 2097152 | tf_op jit(solution)/shard_map/all_to_all | solution.py:523
  441.7 60.2 %reduce-scatter.11.cloned.1.call-start = ((), (), s32[]{:S(2)}) async-start(), calls=%async_computation.12 | async-start | bytes 1310720 | tf_op jit(solution)/shard_map/reduce_scatter | solution.py:212
  457.6 14.3 %collective-permute-start.43 = (bf16[128,2048]{1,0:T(8,128)(2,1)S(1)}, bf16[128,2048]{1,0:T(8,128)(2,1)S(1)}, u32[]{:S(2)}, u32[]{:S(2)}) collective-permute-start(bf16[128,2048]{1,0:T(8,128)(2,1)S(1)} %add_convert_fusion.6), channel_id=1, source_target_pairs={{0,8},{8,0},{1,9},{9,1},{2,10},{10,2},{3,11},{11,3},{4,12},{12,4},... | collective-permute-start | bytes 1572872 | tf_op jit(solution)/shard_map/ppermute | solution.py:204
  480.6 13.9 %all-to-all-start.3 = ((f32[32,1,708]{2,1,0:T(1,128)}), f32[32,1,708]{2,1,0:T(1,128)S(1)}, u32[]{:S(2)}, u32[]{:S(2)}) async-start(f32[32,1,708]{2,1,0:T(1,128)} %all_to_all.22), calls=%async_computation.6 | async-start | bytes 196608 | tf_op jit(solution)/shard_map/all_to_all | solution.py:568
  (113 other events, 962.4 us)
Sparse Core Ops, SparseCore 0:
  15.3 34.2 all-gather.8
  57.6 29.4 all-gather.10
  99.1 59.8 all-gather.12
  181.7 48.1 all-gather.14
  261.6 45.3 reduce-scatter.4
  346.4 45.4 reduce-scatter.6
  415.1 28.7 reduce-scatter.8
  473.5 28.3 reduce-scatter.10

commit v6 on v5

--- a/solution.py
+++ b/solution.py
@@ -384,7 +384,7 @@
         if aligned:
             out_gather = ChipGather(w_out_z, square)
         cot_z = gather(after(cotangent[0], w_out_z), "ctx").reshape(Z * T, D)
-        q_ext = (mm(h1, w_ext) + b_ext).astype(BF)
+        q_ext = mm_pieces(h1, ext_gather.pieces, b_ext, BF)
         kv = gather(q_ext[:, DH:].reshape(2, T, HD), "ctx").transpose(1, 0, 2, 3).reshape(2, S, HD)
         q = q_ext[:, :DH]
         if aligned:
@@ -501,9 +501,12 @@
         ext_sum = ChipSum(product(h1, dq_ext), square, AB)
         order.mark(ext_sum.sent)
 
-        dq_w = order(dq_ext)
-        dh1_away = swap_core(side(dq_w[T:], w_ext, 1, 1))
-        dh1 = turn(side(dq_w[:T], w_ext, 1, 1) + dh1_away, me)
+        if square:
+            up_sum.near, dq_w = lax.optimization_barrier((up_sum.near, dq_ext))
+        else:
+            dq_w = dq_ext
+        dh1 = side(dq_w, w_ext, 1, 1)
+        dh1 = turn(dh1[:T] + swap_core(dh1[T:]), me)
         up_sum.pass_on(order)
         order.mark(up_sum.sent, dh1)
         ext_sum.pass_on(order)

time: 520 us -> 518 us (level)
  waiting for transfers between devices: 128 us -> 140 us
  matrix products: 47.7 us -> 42.3 us
    ppermute x16, waiting for transfers between devices: 69.4 us -> 79.5 us  [over_b(): return lax.ppermute(x, 'b', MATES)]
    dot_general x16 -> x15, matrix products: 38 us -> 31.6 us  [dot(): return lax.dot_general(a, b, (dims, ((), ())), preferred_element_type=F32)]
    pallas_call x2 -> x3, Pallas kernels: 7.54 us -> 11.2 us  [mm_pieces(): pl.pallas_call(kernel, out_shape=jax.ShapeDtypeStruct((count, cols), out)...]
    pallas_call x11 -> x10, Pallas kernels: 23.2 us -> 20.9 us  [side(): pl.pallas_call(kernel, out_shape=jax.ShapeDtypeStruct((count, cols), out)...]
  transfers between devices with their start and end apart: 58 -> 58, of which waited for: 27 -> 29; matrix products, arithmetic and copies ran while one was open for 31% -> 29% of each run, Pallas kernels for 7% -> 7%
where the time goes in v6:
time: 518 us; the launch traced here: 509 us
  waiting for transfers between devices  140 us (27%)
  local copies, waits for them, and re-layouts  101 us (19%)
  other arithmetic  66.2 us (13%)
  starting transfers between devices  65.9 us (13%)
  Pallas kernels  52.7 us (10%)
  matrix products  42.3 us (8%)
  blocking collectives  24.2 us (5%)
  between operations  16.6 us (3%)
    ppermute x16, waiting for transfers between devices, over_b(): return lax.ppermute(x, 'b', MATES)  79.5 us
    unnamed x234, local copies, waits for them, and re-layouts  50.2 us
    dot_general x15, matrix products, dot(): return lax.dot_general(a, b, (dims, ((), ())), preferred_element_type=F32)  31.6 us
    all_gather x1, blocking collectives, gather(): return lax.all_gather(x, axes, axis=0, tiled=False)  24.2 us
    ppermute x16, starting transfers between devices, over_a(): return lax.ppermute(x, 'a', MATES)  22 us
    pallas_call x10, Pallas kernels, side(): pl.pallas_call(kernel, out_shape=jax.ShapeDtypeStruct((count, cols), out)...  20.9 us
    ppermute x16, starting transfers between devices, over_b(): return lax.ppermute(x, 'b', MATES)  19.2 us
    ppermute x16, waiting for transfers between devices, over_a(): return lax.ppermute(x, 'a', MATES)  18.1 us
  transfers between devices with their start and end apart: 58, of which 29 were waited for; matrix products, arithmetic and copies ran while one was open for 29% of the time, Pallas kernels for 7%

profile of v6, /device:TPU:0, one launch (start us, length us, event | category | flops | bytes accessed | tf_op | source)
XLA Modules:
  0.0 509.1 jit_solution(14045875798733773663)
XLA Ops:
  16.5 2.9 collective-permute-start.4
  23.3 4.0 all-to-all-start
  27.8 17.3 %all-to-all-done = bf16[32,2,354]{2,1,0:T(2,128)(2,1)S(1)} async-done(((bf16[32,2,354]{2,1,0:T(2,128)(2,1)}), bf16[32,2,354]{2,1,0:T(2,128)(2,1)S(1)}, u32[]{:S(2)}, u32[]{:S(2)}) %all-to-all-start) | async-done | bytes 45344 | tf_op jit(solution)/shard_map/all_to_all | solution.py:345
  46.1 3.5 all-gather.9.cloned.1.call-done
  66.8 4.2 all-to-all-start.1
  73.6 5.0 collective-permute-done.2.refs_1_
  79.9 7.2 %all-gather.11.cloned.1.call-done.refs_0_ = bf16[256,2048]{1,0:T(8,128)(2,1)} async-done(((bf16[64,2048]{1,0:T(8,128)(2,1)}), bf16[256,2048]{1,0:T(8,128)(2,1)}) %all-gather.11.cloned.1.call-update) | async-done | bytes 1048592 | tf_op jit(solution)/shard_map/all_gather | solution.py:208
  88.0 3.0 collective-permute-start.6
  116.1 4.0 rows_product.3
  120.1 24.2 %all_gather.31 = bf16[4,2,128,128]{3,2,1,0:T(8,128)(2,1)S(1)} all-gather(bf16[1,2,128,128]{3,2,1,0:T(8,128)(2,1)S(1)} %bitcast.224), channel_id=1, replica_groups=mesh['a'=2,'b'=2,'core'=2,'ctx'=4] {'ctx'}, dimensions={0}, use_global_device_ids=true | all-gather | bytes 327680 | tf_op jit(solution)/shard_map/all_gather | solution.py:208
  149.9 2.8 fusion.63
  152.7 7.8 %fusion.7 = f32[2,8,128,512]{2,3,1,0:T(8,128)} fusion(f32[2,512,128,8]{2,1,3,0:T(8,128)} %fusion.63, pred[2,128,512]{1,2,0:T(8,128)(4,1)} %compare_and_fusion), kind=kOutput, calls=%fused_computation.21 | output fusion | flops 6296574 | bytes 8519680 | tf_op jit(solution)/shard_map/div | solution.py:403
  163.1 3.7 fusion.23
  170.8 4.0 rows_product.5
  177.8 3.2 rows_product.4
  191.3 19.5 %collective-permute-done.18 = bf16[512,1024]{1,0:T(8,128)(2,1)S(1)} collective-permute-done((bf16[512,1024]{1,0:T(8,128)(2,1)}, bf16[512,1024]{1,0:T(8,128)(2,1)S(1)}, u32[]{:S(2)}, u32[]{:S(2)}) %collective-permute-start.18) | collective-permute-done | bytes 1048608 | tf_op jit(solution)/shard_map/ppermute | solution.py:204
  218.7 2.7 side.10.d_ref
  222.8 4.3 side.11.d_ref
  238.2 3.9 hidden.2
  242.1 6.2 %hidden.3 = (bf16[512,1024]{1,0:T(8,128)(2,1)S(1)}, bf16[512,1024]{1,0:T(8,128)(2,1)S(1)}) custom-call(bf16[512,2048]{1,0:T(8,128)(2,1)} %collective-permute-done.22.h_ref, bf16[2048,1024]{1,0:T(8,128)(2,1)S(1)} %copy-done.8, f32[1,1024]{1,0:T(1,128)S(1)} %bitcast.184, f32[512,1024]{1,0:T(8,128)S(1)} %copy-done.17), custom_call_target="tpu_custom_call" | custom-call | flops 2147483648 | bytes 6291456 | tf_op jit(solution)/shard_map/hidden/pallas_call | solution.py:140
  248.3 4.3 near_product.3
  256.6 3.1 near_product.2
  259.8 3.7 add_convert_fusion.1
  273.3 3.7 convolution_convert_fusion
  278.8 2.8 pad_maximum_fusion
  288.4 14.4 %collective-permute-done.24 = bf16[256,2048]{1,0:T(8,128)(2,1)S(1)} collective-permute-done((bf16[256,2048]{1,0:T(8,128)(2,1)}, bf16[256,2048]{1,0:T(8,128)(2,1)S(1)}, u32[]{:S(2)}, u32[]{:S(2)}) %collective-permute-start.24) | collective-permute-done | bytes 1048608 | tf_op jit(solution)/shard_map/ppermute | solution.py:204
  303.8 2.7 fusion.8
  306.5 2.5 fusion.9
  317.1 3.0 columns_product.1
  323.3 5.6 %collective-permute-done.28 = bf16[128,2048]{1,0:T(8,128)(2,1)S(1)} collective-permute-done((bf16[128,2048]{1,0:T(8,128)(2,1)}, bf16[128,2048]{1,0:T(8,128)(2,1)S(1)}, u32[]{:S(2)}, u32[]{:S(2)}) %collective-permute-start.28) | collective-permute-done | bytes 524320 | tf_op jit(solution)/shard_map/ppermute | solution.py:200
  334.0 4.5 all-to-all-start.2
  340.7 3.4 side.12
  344.2 3.7 add_convert_fusion
  351.7 5.0 collective-permute-done.33
  366.9 2.7 fusion.15
  369.7 2.7 fusion.16
  374.2 17.1 %collective-permute-done.31 = bf16[512,1152]{1,0:T(8,128)(2,1)S(1)} collective-permute-done((bf16[512,1152]{1,0:T(8,128)(2,1)S(1)}, bf16[512,1152]{1,0:T(8,128)(2,1)S(1)}, u32[]{:S(2)}, u32[]{:S(2)}) %collective-permute-start.31) | collective-permute-done | bytes 1179680 | tf_op jit(solution)/shard_map/ppermute | solution.py:204
  408.0 2.6 collective-permute-done.37
  432.1 3.5 add_convert_fusion.3
  435.7 4.6 all-to-all-start.4
  440.6 3.1 add_add_fusion
  443.7 4.4 collective-permute-done.38
  458.6 4.2 collective-permute-done.42
  462.8 7.8 %collective-permute-done.43 = bf16[128,2048]{1,0:T(8,128)(2,1)S(1)} collective-permute-done((bf16[128,2048]{1,0:T(8,128)(2,1)S(1)}, bf16[128,2048]{1,0:T(8,128)(2,1)S(1)}, u32[]{:S(2)}, u32[]{:S(2)}) %collective-permute-start.43) | collective-permute-done | bytes 524320 | tf_op jit(solution)/shard_map/ppermute | solution.py:204
  477.7 3.6 all-to-all-start.3
  484.5 2.5 copy.97
  487.0 3.7 all-to-all-done.3
  492.6 7.5 %reduce-scatter.11.cloned.1.call-done = bf16[1,64,2048]{2,1,0:T(8,128)(2,1)} async-done(((bf16[4,64,2048]{2,1,0:T(8,128)(2,1)}), bf16[1,64,2048]{2,1,0:T(8,128)(2,1)}) %reduce-scatter.11.cloned.1.call-update) | async-done | bytes 262160 | tf_op jit(solution)/shard_map/reduce_scatter | solution.py:212
  (527 shorter events, 226.9 us)
Async XLA Ops:
  7.3 42.3 %all-gather.9.cloned.1.call-start = ((), (), s32[]{:S(2)}) async-start(), calls=%async_computation.13 | async-start | bytes 1474560 | tf_op jit(solution)/shard_map/all_gather | solution.py:208
  16.5 57.1 %collective-permute-start.4 = (bf16[256,2048]{1,0:T(8,128)(2,1)}, bf16[256,2048]{1,0:T(8,128)(2,1)}, u32[]{:S(2)}, u32[]{:S(2)}) collective-permute-start(bf16[256,2048]{1,0:T(8,128)(2,1)} %param.31), channel_id=1, source_target_pairs={{0,8},{8,0},{1,9},{9,1},{2,10},{10,2},{3,11},{11,3},{4,12},{12,4},... | collective-permute-start | bytes 3145736 | tf_op jit(solution)/shard_map/ppermute | solution.py:204
  19.4 54.3 %collective-permute-start.5 = (bf16[256,2048]{1,0:T(8,128)(2,1)}, bf16[256,2048]{1,0:T(8,128)(2,1)}, u32[]{:S(2)}, u32[]{:S(2)}) collective-permute-start(bf16[256,2048]{1,0:T(8,128)(2,1)} %param.31), channel_id=1, source_target_pairs={{0,16},{16,0},{1,17},{17,1},{2,18},{18,2},{3,19},{19,3},{4,20},{20... | collective-permute-start | bytes 3145736 | tf_op jit(solution)/shard_map/ppermute | solution.py:200
  23.3 21.8 %all-to-all-start = ((bf16[32,2,354]{2,1,0:T(2,128)(2,1)}), bf16[32,2,354]{2,1,0:T(2,128)(2,1)S(1)}, u32[]{:S(2)}, u32[]{:S(2)}) async-start(bf16[32,2,354]{2,1,0:T(2,128)(2,1)} %reshape.316), calls=%async_computation | async-start | bytes 98304 | tf_op jit(solution)/shard_map/all_to_all | solution.py:345
  27.3 59.9 %all-gather.11.cloned.1.call-start = ((), (), s32[]{:S(2)}) async-start(), calls=%async_computation.14 | async-start | bytes 1310720 | tf_op jit(solution)/shard_map/all_gather | solution.py:208
  51.0 27.6 %collective-permute-start.2 = (bf16[512,1152]{1,0:T(8,128)(2,1)S(1)}, bf16[512,1152]{1,0:T(8,128)(2,1)S(1)}, u32[]{:S(2)}, u32[]{:S(2)}) collective-permute-start(bf16[512,1152]{1,0:T(8,128)(2,1)S(1)} %bitcast.178), channel_id=1, source_target_pairs={{0,8},{8,0},{1,9},{9,1},{2,10},{10,2},{3,11},{11,3},{4,12},{12,4},... | collective-permute-start | bytes 3538952 | tf_op jit(solution)/shard_map/ppermute | solution.py:204
  52.5 27.4 %collective-permute-start.3 = (bf16[512,1152]{1,0:T(8,128)(2,1)S(1)}, bf16[512,1152]{1,0:T(8,128)(2,1)}, u32[]{:S(2)}, u32[]{:S(2)}) collective-permute-start(bf16[512,1152]{1,0:T(8,128)(2,1)S(1)} %bitcast.179), channel_id=1, source_target_pairs={{0,16},{16,0},{1,17},{17,1},{2,18},{18,2},{3,19},{19,3},{4,20},{20... | collective-permute-start | bytes 3538952 | tf_op jit(solution)/shard_map/ppermute | solution.py:200
  66.8 41.1 %all-to-all-start.1 = ((bf16[8,64,1024]{2,1,0:T(8,128)(2,1)}), bf16[8,64,1024]{2,1,0:T(8,128)(2,1)}, u32[]{:S(2)}, u32[]{:S(2)}) async-start(bf16[8,64,1024]{2,1,0:T(8,128)(2,1)} %fusion.85), calls=%async_computation.1 | async-start | bytes 2097152 | tf_op jit(solution)/shard_map/all_to_all | solution.py:376
  71.0 92.0 %all-gather.13.cloned.1.call-start = ((), (), s32[]{:S(2)}) async-start(), calls=%async_computation.15 | async-start | bytes 2621440 | tf_op jit(solution)/shard_map/all_gather | solution.py:208
  72.4 23.1 %collective-permute-start.1 = (bf16[128,2048]{1,0:T(8,128)(2,1)}, bf16[128,2048]{1,0:T(8,128)(2,1)}, u32[]{:S(2)}, u32[]{:S(2)}) collective-permute-start(bf16[128,2048]{1,0:T(8,128)(2,1)} %pad_maximum_fusion.5), channel_id=1, source_target_pairs={{0,4},{4,0},{1,5},{5,1},{2,6},{6,2},{3,7},{7,3},{8,12},{12,8},{9,1... | collective-permute-start | bytes 1572872 | tf_op jit(solution)/shard_map/ppermute | solution.py:196
  88.0 17.6 %collective-permute-start.6 = (bf16[256,1152]{1,0:T(8,128)(2,1)}, bf16[256,1152]{1,0:T(8,128)(2,1)}, u32[]{:S(2)}, u32[]{:S(2)}) collective-permute-start(bf16[256,1152]{1,0:T(8,128)(2,1)} %slice.475), channel_id=1, source_target_pairs={{0,16},{16,0},{1,17},{17,1},{2,18},{18,2},{3,19},{19,3},{4,20},{20... | collective-permute-start | bytes 1769480 | tf_op jit(solution)/shard_map/ppermute | solution.py:200
  92.9 16.9 %collective-permute-start.7 = (bf16[256,1152]{1,0:T(8,128)(2,1)}, bf16[256,1152]{1,0:T(8,128)(2,1)}, u32[]{:S(2)}, u32[]{:S(2)}) collective-permute-start(bf16[256,1152]{1,0:T(8,128)(2,1)} %slice.476), channel_id=1, source_target_pairs={{0,8},{8,0},{1,9},{9,1},{2,10},{10,2},{3,11},{11,3},{4,12},{12,4},... | collective-permute-start | bytes 1769480 | tf_op jit(solution)/shard_map/ppermute | solution.py:204
  97.8 48.3 %collective-permute-start.10 = (bf16[256,2048]{1,0:T(8,128)(2,1)}, bf16[256,2048]{1,0:T(8,128)(2,1)S(1)}, u32[]{:S(2)}, u32[]{:S(2)}) collective-permute-start(bf16[256,2048]{1,0:T(8,128)(2,1)} %all-gather.11.cloned.1.call-done.refs_0_), channel_id=1, source_target_pairs={{0,8},{8,0},{1,9},{9,1},{2,10},{10,2},{3,11},{11,3},{4,12},{12,4},... | collective-permute-start | bytes 3145736 | tf_op jit(solution)/shard_map/ppermute | solution.py:204
  97.8 48.3 %collective-permute-start.11 = (bf16[256,2048]{1,0:T(8,128)(2,1)}, bf16[256,2048]{1,0:T(8,128)(2,1)S(1)}, u32[]{:S(2)}, u32[]{:S(2)}) collective-permute-start(bf16[256,2048]{1,0:T(8,128)(2,1)} %all-gather.11.cloned.1.call-done.refs_0_), channel_id=1, source_target_pairs={{0,16},{16,0},{1,17},{17,1},{2,18},{18,2},{3,19},{19,3},{4,20},{20... | collective-permute-start | bytes 3145736 | tf_op jit(solution)/shard_map/ppermute | solution.py:200
  97.8 134.9 %all-gather.15.cloned.1.call-start = ((), (), s32[]{:S(2)}) async-start(), calls=%async_computation.16 | async-start | bytes 2621440 | tf_op jit(solution)/shard_map/all_gather | solution.py:208
  99.8 60.7 %collective-permute-start.14 = (bf16[128,2048]{1,0:T(8,128)(2,1)}, bf16[128,2048]{1,0:T(8,128)(2,1)}, u32[]{:S(2)}, u32[]{:S(2)}) collective-permute-start(bf16[128,2048]{1,0:T(8,128)(2,1)} %slice.519), channel_id=1, source_target_pairs={{0,16},{16,0},{1,17},{17,1},{2,18},{18,2},{3,19},{19,3},{4,20},{20... | collective-permute-start | bytes 1572872 | tf_op jit(solution)/shard_map/ppermute | solution.py:200
  105.5 54.9 %collective-permute-start.15 = (bf16[128,2048]{1,0:T(8,128)(2,1)}, bf16[128,2048]{1,0:T(8,128)(2,1)}, u32[]{:S(2)}, u32[]{:S(2)}) collective-permute-start(bf16[128,2048]{1,0:T(8,128)(2,1)} %slice.520), channel_id=1, source_target_pairs={{0,8},{8,0},{1,9},{9,1},{2,10},{10,2},{3,11},{11,3},{4,12},{12,4},... | collective-permute-start | bytes 1572872 | tf_op jit(solution)/shard_map/ppermute | solution.py:204
  147.0 14.2 %collective-permute-start.12 = (bf16[128,2048]{1,0:T(8,128)(2,1)}, bf16[128,2048]{1,0:T(8,128)(2,1)S(1)}, u32[]{:S(2)}, u32[]{:S(2)}) collective-permute-start(bf16[128,2048]{1,0:T(8,128)(2,1)} %slice.517), channel_id=1, source_target_pairs={{0,16},{16,0},{1,17},{17,1},{2,18},{18,2},{3,19},{19,3},{4,20},{20... | collective-permute-start | bytes 1572872 | tf_op jit(solution)/shard_map/ppermute | solution.py:200
  149.2 13.9 %collective-permute-start.13 = (bf16[128,2048]{1,0:T(8,128)(2,1)}, bf16[128,2048]{1,0:T(8,128)(2,1)S(1)}, u32[]{:S(2)}, u32[]{:S(2)}) collective-permute-start(bf16[128,2048]{1,0:T(8,128)(2,1)} %slice.518), channel_id=1, source_target_pairs={{0,8},{8,0},{1,9},{9,1},{2,10},{10,2},{3,11},{11,3},{4,12},{12,4},... | collective-permute-start | bytes 1572872 | tf_op jit(solution)/shard_map/ppermute | solution.py:204
  184.4 124.6 %reduce-scatter.5.cloned.1.call-start = ((), (), s32[]{:S(2)}) async-start(), calls=%async_computation.9 | async-start | bytes 2621440 | tf_op jit(solution)/shard_map/reduce_scatter | solution.py:212
  184.9 37.8 %collective-permute-start.17 = (bf16[512,2048]{1,0:T(8,128)(2,1)}, bf16[512,2048]{1,0:T(8,128)(2,1)}, u32[]{:S(2)}, u32[]{:S(2)}) collective-permute-start(bf16[512,2048]{1,0:T(8,128)(2,1)} %all-gather.13.cloned.1.call-done.a_ref), channel_id=1, source_target_pairs={{0,4},{4,0},{1,5},{5,1},{2,6},{6,2},{3,7},{7,3},{8,12},{12,8},{9,1... | collective-permute-start | bytes 6291464 | tf_op jit(solution)/shard_map/ppermute | solution.py:196
  185.5 25.4 %collective-permute-start.18 = (bf16[512,1024]{1,0:T(8,128)(2,1)}, bf16[512,1024]{1,0:T(8,128)(2,1)S(1)}, u32[]{:S(2)}, u32[]{:S(2)}) collective-permute-start(bf16[512,1024]{1,0:T(8,128)(2,1)} %bitcast.26), channel_id=1, source_target_pairs={{0,8},{8,0},{1,9},{9,1},{2,10},{10,2},{3,11},{11,3},{4,12},{12,4},... | collective-permute-start | bytes 3145736 | tf_op jit(solution)/shard_map/ppermute | solution.py:204
  186.4 25.2 %collective-permute-start.19 = (bf16[512,1024]{1,0:T(8,128)(2,1)}, bf16[512,1024]{1,0:T(8,128)(2,1)}, u32[]{:S(2)}, u32[]{:S(2)}) collective-permute-start(bf16[512,1024]{1,0:T(8,128)(2,1)} %bitcast.26), channel_id=1, source_target_pairs={{0,16},{16,0},{1,17},{17,1},{2,18},{18,2},{3,19},{19,3},{4,20},{20... | collective-permute-start | bytes 3145736 | tf_op jit(solution)/shard_map/ppermute | solution.py:200
  211.7 15.4 %collective-permute-start.20 = (bf16[256,1024]{1,0:T(8,128)(2,1)S(1)}, bf16[256,1024]{1,0:T(8,128)(2,1)S(1)}, u32[]{:S(2)}, u32[]{:S(2)}) collective-permute-start(bf16[256,1024]{1,0:T(8,128)(2,1)S(1)} %slice.530), channel_id=1, source_target_pairs={{0,16},{16,0},{1,17},{17,1},{2,18},{18,2},{3,19},{19,3},{4,20},{20... | collective-permute-start | bytes 1572872 | tf_op jit(solution)/shard_map/ppermute | solution.py:200
  214.5 12.6 %collective-permute-start.21 = (bf16[256,1024]{1,0:T(8,128)(2,1)S(1)}, bf16[256,1024]{1,0:T(8,128)(2,1)S(1)}, u32[]{:S(2)}, u32[]{:S(2)}) collective-permute-start(bf16[256,1024]{1,0:T(8,128)(2,1)S(1)} %slice.531), channel_id=1, source_target_pairs={{0,8},{8,0},{1,9},{9,1},{2,10},{10,2},{3,11},{11,3},{4,12},{12,4},... | collective-permute-start | bytes 1572872 | tf_op jit(solution)/shard_map/ppermute | solution.py:204
  277.0 26.7 %collective-permute-start.26 = (bf16[512,2048]{1,0:T(8,128)(2,1)}, bf16[512,2048]{1,0:T(8,128)(2,1)}, u32[]{:S(2)}, u32[]{:S(2)}) collective-permute-start(bf16[512,2048]{1,0:T(8,128)(2,1)} %convolution_convert_fusion), channel_id=1, source_target_pairs={{0,4},{4,0},{1,5},{5,1},{2,6},{6,2},{3,7},{7,3},{8,12},{12,8},{9,1... | collective-permute-start | bytes 6291464 | tf_op jit(solution)/shard_map/ppermute | solution.py:196
  277.0 25.8 %collective-permute-start.24 = (bf16[256,2048]{1,0:T(8,128)(2,1)}, bf16[256,2048]{1,0:T(8,128)(2,1)S(1)}, u32[]{:S(2)}, u32[]{:S(2)}) collective-permute-start(bf16[256,2048]{1,0:T(8,128)(2,1)} %convolution_convert_fusion.4), channel_id=1, source_target_pairs={{0,8},{8,0},{1,9},{9,1},{2,10},{10,2},{3,11},{11,3},{4,12},{12,4},... | collective-permute-start | bytes 3145736 | tf_op jit(solution)/shard_map/ppermute | solution.py:204
  278.5 25.3 %collective-permute-start.25 = (bf16[256,2048]{1,0:T(8,128)(2,1)S(1)}, bf16[256,2048]{1,0:T(8,128)(2,1)S(1)}, u32[]{:S(2)}, u32[]{:S(2)}) collective-permute-start(bf16[256,2048]{1,0:T(8,128)(2,1)S(1)} %convolution_convert_fusion.3), channel_id=1, source_target_pairs={{0,16},{16,0},{1,17},{17,1},{2,18},{18,2},{3,19},{19,3},{4,20},{20... | collective-permute-start | bytes 3145736 | tf_op jit(solution)/shard_map/ppermute | solution.py:200
  314.4 14.5 %collective-permute-start.28 = (bf16[128,2048]{1,0:T(8,128)(2,1)}, bf16[128,2048]{1,0:T(8,128)(2,1)S(1)}, u32[]{:S(2)}, u32[]{:S(2)}) collective-permute-start(bf16[128,2048]{1,0:T(8,128)(2,1)} %fusion.8), channel_id=1, source_target_pairs={{0,16},{16,0},{1,17},{17,1},{2,18},{18,2},{3,19},{19,3},{4,20},{20... | collective-permute-start | bytes 1572872 | tf_op jit(solution)/shard_map/ppermute | solution.py:200
  314.7 14.3 %collective-permute-start.29 = (bf16[128,2048]{1,0:T(8,128)(2,1)}, bf16[128,2048]{1,0:T(8,128)(2,1)S(1)}, u32[]{:S(2)}, u32[]{:S(2)}) collective-permute-start(bf16[128,2048]{1,0:T(8,128)(2,1)} %fusion.9), channel_id=1, source_target_pairs={{0,8},{8,0},{1,9},{9,1},{2,10},{10,2},{3,11},{11,3},{4,12},{12,4},... | collective-permute-start | bytes 1572872 | tf_op jit(solution)/shard_map/ppermute | solution.py:204
  330.9 25.8 %collective-permute-start.33 = (bf16[512,1024]{1,0:T(8,128)(2,1)}, bf16[512,1024]{1,0:T(8,128)(2,1)}, u32[]{:S(2)}, u32[]{:S(2)}) collective-permute-start(bf16[512,1024]{1,0:T(8,128)(2,1)} %convolution_convert_fusion.6), channel_id=1, source_target_pairs={{0,8},{8,0},{1,9},{9,1},{2,10},{10,2},{3,11},{11,3},{4,12},{12,4},... | collective-permute-start | bytes 3145736 | tf_op jit(solution)/shard_map/ppermute | solution.py:204
  332.0 25.4 %collective-permute-start.34 = (bf16[512,1024]{1,0:T(8,128)(2,1)}, bf16[512,1024]{1,0:T(8,128)(2,1)}, u32[]{:S(2)}, u32[]{:S(2)}) collective-permute-start(bf16[512,1024]{1,0:T(8,128)(2,1)} %convolution_convert_fusion.5), channel_id=1, source_target_pairs={{0,16},{16,0},{1,17},{17,1},{2,18},{18,2},{3,19},{19,3},{4,20},{20... | collective-permute-start | bytes 3145736 | tf_op jit(solution)/shard_map/ppermute | solution.py:200
  334.0 17.6 %all-to-all-start.2 = ((bf16[4,2,128,128]{3,2,1,0:T(8,128)(2,1)}), bf16[4,2,128,128]{3,2,1,0:T(8,128)(2,1)S(1)}, u32[]{:S(2)}, u32[]{:S(2)}) async-start(bf16[4,2,128,128]{3,2,1,0:T(8,128)(2,1)} %bitcast.176), calls=%async_computation.3 | async-start | bytes 524288 | tf_op jit(solution)/shard_map/all_to_all | solution.py:487
  338.5 66.6 %reduce-scatter.7.cloned.1.call-start = ((), (), s32[]{:S(2)}) async-start(), calls=%async_computation.10 | async-start | bytes 2621440 | tf_op jit(solution)/shard_map/reduce_scatter | solution.py:212
  347.9 106.0 %reduce-scatter.9.cloned.1.call-start = ((), (), s32[]{:S(2)}) async-start(), calls=%async_computation.11 | async-start | bytes 1474560 | tf_op jit(solution)/shard_map/reduce_scatter | solution.py:212
  363.6 27.7 %collective-permute-start.31 = (bf16[512,1152]{1,0:T(8,128)(2,1)S(1)}, bf16[512,1152]{1,0:T(8,128)(2,1)S(1)}, u32[]{:S(2)}, u32[]{:S(2)}) collective-permute-start(bf16[512,1152]{1,0:T(8,128)(2,1)S(1)} %convolution_convert_fusion.2), channel_id=1, source_target_pairs={{0,8},{8,0},{1,9},{9,1},{2,10},{10,2},{3,11},{11,3},{4,12},{12,4},... | collective-permute-start | bytes 3538952 | tf_op jit(solution)/shard_map/ppermute | solution.py:204
  365.2 27.4 %collective-permute-start.32 = (bf16[512,1152]{1,0:T(8,128)(2,1)S(1)}, bf16[512,1152]{1,0:T(8,128)(2,1)S(1)}, u32[]{:S(2)}, u32[]{:S(2)}) collective-permute-start(bf16[512,1152]{1,0:T(8,128)(2,1)S(1)} %convolution_convert_fusion.1), channel_id=1, source_target_pairs={{0,16},{16,0},{1,17},{17,1},{2,18},{18,2},{3,19},{19,3},{4,20},{20... | collective-permute-start | bytes 3538952 | tf_op jit(solution)/shard_map/ppermute | solution.py:200
  393.8 14.2 %collective-permute-start.36 = (bf16[256,1152]{1,0:T(8,128)(2,1)}, bf16[256,1152]{1,0:T(8,128)(2,1)}, u32[]{:S(2)}, u32[]{:S(2)}) collective-permute-start(bf16[256,1152]{1,0:T(8,128)(2,1)} %add_convert_fusion.5), channel_id=1, source_target_pairs={{0,16},{16,0},{1,17},{17,1},{2,18},{18,2},{3,19},{19,3},{4,20},{20... | collective-permute-start | bytes 1769480 | tf_op jit(solution)/shard_map/ppermute | solution.py:200
  396.7 13.9 %collective-permute-start.37 = (bf16[256,1152]{1,0:T(8,128)(2,1)}, bf16[256,1152]{1,0:T(8,128)(2,1)}, u32[]{:S(2)}, u32[]{:S(2)}) collective-permute-start(bf16[256,1152]{1,0:T(8,128)(2,1)} %add_convert_fusion.4), channel_id=1, source_target_pairs={{0,8},{8,0},{1,9},{9,1},{2,10},{10,2},{3,11},{11,3},{4,12},{12,4},... | collective-permute-start | bytes 1769480 | tf_op jit(solution)/shard_map/ppermute | solution.py:204
  413.9 18.2 %collective-permute-start.40 = (bf16[256,1024]{1,0:T(8,128)(2,1)}, bf16[256,1024]{1,0:T(8,128)(2,1)S(1)}, u32[]{:S(2)}, u32[]{:S(2)}) collective-permute-start(bf16[256,1024]{1,0:T(8,128)(2,1)} %fusion.15), channel_id=1, source_target_pairs={{0,16},{16,0},{1,17},{17,1},{2,18},{18,2},{3,19},{19,3},{4,20},{20... | collective-permute-start | bytes 1572872 | tf_op jit(solution)/shard_map/ppermute | solution.py:200
  414.3 17.8 %collective-permute-start.41 = (bf16[256,1024]{1,0:T(8,128)(2,1)}, bf16[256,1024]{1,0:T(8,128)(2,1)S(1)}, u32[]{:S(2)}, u32[]{:S(2)}) collective-permute-start(bf16[256,1024]{1,0:T(8,128)(2,1)} %fusion.16), channel_id=1, source_target_pairs={{0,8},{8,0},{1,9},{9,1},{2,10},{10,2},{3,11},{11,3},{4,12},{12,4},... | collective-permute-start | bytes 1572872 | tf_op jit(solution)/shard_map/ppermute | solution.py:204
  416.3 31.8 %collective-permute-start.38 = (bf16[256,2048]{1,0:T(8,128)(2,1)}, bf16[256,2048]{1,0:T(8,128)(2,1)}, u32[]{:S(2)}, u32[]{:S(2)}) collective-permute-start(bf16[256,2048]{1,0:T(8,128)(2,1)} %convert_element_type.285), channel_id=1, source_target_pairs={{0,8},{8,0},{1,9},{9,1},{2,10},{10,2},{3,11},{11,3},{4,12},{12,4},... | collective-permute-start | bytes 3145736 | tf_op jit(solution)/shard_map/ppermute | solution.py:204
  417.3 30.8 %collective-permute-start.39 = (bf16[256,2048]{1,0:T(8,128)(2,1)}, bf16[256,2048]{1,0:T(8,128)(2,1)}, u32[]{:S(2)}, u32[]{:S(2)}) collective-permute-start(bf16[256,2048]{1,0:T(8,128)(2,1)} %convert_element_type.286), channel_id=1, source_target_pairs={{0,16},{16,0},{1,17},{17,1},{2,18},{18,2},{3,19},{19,3},{4,20},{20... | collective-permute-start | bytes 3145736 | tf_op jit(solution)/shard_map/ppermute | solution.py:200
  435.7 42.0 %all-to-all-start.4 = ((bf16[8,64,1024]{2,1,0:T(8,128)(2,1)}), bf16[8,64,1024]{2,1,0:T(8,128)(2,1)}, u32[]{:S(2)}, u32[]{:S(2)}) async-start(bf16[8,64,1024]{2,1,0:T(8,128)(2,1)} %bitcast.215), calls=%async_computation.8 | async-start | bytes 2097152 | tf_op jit(solution)/shard_map/all_to_all | solution.py:526
  440.3 59.8 %reduce-scatter.11.cloned.1.call-start = ((), (), s32[]{:S(2)}) async-start(), calls=%async_computation.12 | async-start | bytes 1310720 | tf_op jit(solution)/shard_map/reduce_scatter | solution.py:212
  452.2 10.6 %collective-permute-start.42 = (bf16[128,2048]{1,0:T(8,128)(2,1)}, bf16[128,2048]{1,0:T(8,128)(2,1)S(1)}, u32[]{:S(2)}, u32[]{:S(2)}) collective-permute-start(bf16[128,2048]{1,0:T(8,128)(2,1)} %add_convert_fusion.7), channel_id=1, source_target_pairs={{0,16},{16,0},{1,17},{17,1},{2,18},{18,2},{3,19},{19,3},{4,20},{20... | collective-permute-start | bytes 1572872 | tf_op jit(solution)/shard_map/ppermute | solution.py:200
  456.3 14.3 %collective-permute-start.43 = (bf16[128,2048]{1,0:T(8,128)(2,1)S(1)}, bf16[128,2048]{1,0:T(8,128)(2,1)S(1)}, u32[]{:S(2)}, u32[]{:S(2)}) collective-permute-start(bf16[128,2048]{1,0:T(8,128)(2,1)S(1)} %add_convert_fusion.6), channel_id=1, source_target_pairs={{0,8},{8,0},{1,9},{9,1},{2,10},{10,2},{3,11},{11,3},{4,12},{12,4},... | collective-permute-start | bytes 1572872 | tf_op jit(solution)/shard_map/ppermute | solution.py:204
  477.7 13.1 %all-to-all-start.3 = ((f32[32,1,708]{2,1,0:T(1,128)}), f32[32,1,708]{2,1,0:T(1,128)S(1)}, u32[]{:S(2)}, u32[]{:S(2)}) async-start(f32[32,1,708]{2,1,0:T(1,128)} %all_to_all.22), calls=%async_computation.6 | async-start | bytes 196608 | tf_op jit(solution)/shard_map/all_to_all | solution.py:571
  (112 other events, 970.6 us)
Sparse Core Ops, SparseCore 0:
  15.3 34.2 all-gather.8
  57.6 29.5 all-gather.10
  97.9 59.7 all-gather.12
  184.5 46.5 all-gather.14
  263.6 43.6 reduce-scatter.4
  348.0 44.3 reduce-scatter.6
  414.0 28.2 reduce-scatter.8
  472.2 27.8 reduce-scatter.10
